TPU v7x, 32 devices: a whole 2x2x4 slice. The times are simulated.
32 devices in a mesh: dp: 8 (over z, y), mp: 4 (over x, core).
Axes of the slice: x: 2, y: 2, z: 4, core: 2. Of those that a mesh axis runs over, the one named last changes fastest.
Arguments:
- patches: bfloat16 [16384, 768], P(('dp', 'mp')), may hold values from -6 to 6
- conditioning: bfloat16 [16384, 768], P(('dp', 'mp')), may hold values from -6 to 6
- cotangent: bfloat16 [16384, 768], P(('dp', 'mp')), may hold values from -6 to 6
- segments: int32 [64, 256], P('dp'), may hold values from 0 to 3, never falling along the last dimension, each value on 1 to 128 neighbouring positions
- routes: int32 [16384, 2], P('dp'), may hold values from 0 to 7, all different within a row; in each aligned block of 2048 rows (0 to 2047, 2048 to 4095, ...) at most 768 rows name the same one
- gate_values: float32 [16384, 2], P('dp'), may hold values from 0.2 to 0.8
- ada_weight: bfloat16 [768, 4608], replicated, may hold values from -0.21875 to 0.21875
- ada_bias: float32 [4608], replicated, may hold values from -3 to 3
- qkv_weight: bfloat16 [768, 3, 768], P(None, None, 'mp'), may hold values from -0.21875 to 0.21875
- out_weight: bfloat16 [768, 768], P('mp'), may hold values from -1.75 to 1.75
- shared_up: bfloat16 [768, 3072], P(None, 'mp'), may hold values from -0.21875 to 0.21875
- shared_down: bfloat16 [3072, 768], P('mp'), may hold values from -0.109375 to 0.109375
- expert_up: bfloat16 [8, 768, 3072], P(None, None, 'mp'), may hold values from -0.21875 to 0.21875
- expert_down: bfloat16 [8, 3072, 768], P(None, 'mp'), may hold values from -0.109375 to 0.109375
Outputs:
- output: bfloat16 [16384, 768], P(('dp', 'mp'))
- patches_grad: float32 [16384, 768], P(('dp', 'mp'))
- conditioning_grad: float32 [16384, 768], P(('dp', 'mp'))
- ada_weight_grad: float32 [768, 4608], P('dp', 'mp')
- ada_bias_grad: float32 [4608], P(('dp', 'mp'))
- qkv_weight_grad: float32 [768, 3, 768], P('dp', None, 'mp')
- out_weight_grad: float32 [768, 768], P('mp', 'dp')
- shared_up_grad: float32 [768, 3072], P('dp', 'mp')
- shared_down_grad: float32 [3072, 768], P('mp', 'dp')
- expert_up_grad: float32 [8, 768, 3072], P(None, 'dp', 'mp')
- expert_down_grad: float32 [8, 3072, 768], P(None, 'mp', 'dp')
Inputs may be any that keep to these rules, and one draw needn't show every extreme that they name: Each row names two different experts. In the patches of one index of dp (2048 rows of routes) no expert is named more than 768 times, a bound that some expert reaches in some such block. `segments`: along a row the numbers never fall; an image spans 1 to 128 patches of its row, some image exactly 128.
All inputs are finite; a program needn't handle non-finite values.
Results may differ from a plain program's by a relative error of at most 0.02.
The roundings to bfloat16 on the way count: a program that leaves them out, or rounds other values in their place, can miss the bound.
Values may be sent and summed in bfloat16 or wider, within the bound.
A program may use at most 320 MiB of HBM per device.

v0:
```python
import jax
import jax.numpy as jnp
from jax import lax
from jax.sharding import PartitionSpec as P

HEAD_DIM = 64
CAP = 768


def layer_norm(values):
    center = values - jnp.mean(values, axis=-1, keepdims=True)
    spread = jnp.mean(center * center, axis=-1, keepdims=True)
    return center * lax.rsqrt(spread + 1e-06)


def modulate(rows, shift, scale):
    return layer_norm(rows) * (1.0 + scale) + shift


def second_piece(base, shift, scale, gate, branch):
    middle = base + gate * branch
    return (middle, modulate(middle, shift, scale))


def contract_rows(left, right):
    return lax.dot_general(
        left, right, (((0,), (0,)), ((), ())), preferred_element_type=jnp.float32
    )


def contract_cols(left, right):
    return lax.dot_general(
        left, right, (((1,), (1,)), ((), ())), preferred_element_type=jnp.float32
    )


def gelu_value(values):
    return jax.nn.gelu(values, approximate=True)


def gelu_grad(values, upstream):
    unused, backward = jax.vjp(gelu_value, values)
    return backward(upstream)[0]


def route_tables(routes, experts, capacity):
    tokens = routes.shape[0]
    picks = routes.shape[1]
    flat = routes.reshape(-1)
    onehot = (flat[:, None] == jnp.arange(experts, dtype=jnp.int32)[None, :]).astype(jnp.int32)
    before = jnp.cumsum(onehot, axis=0) - onehot
    slot = jnp.sum(before * onehot, axis=1)
    place = flat * capacity + slot
    order = jnp.arange(picks * tokens, dtype=jnp.int32)
    token_of = jnp.full((experts * capacity,), tokens, jnp.int32).at[place].set(order // picks)
    entry_of = jnp.full((experts * capacity,), picks * tokens, jnp.int32).at[place].set(order)
    return (place.reshape(tokens, picks), token_of, entry_of)


def masked_scores(queries, key_rows, same, factor):
    scores = (
        jnp.einsum("rqhe,rkhe->rhqk", queries, key_rows, preferred_element_type=jnp.float32)
        * factor
    )
    return jnp.where(same, scores, -1000000000.0)


def local(
    patches,
    conditioning,
    cotangent,
    segments,
    routes,
    gate_values,
    ada_weight,
    ada_bias,
    qkv_weight,
    out_weight,
    shared_up,
    shared_down,
    expert_up,
    expert_down,
):
    bf16 = jnp.bfloat16
    f32 = jnp.float32
    width = patches.shape[1]
    group_rows = routes.shape[0]
    row_count, seq_len = segments.shape
    experts = expert_up.shape[0]
    heads_local = qkv_weight.shape[2] // HEAD_DIM
    factor = HEAD_DIM ** (-0.5)
    cond32 = conditioning.astype(f32)
    silu_cond = jax.nn.silu(cond32).astype(bf16)
    modulation = jnp.dot(silu_cond, ada_weight, preferred_element_type=f32) + ada_bias[None, :]
    shift_one, scale_one, gate_one, shift_two, scale_two, gate_two = [
        modulation[:, number * width : (number + 1) * width] for number in range(6)
    ]
    patches32 = patches.astype(f32)
    normed_one = modulate(patches32, shift_one, scale_one).astype(bf16)
    gathered_one = lax.all_gather(normed_one, "mp", axis=0, tiled=True)
    qkv_flat = qkv_weight.reshape(width, -1)
    qkv_all = jnp.dot(gathered_one, qkv_flat, preferred_element_type=f32).astype(bf16)
    qkv_all = qkv_all.reshape(row_count, seq_len, 3, heads_local, HEAD_DIM)
    queries = qkv_all[:, :, 0]
    key_rows = qkv_all[:, :, 1]
    value_rows = qkv_all[:, :, 2]
    same = segments[:, None, :, None] == segments[:, None, None, :]
    masked = masked_scores(queries, key_rows, same, factor)
    top = jnp.max(masked, axis=-1, keepdims=True)
    expo = jnp.exp(masked - top)
    total = jnp.sum(expo, axis=-1, keepdims=True)
    log_total = top + jnp.log(total)
    light = (expo / total).astype(bf16)
    attended = (
        jnp.einsum("rhqk,rkhe->rqhe", light, value_rows, preferred_element_type=f32)
        .astype(bf16)
        .reshape(group_rows, -1)
    )
    rows = attended
    attn_out = lax.psum_scatter(
        jnp.dot(rows, out_weight, preferred_element_type=f32).astype(jnp.bfloat16),
        "mp",
        scatter_dimension=0,
        tiled=True,
    ).astype(jnp.float32)
    middle, normed_two = second_piece(patches32, shift_two, scale_two, gate_one, attn_out)
    gathered_two = lax.all_gather(normed_two.astype(bf16), "mp", axis=0, tiled=True)
    place, token_of, entry_of = route_tables(routes, experts, CAP)
    shared_pre = jnp.dot(gathered_two, shared_up, preferred_element_type=f32)
    shared_hidden = gelu_value(shared_pre).astype(bf16)
    padded_two = jnp.concatenate([gathered_two, jnp.zeros((1, width), bf16)], axis=0)
    dispatched = padded_two[token_of].reshape(experts, CAP, width)
    expert_pre = jnp.einsum("ecd,edf->ecf", dispatched, expert_up, preferred_element_type=f32)
    expert_hidden = gelu_value(expert_pre).astype(bf16)
    expert_out = jnp.einsum(
        "ecf,efd->ecd", expert_hidden, expert_down, preferred_element_type=f32
    ).reshape(-1, width)
    rows_place = place
    routed = jnp.sum(gate_values[:, :, None] * expert_out[rows_place], axis=1)
    mlp_out = lax.psum_scatter(
        (jnp.dot(shared_hidden, shared_down, preferred_element_type=f32) + routed).astype(
            jnp.bfloat16
        ),
        "mp",
        scatter_dimension=0,
        tiled=True,
    ).astype(jnp.float32)
    output = (middle + gate_two * mlp_out).astype(bf16)
    grad_out = cotangent.astype(f32)
    grad_gate_two = grad_out * mlp_out
    grad_mlp = (grad_out * gate_two).astype(bf16)
    grad_rows = lax.all_gather(grad_mlp, "mp", axis=0, tiled=True)
    shared_down_grad = contract_rows(shared_hidden, grad_rows)
    shared_dpre = gelu_grad(shared_pre, contract_cols(grad_rows, shared_down)).astype(bf16)
    shared_up_grad = contract_rows(gathered_two, shared_dpre)
    gate_flat = jnp.concatenate([gate_values.reshape(-1), jnp.zeros((1,), f32)], axis=0)
    padded_grad = jnp.concatenate([grad_rows, jnp.zeros((1, width), bf16)], axis=0)
    slot_grads = (
        (gate_flat[entry_of][:, None] * padded_grad[token_of].astype(f32))
        .astype(bf16)
        .reshape(experts, CAP, width)
    )
    expert_dact = jnp.einsum("ecd,efd->ecf", slot_grads, expert_down, preferred_element_type=f32)
    expert_down_grad = jnp.einsum(
        "ecf,ecd->efd", expert_hidden, slot_grads, preferred_element_type=f32
    )
    expert_dpre = gelu_grad(expert_pre, expert_dact).astype(bf16)
    expert_up_grad = jnp.einsum("ecd,ecf->edf", dispatched, expert_dpre, preferred_element_type=f32)
    slot_back = jnp.einsum(
        "ecf,edf->ecd", expert_dpre, expert_up, preferred_element_type=f32
    ).reshape(-1, width)
    rows_place = place
    grad_normed_two = lax.psum_scatter(
        (contract_cols(shared_dpre, shared_up) + jnp.sum(slot_back[rows_place], axis=1)).astype(
            jnp.bfloat16
        ),
        "mp",
        scatter_dimension=0,
        tiled=True,
    ).astype(jnp.float32)
    unused, second_back = jax.vjp(second_piece, patches32, shift_two, scale_two, gate_one, attn_out)
    grad_base, grad_shift_two, grad_scale_two, grad_gate_one, grad_attn = second_back(
        (grad_out, grad_normed_two)
    )
    grad_attn_rows = lax.all_gather(grad_attn.astype(bf16), "mp", axis=0, tiled=True)
    out_weight_grad = contract_rows(attended, grad_attn_rows)
    grad_heads = (
        contract_cols(grad_attn_rows, out_weight)
        .astype(bf16)
        .reshape(row_count, seq_len, heads_local, HEAD_DIM)
    )
    probs_back = jnp.exp(masked_scores(queries, key_rows, same, factor) - log_total)
    light_back = probs_back.astype(bf16)
    grad_light = jnp.einsum("rqhe,rkhe->rhqk", grad_heads, value_rows, preferred_element_type=f32)
    row_term = jnp.sum(probs_back * grad_light, axis=-1, keepdims=True)
    grad_scores = (probs_back * (grad_light - row_term)).astype(bf16)
    grad_query = (
        jnp.einsum("rhqk,rkhe->rqhe", grad_scores, key_rows, preferred_element_type=f32) * factor
    )
    grad_key = (
        jnp.einsum("rhqk,rqhe->rkhe", grad_scores, queries, preferred_element_type=f32) * factor
    )
    grad_value = jnp.einsum("rhqk,rqhe->rkhe", light_back, grad_heads, preferred_element_type=f32)
    grad_qkv = (
        jnp.stack([grad_query, grad_key, grad_value], axis=2).astype(bf16).reshape(group_rows, -1)
    )
    qkv_weight_grad = contract_rows(gathered_one, grad_qkv).reshape(width, 3, -1)
    rows = grad_qkv
    grad_normed_one = lax.psum_scatter(
        contract_cols(rows, qkv_flat).astype(jnp.bfloat16), "mp", scatter_dimension=0, tiled=True
    ).astype(jnp.float32)
    unused_first, first_back = jax.vjp(modulate, patches32, shift_one, scale_one)
    grad_first, grad_shift_one, grad_scale_one = first_back(grad_normed_one)
    patches_grad = grad_base + grad_first
    grad_modulation = jnp.concatenate(
        [
            grad_shift_one,
            grad_scale_one,
            grad_gate_one,
            grad_shift_two,
            grad_scale_two,
            grad_gate_two,
        ],
        axis=1,
    ).astype(bf16)
    ada_grad = contract_rows(silu_cond, grad_modulation)
    bias_grad = jnp.sum(grad_modulation.astype(f32), axis=0).reshape(lax.axis_size("dp"), -1)
    unused_silu, silu_back = jax.vjp(jax.nn.silu, cond32)
    conditioning_grad = silu_back(contract_cols(grad_modulation, ada_weight))[0]
    qkv_sum, out_sum, up_sum, down_sum, expert_up_sum, expert_down_sum, ada_sum, bias_sum = (
        lax.psum_scatter(qkv_weight_grad, "dp", scatter_dimension=0, tiled=True),
        lax.psum_scatter(out_weight_grad, "dp", scatter_dimension=1, tiled=True),
        lax.psum_scatter(shared_up_grad, "dp", scatter_dimension=0, tiled=True),
        lax.psum_scatter(shared_down_grad, "dp", scatter_dimension=1, tiled=True),
        lax.psum_scatter(expert_up_grad, "dp", scatter_dimension=1, tiled=True),
        lax.psum_scatter(expert_down_grad, "dp", scatter_dimension=2, tiled=True),
        lax.psum_scatter(ada_grad, "dp", scatter_dimension=0, tiled=True),
        lax.psum_scatter(bias_grad, "dp", scatter_dimension=0, tiled=True),
    )
    ada_sum, bias_sum = (
        lax.psum_scatter(
            ada_sum.astype(jnp.bfloat16), "mp", scatter_dimension=1, tiled=True
        ).astype(jnp.float32),
        lax.psum_scatter(
            bias_sum.astype(jnp.bfloat16), "mp", scatter_dimension=1, tiled=True
        ).astype(jnp.float32),
    )
    return (
        output,
        patches_grad,
        conditioning_grad,
        ada_sum,
        bias_sum.reshape(-1),
        qkv_sum,
        out_sum,
        up_sum,
        down_sum,
        expert_up_sum,
        expert_down_sum,
    )


def solution(mesh):
    in_specs = (
        P(("dp", "mp"), None),
        P(("dp", "mp"), None),
        P(("dp", "mp"), None),
        P("dp", None),
        P("dp", None),
        P("dp", None),
        P(),
        P(),
        P(None, None, "mp"),
        P("mp", None),
        P(None, "mp"),
        P("mp", None),
        P(None, None, "mp"),
        P(None, "mp", None),
    )
    out_specs = (
        P(("dp", "mp"), None),
        P(("dp", "mp"), None),
        P(("dp", "mp"), None),
        P("dp", "mp"),
        P(("dp", "mp")),
        P("dp", None, "mp"),
        P("mp", "dp"),
        P("dp", "mp"),
        P("mp", "dp"),
        P(None, "dp", "mp"),
        P(None, "mp", "dp"),
    )
    return jax.shard_map(local, mesh=mesh, in_specs=in_specs, out_specs=out_specs, check_vma=False)
```

profile of v0, /device:TPU:0, one launch (start us, length us, event | category | flops | bytes accessed | tf_op | source)
XLA Modules:
  0.0 1880.4 jit_solution(9015619450793065419)
XLA Ops:
  10.8 6.8 convolution_add_fusion
  17.6 3.6 copy-done.7
  23.1 30.9 %all-gather.5.cloned.1.call-done = bf16[2048,768]{1,0:T(8,128)(2,1)} async-done(((bf16[512,768]{1,0:T(8,128)(2,1)}), bf16[2048,768]{1,0:T(8,128)(2,1)}) %all-gather.5.cloned.1.call-update) | async-done | bytes 3145744 | tf_op jit(solution)/shard_map/all_gather | solution.py:100
  53.9 3.9 convolution_convert_fusion.2
  65.5 2.8 convolution_convert_fusion.1
  68.9 37.6 %reduce-scatter.20.cloned.1.call-done = bf16[512,768]{1,0:T(8,128)(2,1)} async-done(((bf16[2048,768]{1,0:T(8,128)(2,1)}), bf16[512,768]{1,0:T(8,128)(2,1)}) %reduce-scatter.20.cloned.1.call-update) | async-done | bytes 786448 | tf_op jit(solution)/shard_map/reduce_scatter | solution.py:120
  109.6 3.9 fusion.44
  115.5 2.3 reduce-window.6
  119.4 2.0 reduce_sum.141
  121.4 3.0 compare_select_fusion
  128.0 15.5 scatter_custom_fusion.1
  143.5 34.3 %gather_fusion.2 = f32[6144]{0:T(1024)S(1)} fusion(f32[4097]{0:T(1024)S(1)} %pad_maximum_fusion, s32[6144]{0:T(1024)S(1)} %fusion.65), kind=kCustom, calls=%fused_computation.2 | custom fusion | bytes 73728 | tf_op jit(solution)/shard_map/gather | solution.py:159
  177.9 15.7 scatter_custom_fusion
  193.7 3.7 concatenate.15
  197.4 30.4 %gather_fusion.3 = bf16[6144,768]{1,0:T(8,128)(2,1)} fusion(bf16[2049,768]{1,0:T(8,128)(2,1)} %concatenate.15, s32[6144]{0:T(1024)S(1)} %fusion.64), kind=kCustom, calls=%fused_computation.3 | custom fusion | bytes 18898944 | tf_op jit(solution)/shard_map/gather | solution.py:159
  227.8 3.7 concatenate.13
  231.5 30.4 %gather_fusion = bf16[6144,768]{1,0:T(8,128)(2,1)} fusion(bf16[2049,768]{1,0:T(8,128)(2,1)} %concatenate.13, s32[6144]{0:T(1024)S(1)} %fusion.64), kind=kCustom, calls=%fused_computation | custom fusion | bytes 18898944 | tf_op jit(solution)/shard_map/gather | solution.py:132
  261.9 13.6 copy.69
  275.5 16.5 fusion.85
  292.0 26.9 %fusion.6 = bf16[8,768,768]{2,1,0:T(8,128)(2,1)} fusion(f32[8,768,768]{2,1,0:T(8,128)} %fusion.85, bf16[8,768,768]{2,1,0:T(8,128)(2,1)} %param.27, f32[8,768,768]{1,2,0:T(8,128)} %copy.69, f32[8,768]{1,0:T(8,128)S(1)} %mul.332), kind=kOutput, calls=%fused_computation.15 | convolution fusion | flops 7351566336 | bytes 56647680 | tf_op jit(solution)/shard_map/ecd,efd->ecf/dot_general | solution.py:163
  318.9 16.7 fusion.87
  335.6 26.6 %gather_fusion.4 = f32[4096,768]{1,0:T(8,128)} fusion(f32[6144,768]{1,0:T(8,128)} %bitcast.135, s32[4096]{0:T(1024)S(1)} %broadcast_clamp_fusion), kind=kCustom, calls=%fused_computation.4 | custom fusion | bytes 25182208 | tf_op jit(solution)/shard_map/gather | solution.py:174
  362.3 15.1 reshape.246
  377.4 36.4 %reduce_sum.146 = f32[2048,768]{1,0:T(8,128)} reduce(f32[2048,2,768]{2,1,0:T(2,128)} %reshape.246, f32[]{:T(128)} %constant.26.clone.1), dimensions={1}, to_apply=%region_14.15 | reduce | flops 1572864 | bytes 18874372 | tf_op jit(solution)/shard_map/reduce_sum | solution.py:174
  413.8 4.8 fusion.86
  418.7 7.4 fusion.13
  427.7 4.1 add_convert_fusion
  431.9 19.4 %fusion.79 = f32[8,768,768]{2,1,0:T(8,128)} fusion(bf16[8,768,768]{2,1,0:T(8,128)(2,1)} %param.27, f32[8,768,768]{2,1,0:T(8,128)} %fusion.85), kind=kOutput, calls=%fused_computation.166 | convolution fusion | flops 7290224640 | bytes 47185920 | tf_op jit(solution)/shard_map/ecf,efd->ecd/dot_general | solution.py:135
  451.3 26.7 %gather_fusion.1 = f32[4096,768]{1,0:T(8,128)} fusion(f32[6144,768]{1,0:T(8,128)} %bitcast.134, s32[4096]{0:T(1024)S(1)} %broadcast_clamp_fusion), kind=kCustom, calls=%fused_computation.1 | custom fusion | bytes 25182208 | tf_op jit(solution)/shard_map/gather | solution.py:139
  478.0 15.2 reshape.218
  493.2 20.5 %multiply_reduce_fusion = f32[2048,768]{1,0:T(8,128)} fusion(f32[2048,2,768]{2,1,0:T(2,128)} %reshape.218, f32[2048,2]{1,0:T(8,128)S(1)} %copy-done.16), kind=kLoop, calls=%fused_computation.18 | loop fusion | flops 4718592 | bytes 18890752 | tf_op jit(solution)/shard_map/reduce_sum | solution.py:139
  513.7 10.3 add_convert_fusion.1
  524.3 2.0 multiply_reduce_fusion.2
  526.3 35.5 %reduce-scatter.22.cloned.1.call-done = bf16[512,768]{1,0:T(8,128)(2,1)} async-done(((bf16[2048,768]{1,0:T(8,128)(2,1)}), bf16[512,768]{1,0:T(8,128)(2,1)}) %reduce-scatter.22.cloned.1.call-update) | async-done | bytes 786448 | tf_op jit(solution)/shard_map/reduce_scatter | solution.py:140
  561.8 3.9 fusion.81
  566.9 2.5 multiply_convert_fusion.8
  569.6 28.6 %all-gather.11.cloned.1.call-done = bf16[2048,768]{1,0:T(8,128)(2,1)} async-done(((bf16[512,768]{1,0:T(8,128)(2,1)}), bf16[2048,768]{1,0:T(8,128)(2,1)}) %all-gather.11.cloned.1.call-update) | async-done | bytes 3145744 | tf_op jit(solution)/shard_map/all_gather | solution.py:185
  598.2 3.2 convolution_convert_fusion.3
  601.6 4.0 fusion.48
  605.6 4.3 multiply_reduce_fusion.1
  609.9 4.5 multiply_convert_fusion.2
  620.1 4.0 convolution_convert_fusion
  624.5 37.9 %reduce-scatter.26.cloned.1.call-done = bf16[512,768]{1,0:T(8,128)(2,1)} async-done(((bf16[2048,768]{1,0:T(8,128)(2,1)}), bf16[512,768]{1,0:T(8,128)(2,1)}) %reduce-scatter.26.cloned.1.call-update) | async-done | bytes 786448 | tf_op jit(solution)/shard_map/reduce_scatter | solution.py:209
  667.5 2.1 copy-done.11
  669.6 7.2 fusion.75
  677.9 4.1 convolution_bitcast_fusion
  682.7 4.3 convert_reduce_fusion
  687.1 38.6 %all-reduce.2 = bf16[8,576]{1,0:T(8,128)(2,1)S(1)} all-reduce(f32[8,576]{1,0:T(8,128)S(1)} %reshape.203), channel_id=8, replica_groups=mesh['dp'=8,'mp'=4] {'dp'}, use_global_device_ids=true, to_apply=%region_25.26.clone | all-reduce | flops 4608 | bytes 27648
  727.3 180.2 %reduce-scatter.28.cloned.1.call-done = f32[96,4608]{1,0:T(8,128)} async-done(((f32[768,4608]{1,0:T(8,128)}), f32[96,4608]{1,0:T(8,128)}) %reduce-scatter.28.cloned.1.call-update) | async-done | bytes 1769488 | tf_op jit(solution)/shard_map/reduce_scatter | solution.py:237
  910.6 6.9 fusion.88
  917.9 8.3 fusion.78
  926.3 6.7 fusion.20
  933.1 24.3 %fusion.16 = f32[8,768,768]{1,2,0:T(8,128)} fusion(f32[8,768,768]{1,2,0:T(8,128)} %copy.69, f32[8,768]{1,0:T(8,128)S(1)} %copy-done.46, f32[8,768,768]{2,1,0:T(8,128)} %fusion.85), kind=kOutput, calls=%fused_computation.42 | convolution fusion | flops 7299661824 | bytes 56647680 | tf_op jit(solution)/shard_map/ecf,ecd->efd/dot_general | solution.py:164
  957.6 16.7 fusion.89
  976.1 2.2 fusion.37
  978.3 2.4 fusion.80
  982.3 8.3 fusion.43
  990.6 4.0 reduce-scatter.42.cloned.1.call-done
  996.1 26.9 %reduce-scatter.40.cloned.1.call-done = bf16[1152,96]{1,0:T(8,128)(2,1)} async-done(((bf16[4608,96]{1,0:T(8,128)(2,1)}), bf16[1152,96]{1,0:T(8,128)(2,1)}) %reduce-scatter.40.cloned.1.call-update) | async-done | bytes 221200
  1024.9 71.2 %reduce-scatter.32.cloned.1.call-done = f32[96,768]{1,0:T(8,128)} async-done(((f32[768,768]{1,0:T(8,128)}), f32[96,768]{1,0:T(8,128)}) %reduce-scatter.32.cloned.1.call-update) | async-done | bytes 294928 | tf_op jit(solution)/shard_map/reduce_scatter | solution.py:233
  1096.1 72.2 %reduce-scatter.34.cloned.1.call-done = f32[768,96]{0,1:T(8,128)} async-done(((f32[768,768]{0,1:T(8,128)}), f32[768,96]{0,1:T(8,128)}) %reduce-scatter.34.cloned.1.call-update) | async-done | bytes 294928 | tf_op jit(solution)/shard_map/reduce_scatter | solution.py:234
  1168.2 71.9 %reduce-scatter.30.cloned.1.call-done = f32[96,3,192]{2,0,1:T(8,128)} async-done(((f32[768,3,192]{2,0,1:T(8,128)}), f32[96,3,192]{2,0,1:T(8,128)}) %reduce-scatter.30.cloned.1.call-update) | async-done | bytes 221200 | tf_op jit(solution)/shard_map/reduce_scatter | solution.py:231
  1240.1 316.7 %reduce-scatter.38.cloned.1.call-done = f32[8,768,96]{1,2,0:T(8,128)} async-done(((f32[8,768,768]{1,2,0:T(8,128)}), f32[8,768,96]{1,2,0:T(8,128)}) %reduce-scatter.38.cloned.1.call-update) | async-done | bytes 2359312 | tf_op jit(solution)/shard_map/reduce_scatter | solution.py:236
  1556.8 316.8 %reduce-scatter.36.cloned.1.call-done = f32[8,96,768]{2,1,0:T(8,128)} async-done(((f32[8,768,768]{2,1,0:T(8,128)}), f32[8,96,768]{2,1,0:T(8,128)}) %reduce-scatter.36.cloned.1.call-update) | async-done | bytes 2359312 | tf_op jit(solution)/shard_map/reduce_scatter | solution.py:235
  (235 shorter events, 51.9 us)
Async XLA Ops:
  7.2 411.5 %copy-start = (bf16[768,768]{1,0:T(8,128)(2,1)S(1)}, bf16[768,768]{1,0:T(8,128)(2,1)}, u32[]{:S(2)}) copy-start(bf16[768,768]{1,0:T(8,128)(2,1)} %param.24) | copy-start | bytes 3538948
  7.2 46.7 %all-gather.5.cloned.1.call-start = ((), (), s32[]{:S(2)}) async-start(), calls=%async_computation.13 | async-start | bytes 3932160 | tf_op jit(solution)/shard_map/all_gather | solution.py:100
  8.6 8.9 copy-start.36
  10.7 6.8 copy-start.40
  10.7 10.4 copy-start.5
  17.6 3.6 copy-start.7
  21.2 32.7 %copy-start.55 = (bf16[768,3,192]{0,2,1:T(8,128)(2,1)S(1)}, bf16[768,3,192]{0,2,1:T(8,128)(2,1)}, u32[]{:S(2)}) copy-start(bf16[768,3,192]{0,2,1:T(8,128)(2,1)} %param.22) | copy-start | bytes 2654212
  22.5 84.0 %reduce-scatter.20.cloned.1.call-start = ((), (), s32[]{:S(2)}) async-start(), calls=%async_computation.14 | async-start | bytes 3932160 | tf_op jit(solution)/shard_map/reduce_scatter | solution.py:120
  58.8 3.6 copy-start.23
  62.4 3.1 copy-start.30
  68.3 41.2 %copy-start.12 = (bf16[512,768]{1,0:T(8,128)(2,1)S(1)}, bf16[512,768]{1,0:T(8,128)(2,1)}, u32[]{:S(2)}) copy-start(bf16[512,768]{1,0:T(8,128)(2,1)} %param.16) | copy-start | bytes 2359300
  68.4 125.3 %all-gather.9.cloned.1.call-start = ((), (), s32[]{:S(2)}) async-start(), calls=%async_computation.17 | async-start | bytes 3932160 | tf_op jit(solution)/shard_map/all_gather | solution.py:152
  108.5 5.0 copy-start.3
  108.5 5.0 copy-start.38
  109.6 3.9 copy-start.43
  109.6 4.6 copy-start.51
  113.5 4.8 copy-start.52
  113.5 114.3 %all-gather.7.cloned.1.call-start = ((), (), s32[]{:S(2)}) async-start(), calls=%async_computation.15 | async-start | bytes 3932160 | tf_op jit(solution)/shard_map/all_gather | solution.py:127
  114.1 410.1 %reduce-scatter.24.cloned.1.call-start = ((), (), s32[]{:S(2)}) async-start(), calls=%async_computation.18 | async-start | bytes 3932160 | tf_op jit(solution)/shard_map/reduce_scatter | solution.py:173
  118.7 59.1 %copy-start.15 = (f32[2048,2]{1,0:T(8,128)}, f32[2048,2]{1,0:T(8,128)S(1)}, u32[]{:S(2)}) copy-start(f32[2048,2]{1,0:T(8,128)S(1)} %copy.64) | copy-start | bytes 49156
  177.9 114.1 %copy-start.45 = (f32[8,768]{1,0:T(8,128)}, f32[8,768]{1,0:T(8,128)S(1)}, u32[]{:S(2)}) copy-start(f32[8,768]{1,0:T(8,128)S(1)} %mul.332) | copy-start | bytes 73732
  377.4 36.4 %copy-start.53 = (bf16[768,768]{1,0:T(8,128)(2,1)S(1)}, bf16[768,768]{1,0:T(8,128)(2,1)}, u32[]{:S(2)}) copy-start(bf16[768,768]{1,0:T(8,128)(2,1)} %param.25) | copy-start | bytes 3538948
  413.8 4.8 copy-start.25
  413.8 13.9 slice-start.4
  418.7 9.0 slice-start.5
  431.8 130.0 %reduce-scatter.22.cloned.1.call-start = ((), (), s32[]{:S(2)}) async-start(), calls=%async_computation.16 | async-start | bytes 3932160 | tf_op jit(solution)/shard_map/reduce_scatter | solution.py:140
  478.0 15.2 copy-start.16
  493.2 20.5 %copy-start.54 = (bf16[768,768]{1,0:T(8,128)(2,1)S(1)}, bf16[768,768]{1,0:T(8,128)(2,1)}, u32[]{:S(2)}) copy-start(bf16[768,768]{1,0:T(8,128)(2,1)} %param.25) | copy-start | bytes 3538948
  513.7 10.5 copy-start.4
  513.7 10.6 copy-start.39
  524.0 37.8 %copy-start.44 = (f32[512]{0:T(512)S(1)}, f32[512]{0:T(512)}, u32[]{:S(2)}) copy-start(f32[512]{0:T(512)} %copy-done.43) | copy-start | bytes 6148
  524.0 74.2 %all-gather.11.cloned.1.call-start = ((), (), s32[]{:S(2)}) async-start(), calls=%async_computation.19 | async-start | bytes 3932160 | tf_op jit(solution)/shard_map/all_gather | solution.py:185
  526.3 40.6 %copy-start.13 = (bf16[512,768]{1,0:T(8,128)(2,1)S(1)}, bf16[512,768]{1,0:T(8,128)(2,1)}, u32[]{:S(2)}) copy-start(bf16[512,768]{1,0:T(8,128)(2,1)} %param.16) | copy-start | bytes 2359300
  565.8 3.8 copy-start.33
  565.8 3.8 copy-start.35
  565.8 32.4 %copy-start.31 = (bf16[192,768]{1,0:T(8,128)(2,1)S(1)}, bf16[192,768]{1,0:T(8,128)(2,1)}, u32[]{:S(2)}) copy-start(bf16[192,768]{1,0:T(8,128)(2,1)} %param.23) | copy-start | bytes 884740
  569.5 92.9 %reduce-scatter.26.cloned.1.call-start = ((), (), s32[]{:S(2)}) async-start(), calls=%async_computation.20 | async-start | bytes 3932160 | tf_op jit(solution)/shard_map/reduce_scatter | solution.py:209
  598.2 7.4 slice-start
  601.4 4.2 slice-start.1
  601.4 4.2 copy-start.24
  609.9 4.5 copy-start.22
  616.5 3.7 copy-start.56
  624.2 39.5 %copy-start.6 = (bf16[512,768]{1,0:T(8,128)(2,1)S(1)}, bf16[512,768]{1,0:T(8,128)(2,1)}, u32[]{:S(2)}) copy-start(bf16[512,768]{1,0:T(8,128)(2,1)} %param.14) | copy-start | bytes 2359300
  624.2 39.5 %copy-start.37 = (f32[512]{0:T(512)S(1)}, f32[512]{0:T(512)}, u32[]{:S(2)}) copy-start(f32[512]{0:T(512)} %copy-done.36) | copy-start | bytes 6148
  624.2 39.5 %copy-start.41 = (f32[512]{0:T(512)S(1)}, f32[512]{0:T(512)}, u32[]{:S(2)}) copy-start(f32[512]{0:T(512)} %copy-done.40) | copy-start | bytes 6148
  624.2 283.3 %reduce-scatter.28.cloned.1.call-start = ((), (), s32[]{:S(2)}) async-start(), calls=%async_computation.21 | async-start | bytes 15925248 | tf_op jit(solution)/shard_map/reduce_scatter | solution.py:237
  662.3 4.5 copy-start.14
  665.2 4.4 copy-start.28
  676.8 5.3 copy-start.57
  676.8 297.5 %reduce-scatter.44.cloned.1.call-start = ((), (), s32[]{:S(2)}) async-start(), calls=%async_computation.29 | async-start | bytes 884736
  682.0 312.6 %reduce-scatter.42.cloned.1.call-start = ((), (), s32[]{:S(2)}) async-start(), calls=%async_computation.28 | async-start | bytes 184320
  727.2 295.8 %reduce-scatter.40.cloned.1.call-start = ((), (), s32[]{:S(2)}) async-start(), calls=%async_computation.27 | async-start | bytes 1474560
  910.5 185.6 %reduce-scatter.32.cloned.1.call-start = ((), (), s32[]{:S(2)}) async-start(), calls=%async_computation.23 | async-start | bytes 2654208 | tf_op jit(solution)/shard_map/reduce_scatter | solution.py:233
  917.5 250.8 %reduce-scatter.34.cloned.1.call-start = ((), (), s32[]{:S(2)}) async-start(), calls=%async_computation.24 | async-start | bytes 2654208 | tf_op jit(solution)/shard_map/reduce_scatter | solution.py:234
  926.3 313.9 %reduce-scatter.30.cloned.1.call-start = ((), (), s32[]{:S(2)}) async-start(), calls=%async_computation.22 | async-start | bytes 2654208 | tf_op jit(solution)/shard_map/reduce_scatter | solution.py:231
  926.3 6.7 copy-start.46
  933.0 623.8 %reduce-scatter.38.cloned.1.call-start = ((), (), s32[]{:S(2)}) async-start(), calls=%async_computation.26 | async-start | bytes 21233664 | tf_op jit(solution)/shard_map/reduce_scatter | solution.py:236
  957.3 916.3 %reduce-scatter.36.cloned.1.call-start = ((), (), s32[]{:S(2)}) async-start(), calls=%async_computation.25 | async-start | bytes 21233664 | tf_op jit(solution)/shard_map/reduce_scatter | solution.py:235
  974.2 4.1 copy-start.48
  974.3 6.5 copy-start.10
  976.1 6.2 slice-start.2
  978.3 4.0 slice-start.3
  978.3 3.9 copy-start.29
  982.3 891.4 %copy-start.1 = (bf16[768,768]{1,0:T(8,128)(2,1)S(1)}, bf16[768,768]{1,0:T(8,128)(2,1)}, u32[]{:S(2)}) copy-start(bf16[768,768]{1,0:T(8,128)(2,1)} %param.24) | copy-start | bytes 3538948
  (18 other events, 29.8 us)
Sparse Core Ops, SparseCore 0:
  22.6 31.2 all-gather.4
  68.5 37.9 reduce-scatter.19
  113.7 28.5 all-gather.8
  143.7 28.5 all-gather.6
  431.9 37.7 reduce-scatter.23
  524.1 37.6 reduce-scatter.21
  569.6 28.5 all-gather.10
  624.3 37.9 reduce-scatter.25
  676.9 230.5 reduce-scatter.27
  911.2 61.5 reduce-scatter.43
  976.0 18.5 reduce-scatter.41
  997.2 25.6 reduce-scatter.39
  1027.1 68.9 reduce-scatter.31
  1100.0 68.1 reduce-scatter.33
  1172.2 67.9 reduce-scatter.29
  1244.4 312.3 reduce-scatter.37
  1561.1 312.4 reduce-scatter.35
where the time goes:
time: 1890 us; the launch traced here: 1880 us
  waiting for transfers between devices  1230 us (65%)
  local copies, waits for them, and re-layouts  266 us (14%)
  matrix products  222 us (12%)
  other arithmetic  105 us (6%)
  blocking collectives  38.6 us (2%)
    reduce_scatter x1, waiting for transfers between devices, local(): lax.psum_scatter(expert_up_grad, 'dp', scatter_dimension=1, tiled=True)  317 us
    reduce_scatter x1, waiting for transfers between devices, local(): lax.psum_scatter(expert_down_grad, 'dp', scatter_dimension=2, tiled=True)  317 us
    reduce_scatter x1, waiting for transfers between devices, local(): lax.psum_scatter(ada_grad, 'dp', scatter_dimension=0, tiled=True)  180 us
    reduce_scatter x1, waiting for transfers between devices, local(): lax.psum_scatter(shared_down_grad, 'dp', scatter_dimension=1, tiled=True)  72.2 us
    reduce_scatter x1, waiting for transfers between devices, local(): lax.psum_scatter(qkv_weight_grad, 'dp', scatter_dimension=0, tiled=True)  71.9 us
    reduce_scatter x1, waiting for transfers between devices, local(): lax.psum_scatter(shared_up_grad, 'dp', scatter_dimension=0, tiled=True)  71.2 us
    gather x2, local copies, waits for them, and re-layouts, local(): routed = jnp.sum(gate_values[:, :, None] * expert_out[rows_place], axis=1)  41.9 us
    gather x2, local copies, waits for them, and re-layouts, local(): slot_back[rows_place]  41.8 us
  transfers between devices with their start and end apart: 17, of which 13 were waited for; matrix products, arithmetic and copies ran while one was open for 16% of the time, Pallas kernels for 0%

commit v1 on v0

v1 whole, which is shorter than its diff:
```python
import functools

import jax
import jax.numpy as jnp
from jax import lax
from jax.experimental import pallas as pl
from jax.experimental.pallas import tpu as pltpu
from jax.sharding import PartitionSpec as P

HEAD_DIM = 64
BF16 = jnp.bfloat16
F32 = jnp.float32
GELU_A = 0.7978845608028654
GELU_B = 0.044715


def nn(a, b):
    return lax.dot_general(a, b, (((1,), (0,)), ((), ())), preferred_element_type=F32)


def nt(a, b):
    return lax.dot_general(a, b, (((1,), (1,)), ((), ())), preferred_element_type=F32)


def tn(a, b):
    return lax.dot_general(a, b, (((0,), (0,)), ((), ())), preferred_element_type=F32)


def cost(flops, bytes_accessed, transcendentals):
    share = 16
    return pl.CostEstimate(
        flops=flops // share, bytes_accessed=bytes_accessed // share, transcendentals=transcendentals // share
    )


def swap(value, axis, mask):
    size = lax.axis_size(axis)
    return lax.ppermute(value, axis, [(i, i ^ mask) for i in range(size)])


def halves_evenly(n_dp, rows):
    return n_dp == 8 and rows % 16 == 0


def dp_steps(n_dp):
    return [("dp", 1 << bit) for bit in range(n_dp.bit_length() - 1)]


def block_order(steps):
    order = [(0, 0)]
    for axis, mask in reversed(steps):
        order = order + [(d ^ mask, m) if axis == "dp" else (d, m ^ mask) for d, m in order]
    return order


def flip(index, mask):
    bit = 1
    while bit <= mask:
        if mask & bit:
            index = index + bit * (1 - 2 * ((index // bit) % 2))
        bit *= 2
    return index


class Chain:
    def __init__(self, keep, send, steps):
        self.keep, self.send, self.steps, self.step = keep, send, steps, 0

    def take(self, results):
        if self.step == len(self.steps):
            self.result = results.pop(0)[0]
        else:
            self.keep, self.send = results.pop(0), results.pop(0)

    def advance(self):
        got = swap(self.send, *self.steps[self.step])
        total = self.keep.astype(F32) + got.astype(F32)
        half = total.shape[0] // 2
        self.step += 1
        self.take([total[:half].astype(BF16), total[half:].astype(BF16)] if half else [total])

    def finish(self):
        while self.step < len(self.steps):
            self.advance()
        return self.result


class Exchange:
    def __init__(self, jobs):
        self.jobs = jobs
        self.operands, self.in_specs, self.out_specs, self.shapes, self.scratch = [], [], [], [], []
        self.plans = []
        for chain, count in jobs:
            blocks, tail = chain.keep.shape[0], chain.keep.shape[1:]
            steps = chain.steps[chain.step : chain.step + count]
            final = chain.step + count == len(chain.steps)
            self.plans.append((steps, final, blocks, tail))
            self.operands += [chain.keep, chain.send]
            self.in_specs += [pl.BlockSpec(memory_space=pl.ANY)] * 2
            left = blocks >> (count if not final else count - 1)
            kept = jax.ShapeDtypeStruct((left,) + tail, F32 if final else BF16)
            outs = [kept] if final else [kept, kept]
            self.shapes += outs
            self.out_specs += [pl.BlockSpec(kept.shape, lambda *_: (0, 0, 0))] * len(outs)
            self.scratch.append(pltpu.VMEM((blocks,) + tail, BF16))
            self.scratch += [pltpu.VMEM((blocks >> n,) + tail, BF16) for n in range(count)]
            self.scratch += [
                pltpu.SemaphoreType.DMA((1,)),
                pltpu.SemaphoreType.DMA((count,)),
                pltpu.SemaphoreType.DMA((count,)),
            ]

    def bind(self, ins, outs, scratch):
        self.ins, self.outs, self.buffers, self.at = [], [], [], [0] * len(self.jobs)
        for n, (steps, final, _, _) in enumerate(self.plans):
            self.ins.append(ins[2 * n : 2 * n + 2])
            number = 1 if final else 2
            self.outs.append(outs[:number])
            outs = outs[number:]
            number = len(steps) + 4
            self.buffers.append(scratch[:number])
            scratch = scratch[number:]

    @staticmethod
    def partner(axis, mask):
        return {axis: flip(lax.axis_index(axis), mask)}

    def load(self, n):
        return pltpu.make_async_copy(self.ins[n][0], self.buffers[n][0], self.buffers[n][-3].at[0])

    def copy(self, n, step):
        steps, _, blocks, _ = self.plans[n]
        work, send_sems, recv_sems = self.buffers[n][0], self.buffers[n][-2], self.buffers[n][-1]
        number = blocks >> step
        source = self.ins[n][1] if step == 0 else work.at[pl.ds(number, number)]
        return pltpu.make_async_remote_copy(
            src_ref=source,
            dst_ref=self.buffers[n][1 + step],
            send_sem=send_sems.at[step],
            recv_sem=recv_sems.at[step],
            device_id=self.partner(*steps[step]),
            device_id_type=pl.DeviceIdType.MESH,
        )

    def begin(self):
        partners = sorted({step for steps, *_ in self.plans for step in steps})
        if partners:
            barrier = pltpu.get_barrier_semaphore()
            for step in partners:
                pl.semaphore_signal(
                    barrier, inc=1, device_id=self.partner(*step), device_id_type=pl.DeviceIdType.MESH
                )
            pl.semaphore_wait(barrier, len(partners))
        for n in range(len(self.jobs)):
            self.copy(n, 0).start()
            self.load(n).start()

    def advance(self, n):
        steps, final, blocks, _ = self.plans[n]
        step = self.at[n]
        self.at[n] += 1
        work, got = self.buffers[n][0], self.buffers[n][1 + step]
        number = blocks >> step
        if step == 0:
            self.load(n).wait()
        self.copy(n, step).wait()
        half = number // 2
        ending = step == len(steps) - 1

        def add(first, count, target, shift):
            def one(i, carry):
                total = work[i].astype(F32) + got[i].astype(F32)
                target[i - shift] = total.astype(target.dtype)
                return carry

            lax.fori_loop(first, first + count, one, 0)

        if ending and final:
            add(0, number, self.outs[n][0], 0)
        elif ending:
            add(0, half, self.outs[n][0], 0)
            add(half, half, self.outs[n][1], half)
        else:
            add(half, half, work, 0)
            self.copy(n, step + 1).start()
            add(0, half, work, 0)

    def early(self):
        for n, (steps, *_) in enumerate(self.plans):
            while self.at[n] < len(steps) - 1:
                self.advance(n)

    def finish(self):
        for step in range(max([len(steps) for steps, *_ in self.plans], default=0)):
            for n, (steps, *_) in enumerate(self.plans):
                if self.at[n] == step and step < len(steps):
                    self.advance(n)

    def spread(self, results):
        results = list(results)
        for chain, count in self.jobs:
            chain.step += count
            chain.take(results)


def remote(exchange, number, vmem):
    if not exchange.jobs:
        return pltpu.CompilerParams(vmem_limit_bytes=vmem << 20)
    return pltpu.CompilerParams(vmem_limit_bytes=vmem << 20, collective_id=number, has_side_effects=True)


def run_drain(jobs, number):
    exchange = Exchange(jobs)

    def body(*refs):
        ins = len(exchange.operands)
        outs = ins + len(exchange.shapes)
        exchange.bind(refs[:ins], refs[ins:outs], refs[outs:])
        exchange.begin()
        exchange.finish()

    exchange.spread(
        pl.pallas_call(
            body,
            grid=(1,),
            in_specs=exchange.in_specs,
            out_specs=exchange.out_specs,
            out_shape=exchange.shapes,
            scratch_shapes=exchange.scratch,
            compiler_params=remote(exchange, number, 60),
            name="drain",
        )(*exchange.operands)
    )


MP_STEPS = [("mp", 1), ("mp", 2)]
MP_ORDER = [m for _, m in block_order(MP_STEPS)]


def gather_mp(own):
    far = swap(own, "mp", 2)
    return [own, far, swap(own, "mp", 1), swap(far, "mp", 1)]


def normalize(values):
    center = values - jnp.mean(values, axis=-1, keepdims=True)
    inverse = lax.rsqrt(jnp.mean(center * center, axis=-1, keepdims=True) + 1e-06)
    return center * inverse, inverse


def normalize_back(normal, inverse, grad):
    return inverse * (
        grad
        - jnp.mean(grad, axis=-1, keepdims=True)
        - normal * jnp.mean(grad * normal, axis=-1, keepdims=True)
    )


def forward_kernel(
    heads, base, shift_one, scale_one, gate_one, shift_two, scale_two, seg_col, seg_row, *refs
):
    weights, out_weights = refs[:4], refs[4:8]
    normed_out, qkv, attended, lse_out, attn_out, second_out = refs[8], refs[9:13], *refs[13:]
    span = heads * HEAD_DIM
    x = base[...].astype(F32)
    normed = (normalize(x)[0] * (1.0 + scale_one[...]) + shift_one[...]).astype(BF16)
    normed_out[...] = normed
    same = seg_col[0] == seg_row[0]
    lane = lax.broadcasted_iota(jnp.int32, (1, 128), 1)
    lse_all = jnp.zeros(lse_out.shape, F32)
    attn = jnp.zeros(x.shape, F32)
    for block in range(4):
        qkv[block][...] = nn(normed, weights[block][...]).astype(BF16)
        for head in range(heads):
            at = head * HEAD_DIM
            q = qkv[block][:, at : at + HEAD_DIM]
            k = qkv[block][:, span + at : span + at + HEAD_DIM]
            v = qkv[block][:, 2 * span + at : 2 * span + at + HEAD_DIM]
            scores = jnp.where(same, nt(q, k) * (HEAD_DIM**-0.5), -1000000000.0)
            top = jnp.max(scores, axis=-1, keepdims=True)
            expo = jnp.exp(scores - top)
            total = jnp.sum(expo, axis=-1, keepdims=True)
            light = (expo * (1.0 / total)).astype(BF16)
            start = block * span + at
            attended[:, start : start + HEAD_DIM] = nn(light, v).astype(BF16)
            lse_all = jnp.where(lane == block * heads + head, top + jnp.log(total), lse_all)
        attn += nn(attended[:, block * span : (block + 1) * span], out_weights[block][...])
    lse_out[...] = lse_all
    attn_out[...] = attn
    middle = x + gate_one[...] * attn
    second_out[...] = (normalize(middle)[0] * (1.0 + scale_two[...]) + shift_two[...]).astype(BF16)


def rows_of(owner, rows):
    return pl.multiple_of(flip(lax.axis_index("dp"), owner) * rows, 8)


def store_blocks(order, m, total, halves, rows):
    half = len(order) // 2
    for place, owner in enumerate(order):
        if owner[1] == m:
            start = 0 if rows == total.shape[0] else rows_of(owner[0], rows)
            halves[place // half][place % half, :rows, :] = total[pl.ds(start, rows), :].astype(BF16)


def row_block(seq, columns):
    return pl.BlockSpec((seq, columns), lambda i, *_: (i, 0))


def column_block(seq, width, number):
    return pl.BlockSpec((seq, width), lambda i, *_: (i, number))


def whole_block(array):
    return pl.BlockSpec(array.shape, lambda i, *_: (0,) * array.ndim, pipeline_mode=pl.Buffered(1))


def segment_blocks(seq):
    return [
        pl.BlockSpec((1, seq, 1), lambda i, *_: (i, 0, 0)),
        pl.BlockSpec((1, 1, seq), lambda i, *_: (i, 0, 0)),
    ]


def run_forward(patches, modulation, segments, qkv_parts, out_parts):
    rows, seq = segments.shape
    tokens, width = patches.shape
    columns = qkv_parts[0].shape[1]
    heads = columns // (3 * HEAD_DIM)
    work = rows * 4 * heads * seq * seq
    shapes = (
        [(width, BF16)] + [(columns, BF16)] * 4 + [(width, BF16), (128, F32), (width, F32), (width, BF16)]
    )
    return pl.pallas_call(
        functools.partial(forward_kernel, heads),
        grid=(rows,),
        in_specs=[row_block(seq, width)]
        + [column_block(seq, width, n) for n in range(5)]
        + segment_blocks(seq)
        + [whole_block(w) for w in qkv_parts + out_parts],
        out_specs=[row_block(seq, c) for c, _ in shapes],
        out_shape=[jax.ShapeDtypeStruct((tokens, c), t) for c, t in shapes],
        compiler_params=pltpu.CompilerParams(vmem_limit_bytes=48 << 20),
        cost_estimate=cost(
            flops=4 * work * HEAD_DIM + 8 * tokens * width * width,
            bytes_accessed=40 * tokens * width,
            transcendentals=work,
        ),
        name="attention_half",
    )(
        patches,
        *([modulation] * 5),
        segments[:, :, None],
        segments[:, None, :],
        *qkv_parts,
        *out_parts,
    )


def middle_back_kernel(
    base, gate_one, scale_two, attn, cotangent, kept, got, _, middle_grad, attn_grad, pieces
):
    width = base.shape[1]
    grad = kept[0].astype(F32) + got[0].astype(F32)
    branch = attn[...]
    gate = gate_one[...]
    normal, inverse = normalize(base[...].astype(F32) + gate * branch)
    total = cotangent[...].astype(F32) + normalize_back(
        normal, inverse, grad * (1.0 + scale_two[...])
    )
    middle_grad[...] = total
    attn_grad[...] = (total * gate).astype(BF16)
    pieces[:, :width] = (total * branch).astype(BF16)
    pieces[:, width : 2 * width] = grad.astype(BF16)
    pieces[:, 2 * width :] = (grad * normal).astype(BF16)


def run_middle_back(patches, modulation, attn, cotangent, kept, got, after):
    tokens, width = patches.shape
    seq = tokens // 2
    wide = row_block(seq, width)
    return pl.pallas_call(
        middle_back_kernel,
        grid=(2,),
        in_specs=[
            wide,
            column_block(seq, width, 2),
            column_block(seq, width, 4),
            wide,
            wide,
            pl.BlockSpec((1, seq, width), lambda i: (0, i, 0)),
            pl.BlockSpec((1, seq, width), lambda i: (0, i, 0)),
            pl.BlockSpec(memory_space=pl.ANY),
        ],
        out_specs=[wide, wide, row_block(seq, 3 * width)],
        out_shape=[
            jax.ShapeDtypeStruct((tokens, width), F32),
            jax.ShapeDtypeStruct((tokens, width), BF16),
            jax.ShapeDtypeStruct((tokens, 3 * width), BF16),
        ],
        compiler_params=pltpu.CompilerParams(vmem_limit_bytes=32 << 20),
        cost_estimate=cost(
            flops=40 * tokens * width, bytes_accessed=36 * tokens * width, transcendentals=0
        ),
        name="middle_back",
    )(patches, modulation, modulation, attn, cotangent, kept, got, after)


def attention_back_kernel(
    heads, exchange, order, rows, base, scale_one, middle_grad, attn_grad, normed, attended, lse, seg_col, seg_row, *refs
):
    qkv, weights, out_weights = refs[:4], refs[4:8], refs[8:12]
    number = len(exchange.operands)
    moved, refs = refs[12 : 12 + number], refs[12 + number :]
    patches_grad, pieces, halves, refs = refs[0], refs[1], refs[2:4], refs[4:]
    number = len(exchange.shapes)
    moved_out, refs = refs[:number], refs[number:]
    totals, grad_qkv, refs = refs[:4], refs[4], refs[5:]
    step, last = pl.program_id(0), pl.num_programs(0) - 1
    exchange.bind(moved, moved_out, refs)

    @pl.when(step == 0)
    def _():
        exchange.begin()

    span = heads * HEAD_DIM
    width = base.shape[1]
    factor = HEAD_DIM**-0.5
    same = seg_col[0] == seg_row[0]
    upper = attn_grad[...]
    normed_grad = jnp.zeros(base.shape, F32)
    for block in range(4):
        if block == 3:

            @pl.when(step == last)
            def _():
                exchange.early()

        grad_heads = nt(upper, out_weights[block][...]).astype(BF16)
        for head in range(heads):
            at = head * HEAD_DIM
            n = block * heads + head
            q = qkv[block][:, at : at + HEAD_DIM]
            k = qkv[block][:, span + at : span + at + HEAD_DIM]
            v = qkv[block][:, 2 * span + at : 2 * span + at + HEAD_DIM]
            g = grad_heads[:, at : at + HEAD_DIM]
            scores = jnp.where(same, nt(q, k) * factor, -1000000000.0)
            probs = jnp.exp(scores - lse[:, n : n + 1])
            grad_probs = nt(g, v)
            term = jnp.sum(probs * grad_probs, axis=-1, keepdims=True)
            grad_scores = (probs * (grad_probs - term)).astype(BF16)
            grad_qkv[:, at : at + HEAD_DIM] = (nn(grad_scores, k) * factor).astype(BF16)
            grad_qkv[:, span + at : span + at + HEAD_DIM] = (tn(grad_scores, q) * factor).astype(BF16)
            grad_qkv[:, 2 * span + at : 2 * span + at + HEAD_DIM] = tn(
                probs.astype(BF16), g
            ).astype(BF16)
        made = grad_qkv[...]
        normed_grad += nt(made, weights[block][...])
        of_qkv = tn(normed[...], made)
        of_out = tn(upper, attended[:, block * span : (block + 1) * span])

        @pl.when(step == 0)
        def _():
            totals[block][:, : 3 * span] = of_qkv
            totals[block][:, 3 * span :] = of_out

        @pl.when(step > 0)
        def _():
            totals[block][:, : 3 * span] += of_qkv
            totals[block][:, 3 * span :] += of_out

        @pl.when(step == last)
        def _():
            store_blocks(order, MP_ORDER[block], totals[block], halves, rows)

    normal, inverse = normalize(base[...].astype(F32))
    patches_grad[...] = middle_grad[...] + normalize_back(
        normal, inverse, normed_grad * (1.0 + scale_one[...])
    )
    pieces[:, :width] = normed_grad.astype(BF16)
    pieces[:, width:] = (normed_grad * normal).astype(BF16)

    @pl.when(step == last)
    def _():
        exchange.finish()


def run_attention_back(
    patches,
    modulation,
    middle_grad,
    attn_grad,
    normed,
    attended,
    lse,
    segments,
    qkv,
    qkv_parts,
    out_parts,
    order,
    rows,
    jobs,
    number,
):
    count, seq = segments.shape
    tokens, width = patches.shape
    columns = qkv[0].shape[1]
    heads = columns // (3 * HEAD_DIM)
    work = count * 4 * heads * seq * seq
    wide = row_block(seq, width)
    half = (len(order) // 2, rows, 4 * columns // 3)
    exchange = Exchange(jobs)
    results = pl.pallas_call(
        functools.partial(attention_back_kernel, heads, exchange, order, rows),
        grid_spec=pltpu.PrefetchScalarGridSpec(
            num_scalar_prefetch=0,
            grid=(count,),
            in_specs=[wide, column_block(seq, width, 1), wide, wide, wide, wide, row_block(seq, 128)]
            + segment_blocks(seq)
            + [row_block(seq, columns)] * 4
            + [whole_block(w) for w in qkv_parts + out_parts]
            + exchange.in_specs,
            out_specs=[wide, row_block(seq, 2 * width)]
            + [pl.BlockSpec(half, lambda i, *_: (0, 0, 0))] * 2
            + exchange.out_specs,
            scratch_shapes=[pltpu.VMEM((width, 4 * columns // 3), F32)] * 4
            + [pltpu.VMEM((seq, columns), BF16)]
            + exchange.scratch,
        ),
        out_shape=[
            jax.ShapeDtypeStruct((tokens, width), F32),
            jax.ShapeDtypeStruct((tokens, 2 * width), BF16),
        ]
        + [jax.ShapeDtypeStruct(half, BF16)] * 2
        + exchange.shapes,
        compiler_params=remote(exchange, number, 62),
        cost_estimate=cost(
            flops=10 * work * HEAD_DIM + 16 * tokens * width * width,
            bytes_accessed=60 * tokens * width,
            transcendentals=work,
        ),
        name="attention_back",
    )(
        patches,
        modulation,
        middle_grad,
        attn_grad,
        normed,
        attended,
        lse,
        segments[:, :, None],
        segments[:, None, :],
        *qkv,
        *qkv_parts,
        *out_parts,
        *exchange.operands,
    )
    exchange.spread(results[4:])
    return results[:4]


BIAS_ROWS = 16


def ada_kernel(orders, rows, cond, *refs):
    pieces, bias, halves, total = refs[:4], refs[4], refs[5:9], refs[9]
    for m in range(4):
        for part in range(2):
            split = pieces[m].shape[1] // 2
            total[...] = tn(cond[...], pieces[m][:, part * split : (part + 1) * split])
            store_blocks(orders[part], m, total, halves[2 * part : 2 * part + 2], rows)
    half = len(orders[0]) // 2
    for place in range(len(orders[0])):
        halves[place // half][place % half, rows:, :] = jnp.broadcast_to(
            bias[place], (BIAS_ROWS, bias.shape[2])
        ).astype(BF16)


def run_ada(silu_cond, grad_modulation, bias, orders, pieces_of, rows):
    tokens, width = silu_cond.shape
    columns = grad_modulation.shape[1] // 4
    half = len(orders[0]) // 2
    shapes = [(half, rows + BIAS_ROWS, columns // 2)] * 2 + [(half, rows, columns // 2)] * 2

    def piece(m):
        return pl.BlockSpec((tokens, columns), lambda i, p: (0, p[m]))

    return pl.pallas_call(
        lambda _, *refs: ada_kernel(orders, rows, *refs),
        grid_spec=pltpu.PrefetchScalarGridSpec(
            num_scalar_prefetch=1,
            grid=(1,),
            in_specs=[whole_block(silu_cond)] + [piece(m) for m in range(4)] + [whole_block(bias)],
            out_specs=[pl.BlockSpec(shape, lambda i, *_: (0, 0, 0)) for shape in shapes],
            scratch_shapes=[pltpu.VMEM((width, columns // 2), F32)],
        ),
        out_shape=[jax.ShapeDtypeStruct(shape, BF16) for shape in shapes],
        compiler_params=pltpu.CompilerParams(vmem_limit_bytes=60 << 20),
        cost_estimate=cost(
            flops=8 * tokens * width * columns, bytes_accessed=20 * width * columns, transcendentals=0
        ),
        name="ada_grads",
    )(pieces_of, silu_cond, *([grad_modulation] * 4), bias)


def gelu_and_slope(values):
    square = values * values
    bent = jnp.tanh(values * (GELU_A + (GELU_A * GELU_B) * square))
    half = 0.5 * (1.0 + bent)
    active = values * half
    return active, half + active * (1.0 - bent) * (GELU_A + (3.0 * GELU_A * GELU_B) * square)


def expert_kernel(columns, first, last, grad_later, exchange, orders, rows, *refs):
    count = len(columns)
    gates, tokens, grads = refs[:3]
    ups, downs, refs = refs[3 : 3 + count], refs[3 + count : 3 + 2 * count], refs[3 + 2 * count :]
    if not first:
        old_out, old_back, refs = refs[0], refs[1], refs[2:]
    number = len(exchange.operands)
    moved, refs = refs[:number], refs[number:]
    halves, refs = refs[: 2 * count], refs[2 * count :]
    out, back, refs = refs[0], refs[1], refs[2:]
    number = len(exchange.shapes)
    moved_out, refs = refs[:number], refs[number:]
    number = 0 if grad_later else 2 * count
    sums, refs = refs[:number], refs[number:]
    step, final = pl.program_id(0), pl.num_programs(0) - 1
    exchange.bind(moved, moved_out, refs)

    @pl.when(step == 0)
    def _():
        exchange.begin()

    @pl.when(step == final)
    def _():
        exchange.early()

    if not grad_later:
        start_sums(step, sums)
    x = tokens[...]
    g32 = grads[...].astype(F32)
    routed = None if first else old_out[...]
    returned = None if first else old_back[...]
    for n, column in enumerate(columns):
        gate = gates[:, column : column + 1]
        slot_grad = (gate * g32).astype(BF16)
        pre = nn(x, ups[n][0])
        grad_hidden = nt(slot_grad, downs[n][0])
        hidden, slope = gelu_and_slope(pre)
        hidden = hidden.astype(BF16)
        grad_pre = (grad_hidden * slope).astype(BF16)
        one = gate * nn(hidden, downs[n][0])
        two = nt(grad_pre, ups[n][0])
        routed = one if routed is None else routed + one
        returned = two if returned is None else returned + two
        if grad_later:
            halves[2 * n][...] = hidden
            halves[2 * n + 1][...] = grad_pre
        else:
            sums[2 * n][...] += tn(x, grad_pre)
            sums[2 * n + 1][...] += tn(slot_grad, hidden)
    out[...] = routed.astype(out.dtype)
    back[...] = returned.astype(back.dtype)
    if not grad_later:
        store_halves(step, orders, sums, halves, rows)

    @pl.when(step == final)
    def _():
        exchange.finish()


def start_sums(step, sums):
    @pl.when(step == 0)
    def _():
        for total in sums:
            total[...] = jnp.zeros_like(total)


def store_halves(step, orders, sums, halves, rows):
    @pl.when(step == pl.num_programs(0) - 1)
    def _():
        for n, order in enumerate(orders):
            half = len(order) // 2
            for place, owner in enumerate(order):
                start = place * rows if half == 1 else rows_of(owner, rows)
                for part in range(2):
                    halves[2 * n + place // half][place % half, part * rows : (part + 1) * rows, :] = sums[
                        2 * n + part
                    ][pl.ds(start, rows), :].astype(BF16)


TILE = 512


def token_tiles(columns):
    return pl.BlockSpec((TILE, columns), lambda t: (t, 0))


def run_experts(columns, weights, orders, rows, gates, tokens, grads, sums, last, grad_later, jobs, number):
    count = len(columns)
    total, width = tokens.shape
    hidden = weights[0][0].shape[2]
    steps = total // TILE
    blocks = width // rows // 2
    first = sums is None
    exchange = Exchange(jobs)

    def weight(index, shape):
        return pl.BlockSpec((1,) + shape, lambda t: (index, 0, 0), pipeline_mode=pl.Buffered(1))

    in_specs = (
        [token_tiles(gates.shape[1]), token_tiles(width), token_tiles(width)]
        + [weight(i, (width, hidden)) for _, _, i in weights]
        + [weight(i, (hidden, width)) for _, _, i in weights]
        + ([] if first else [token_tiles(width), token_tiles(width)])
    )
    given = len(in_specs)
    if grad_later:
        half, half_shape = token_tiles(hidden), (total, hidden)
    else:
        half_shape = (blocks, 2 * rows, hidden)
        half = pl.BlockSpec(half_shape, lambda t: (0, 0, 0))
    made = 2 * count
    aliases = {} if first or last else {given - 2: made, given - 1: made + 1}
    results = pl.pallas_call(
        functools.partial(expert_kernel, columns, first, last, grad_later, exchange, orders, rows),
        grid_spec=pltpu.PrefetchScalarGridSpec(
            num_scalar_prefetch=0,
            grid=(steps,),
            in_specs=in_specs + exchange.in_specs,
            out_specs=[half] * made + [token_tiles(width), token_tiles(width)] + exchange.out_specs,
            scratch_shapes=([] if grad_later else [pltpu.VMEM((width, hidden), F32)] * (2 * count))
            + exchange.scratch,
        ),
        out_shape=[jax.ShapeDtypeStruct(half_shape, BF16)] * made
        + [jax.ShapeDtypeStruct((total, width), BF16 if last else F32)] * 2
        + exchange.shapes,
        input_output_aliases=aliases,
        compiler_params=remote(exchange, number, 60),
        cost_estimate=cost(
            flops=(8 if grad_later else 12) * count * total * width * hidden,
            bytes_accessed=20 * total * width + 8 * count * width * hidden,
            transcendentals=count * total * hidden,
        ),
        name=f"experts_{count}",
    )(
        gates,
        tokens,
        grads,
        *[up for up, _, _ in weights],
        *[down for _, down, _ in weights],
        *(() if first else sums),
        *exchange.operands,
    )
    exchange.spread(results[made + 2 :])
    return results[:made], results[made : made + 2]


def expert_grads_kernel(columns, exchange, waits, orders, rows, *refs):
    count = len(columns)
    gates, tokens, grads = refs[:3]
    saved, refs = refs[3 : 3 + 2 * count], refs[3 + 2 * count :]
    number = len(exchange.operands)
    moved, refs = refs[:number], refs[number + waits :]
    halves, refs = refs[: 2 * count], refs[2 * count :]
    number = len(exchange.shapes)
    moved_out, refs = refs[:number], refs[number:]
    sums, refs = refs[: 2 * count], refs[2 * count :]
    step, final = pl.program_id(0), pl.num_programs(0) - 1
    exchange.bind(moved, moved_out, refs)

    @pl.when(step == 0)
    def _():
        exchange.begin()

    start_sums(step, sums)
    x = tokens[...]
    g32 = grads[...].astype(F32)
    for n, column in enumerate(columns):
        slot_grad = (gates[:, column : column + 1] * g32).astype(BF16)
        sums[2 * n][...] += tn(x, saved[2 * n + 1][...])
        sums[2 * n + 1][...] += tn(slot_grad, saved[2 * n][...])
    store_halves(step, orders, sums, halves, rows)

    @pl.when(step == final)
    def _():
        exchange.finish()


def run_expert_grads(columns, saved, orders, rows, gates, tokens, grads, jobs, after, number):
    count = len(columns)
    total, width = tokens.shape
    hidden = saved[0].shape[1]
    steps = total // TILE
    half_shape = (width // rows // 2, 2 * rows, hidden)
    exchange = Exchange(jobs)
    results = pl.pallas_call(
        functools.partial(expert_grads_kernel, columns, exchange, len(after), orders, rows),
        grid_spec=pltpu.PrefetchScalarGridSpec(
            num_scalar_prefetch=0,
            grid=(steps,),
            in_specs=[token_tiles(gates.shape[1]), token_tiles(width), token_tiles(width)]
            + [token_tiles(hidden)] * (2 * count)
            + exchange.in_specs
            + [pl.BlockSpec(memory_space=pl.ANY)] * len(after),
            out_specs=[pl.BlockSpec(half_shape, lambda t: (0, 0, 0))] * (2 * count)
            + exchange.out_specs,
            scratch_shapes=[pltpu.VMEM((width, hidden), F32)] * (2 * count) + exchange.scratch,
        ),
        out_shape=[jax.ShapeDtypeStruct(half_shape, BF16)] * (2 * count) + exchange.shapes,
        compiler_params=remote(exchange, number, 60),
        cost_estimate=cost(
            flops=4 * count * total * width * hidden,
            bytes_accessed=(4 + 4 * count) * total * width,
            transcendentals=0,
        ),
        name="expert_grads",
    )(gates, tokens, grads, *saved, *exchange.operands, *after)
    exchange.spread(results[2 * count :])
    return results[: 2 * count]


def local(
    patches,
    conditioning,
    cotangent,
    segments,
    routes,
    gate_values,
    ada_weight,
    ada_bias,
    qkv_weight,
    out_weight,
    shared_up,
    shared_down,
    expert_up,
    expert_down,
):
    tokens, width = patches.shape
    group = routes.shape[0]
    experts = expert_up.shape[0]
    seq = segments.shape[1]
    n_dp, n_mp = lax.axis_size("dp"), lax.axis_size("mp")
    dp, mp = lax.axis_index("dp"), lax.axis_index("mp")
    rows = width // n_dp

    qkv_parts = gather_mp(qkv_weight.reshape(width, -1))
    out_parts = gather_mp(out_weight)

    cond32 = conditioning.astype(F32)
    silu_cond = jax.nn.silu(cond32).astype(BF16)
    modulation = jnp.dot(silu_cond, ada_weight, preferred_element_type=F32) + ada_bias[None, :]
    gate_one, gate_two = modulation[:, 2 * width : 3 * width], modulation[:, 5 * width :]
    grad_out = cotangent.astype(F32)
    grad_mlp = (grad_out * gate_two).astype(BF16)

    own_rows = tokens // seq
    own_segments = lax.dynamic_slice_in_dim(segments, mp * own_rows, own_rows, axis=0)
    results = run_forward(patches, modulation, own_segments, qkv_parts, out_parts)
    normed_one, qkv, attended, lse, attn_out, normed_two = results[0], results[1:5], *results[5:]

    grad_parts = gather_mp(grad_mlp)
    all_tokens = jnp.concatenate(gather_mp(normed_two), axis=0)
    all_grads = jnp.concatenate(grad_parts, axis=0)
    number = jnp.arange(16, dtype=jnp.int32)[None, :]
    gates = jnp.sum(
        jnp.where(routes[:, :, None] == number[:, None, :], gate_values[:, :, None], 0.0), axis=1
    )
    gates = jnp.where(number == experts, 1.0, gates)
    gates = jnp.concatenate(
        [lax.dynamic_slice_in_dim(gates, (mp ^ m) * tokens, tokens, axis=0) for m in MP_ORDER],
        axis=0,
    )
    shared = (shared_up[None], shared_down[None], 0)
    weights = {e: (expert_up, expert_down, e) for e in range(experts)}
    weights[experts] = shared
    calls = [(experts,)] + [(e, e + 1) for e in range(0, experts, 2)]
    even = halves_evenly(n_dp, rows)
    step = rows if even else width // 2
    reduced, chains, wholes = {}, {}, {}

    def steps_of(column):
        steps = dp_steps(n_dp)
        return [steps[1], steps[0]] + steps[2:] if column % 2 else steps

    def orders_of(columns):
        return [[d for d, _ in block_order(steps_of(c))] if even else [0, 1] for c in columns]

    def take_halves(columns, halves):
        for n, column in enumerate(columns):
            if even:
                chains[column] = Chain(halves[2 * n], halves[2 * n + 1], steps_of(column))
            else:
                wholes[column] = halves[2 * n : 2 * n + 2]

    def jobs(**counts):
        if not even:
            return []
        return [(chains[c], int(count[1:])) for count, columns in counts.items() for c in columns]

    sums = None
    riding = [
        {},
        dict(n2=(experts,)),
        dict(n2=(0, 1), n1=(experts,)),
        dict(n2=(2, 3), n1=(0, 1)),
        dict(n1=(4, 5)),
    ]
    for number, columns in enumerate(calls):
        last = number == len(calls) - 1
        halves, sums = run_experts(
            columns,
            [weights[c] for c in columns],
            orders_of(columns),
            step,
            gates,
            all_tokens,
            all_grads,
            sums,
            last,
            last,
            jobs(**riding[number]),
            number,
        )
        if last:
            saved = halves
        else:
            take_halves(columns, halves)
    out_sum, back_sum = [s.reshape(n_mp, tokens, width) for s in sums]
    half = n_mp // 2
    from_core = swap(back_sum[half:], "mp", 1)
    near = (back_sum[:half].astype(F32) + from_core.astype(F32)).astype(BF16)
    far = swap(near[1:], "mp", 2)
    halves = run_expert_grads(
        calls[-1],
        saved,
        orders_of(calls[-1]),
        step,
        gates,
        all_tokens,
        all_grads,
        jobs(n1=(4, 5, 2, 3)),
        [from_core],
        5,
    )
    take_halves(calls[-1], halves)
    middle_grad, attn_grad, pieces_two = run_middle_back(
        patches, modulation, attn_out, cotangent, near[:1], far, halves[0]
    )
    tail_steps = [MP_STEPS] * 3
    if even:
        y, z, rest = dp_steps(n_dp)[0], dp_steps(n_dp)[1], dp_steps(n_dp)[2:]
        core, x = MP_STEPS
        tail_steps = [[core, x, y, z] + rest, [core, z, x, y] + rest, [core, y, z, x] + rest]
    tail_orders = [block_order(steps) for steps in tail_steps]

    tail_rows = rows if even else width
    results = run_attention_back(
        patches,
        modulation,
        middle_grad,
        attn_grad,
        normed_one,
        attended,
        lse,
        own_segments,
        qkv,
        qkv_parts,
        out_parts,
        tail_orders[0],
        tail_rows,
        jobs(n2=(6, 7), n1=(4, 5)),
        6,
    )
    patches_grad, pieces_one, heads_halves = results[0], results[1], results[2:4]
    heads_chain = Chain(*heads_halves, tail_steps[0])
    out_chain = Chain(out_sum[:half], out_sum[half:], MP_STEPS)
    mlp_out = out_chain.finish()
    middle = patches.astype(F32) + gate_one * attn_out
    output = (middle + gate_two * mlp_out).astype(BF16)
    grad_gate_two = (grad_out * mlp_out).astype(BF16)
    grad_modulation = jnp.concatenate([pieces_one, pieces_two, grad_gate_two], axis=1)

    bias = jnp.sum(grad_modulation.astype(F32), axis=0).reshape(n_dp, n_mp, -1)
    if even:
        bias_of = bias[
            jnp.array([d for d, _ in tail_orders[1]]) ^ dp, jnp.array([m for _, m in tail_orders[1]]) ^ mp
        ][:, None]
    else:
        bias_of = jnp.zeros((n_mp, 1, 1), F32)
    piece = grad_modulation.shape[1] // n_mp
    bias_of = jnp.pad(bias_of, ((0, 0), (0, 0), (0, piece // 2 - bias_of.shape[2])))
    ada_halves = run_ada(
        silu_cond,
        grad_modulation,
        bias_of,
        tail_orders[1:],
        (jnp.arange(4, dtype=jnp.int32) ^ mp).astype(jnp.int32),
        tail_rows,
    )
    ada_chains = [Chain(*ada_halves[:2], tail_steps[1]), Chain(*ada_halves[2:], tail_steps[2])]
    cond_grad = nt(grad_modulation, ada_weight)
    _, silu_back = jax.vjp(jax.nn.silu, cond32)
    conditioning_grad = silu_back(cond_grad)[0]

    if even:
        run_drain([(heads_chain, 5)] + [(c, 5) for c in ada_chains] + jobs(n1=(6, 7)), 7)
    heads_sum = heads_chain.finish()
    low, high = [c.finish() for c in ada_chains]
    ada_sum = jnp.concatenate([low[:tail_rows], high], axis=1)
    if even:
        for column, chain in chains.items():
            part = chain.finish()
            reduced[column] = part[:rows], part[rows:]
        bias_sum = low[rows, : bias.shape[2]]
    else:
        for column, (first, second) in wholes.items():
            whole = jnp.stack([first[0], second[0]]).reshape(2, 2, step, -1)
            whole = jnp.swapaxes(whole, 0, 1).reshape(2, width, -1)
            part = lax.psum_scatter(whole, "dp", scatter_dimension=1, tiled=True).astype(F32)
            reduced[column] = part[0], part[1]
        heads_sum, ada_sum = [
            lax.psum_scatter(a.astype(BF16), "dp", scatter_dimension=0, tiled=True).astype(F32)
            for a in (heads_sum, ada_sum)
        ]
        bias_sum = lax.psum_scatter(
            lax.psum_scatter(bias, "dp", scatter_dimension=0, tiled=True), "mp", scatter_dimension=1, tiled=True
        )
    qkv_cols = qkv[0].shape[1]
    qkv_sum = heads_sum[:, :qkv_cols].reshape(rows, 3, -1)
    out_total = heads_sum[:, qkv_cols:].T
    up_sum, down_sum = reduced[experts]
    return (
        output,
        patches_grad,
        conditioning_grad,
        ada_sum,
        bias_sum.reshape(-1),
        qkv_sum,
        out_total,
        up_sum,
        down_sum.T,
        jnp.stack([reduced[e][0] for e in range(experts)]),
        jnp.stack([reduced[e][1].T for e in range(experts)]),
    )


def solution(mesh):
    in_specs = (
        P(("dp", "mp"), None),
        P(("dp", "mp"), None),
        P(("dp", "mp"), None),
        P("dp", None),
        P("dp", None),
        P("dp", None),
        P(),
        P(),
        P(None, None, "mp"),
        P("mp", None),
        P(None, "mp"),
        P("mp", None),
        P(None, None, "mp"),
        P(None, "mp", None),
    )
    out_specs = (
        P(("dp", "mp"), None),
        P(("dp", "mp"), None),
        P(("dp", "mp"), None),
        P("dp", "mp"),
        P(("dp", "mp")),
        P("dp", None, "mp"),
        P("mp", "dp"),
        P("dp", "mp"),
        P("mp", "dp"),
        P(None, "dp", "mp"),
        P(None, "mp", "dp"),
    )
    return jax.shard_map(local, mesh=mesh, in_specs=in_specs, out_specs=out_specs, check_vma=False)
```

time: 1890 us -> 604 us (0.32)
  waiting for transfers between devices: 1230 us -> 39.5 us
  Pallas kernels: 0 us -> 447 us
  matrix products: 222 us -> 17 us
  local copies, waits for them, and re-layouts: 266 us -> 67 us
  other arithmetic: 105 us -> 15 us
  blocking collectives: 38.6 us -> 0 us
    reduce_scatter x10 -> x0, waiting for transfers between devices: 1140 us -> none  [the longest x1 317 us: local(): lax.psum_scatter(expert_up_grad, 'dp', scatter_dimension=1, tiled=True)]
    pallas_call x0 -> x11, Pallas kernels: none -> 447 us  [the longest x5 229 us: run_experts(): pl.pallas_call(functools.partial(expert_kernel, columns, first, last, gra...]
    dot_general x26 -> x2, matrix products: 218 us -> 17 us  [the longest x1 10.2 us: nt(): lax.dot_general(a, b, (((1,), (1,)), ((), ())), preferred_element_type=F32)]
    gather x7 -> x1, local copies, waits for them, and re-layouts: 179 us -> 0.64 us  [local(): bias[jnp.array([d for d, _ in tail_orders[1]]) ^ dp, jnp.array([m for _,...]
    reduce_sum x13 -> x2, other arithmetic: 78.3 us -> 2.63 us  [the longest x1 2.61 us: local(): bias = jnp.sum(grad_modulation.astype(F32), axis=0).reshape(n_dp, n_mp, -1)]
    all_gather x4 -> x0, waiting for transfers between devices: 59.5 us -> none  [the longest x1 30.9 us: local(): gathered_one = lax.all_gather(normed_one, 'mp', axis=0, tiled=True)]
    ppermute x0 -> x16, waiting for transfers between devices: none -> 39.5 us  [swap(): return lax.ppermute(value, axis, [(i, i ^ mask) for i in range(size)])]
    unnamed x1 -> x0, blocking collectives: 38.6 us -> none
  transfers between devices with their start and end apart: 17 -> 16, of which waited for: 13 -> 2; matrix products, arithmetic and copies ran while one was open for 16% -> 8% of each run, Pallas kernels for 0% -> 9%
where the time goes in v1:
time: 604 us; the launch traced here: 597 us
  Pallas kernels  447 us (74%)
  local copies, waits for them, and re-layouts  67 us (11%)
  waiting for transfers between devices  39.5 us (7%)
  matrix products  17 us (3%)
  other arithmetic  15 us (2%)
  starting transfers between devices  9.47 us (2%)
    pallas_call x5, Pallas kernels, run_experts(): pl.pallas_call(functools.partial(expert_kernel, columns, first, last, gra...  229 us
    pallas_call x1, Pallas kernels, run_drain(): pl.pallas_call(body, grid=(1,), in_specs=exchange.in_specs, out_specs=exc...  88.8 us
    pallas_call x1, Pallas kernels, run_attention_back(): pl.pallas_call(functools.partial(attention_back_kernel, heads, exchange,...  62 us
    unnamed x114, local copies, waits for them, and re-layouts  39.6 us
    ppermute x16, waiting for transfers between devices, swap(): return lax.ppermute(value, axis, [(i, i ^ mask) for i in range(size)])  39.5 us
    pallas_call x1, Pallas kernels, run_expert_grads(): pl.pallas_call(functools.partial(expert_grads_kernel, columns, exchange,...  37 us
    pallas_call x1, Pallas kernels, run_forward(): pl.pallas_call(functools.partial(forward_kernel, heads), grid=(rows,), in...  16 us
    pallas_call x1, Pallas kernels, run_ada(): pl.pallas_call(lambda _, *refs: ada_kernel(orders, rows, *refs), grid_spe...  12.7 us
  transfers between devices with their start and end apart: 16, of which 2 were waited for; matrix products, arithmetic and copies ran while one was open for 8% of the time, Pallas kernels for 9%

profile of v1, /device:TPU:0, one launch (start us, length us, event | category | flops | bytes accessed | tf_op | source)
XLA Modules:
  0.0 596.6 jit_solution(3582327467599749864)
XLA Ops:
  0.7 3.0 collective-permute-start
  3.8 20.6 %collective-permute-done = bf16[768,576]{0,1:T(8,128)(2,1)} collective-permute-done((bf16[768,576]{0,1:T(8,128)(2,1)}, bf16[768,576]{0,1:T(8,128)(2,1)}, u32[]{:S(2)}, u32[]{:S(2)}) %collective-permute-start) | collective-permute-done | bytes 884768 | tf_op jit(solution)/shard_map/ppermute | solution.py:38
  24.5 6.7 %convolution_add_fusion.shift_one.scale_one.gate_one.shift_two.scale_two = f32[512,4608]{1,0:T(8,128)S(1)} fusion(bf16[768,4608]{1,0:T(8,128)(2,1)} %param.22, f32[4608]{0:T(1024)} %param.23, bf16[512,768]{1,0:T(8,128)(2,1)} %param.17), kind=kOutput, calls=%fused_computation.2 | convolution fusion | flops 3628597248 | bytes 17319936 | tf_op jit(solution)/shard_map/dot_general | solution.py:853
  31.2 3.7 copy-done.2
  34.9 1.2 fusion.2
  36.0 2.1 collective-permute-start.9
  38.6 1.3 copy.71.refs_0_.refs_4_
  40.2 2.3 copy.72.refs_1_.refs_5_
  42.7 2.3 copy.73.refs_2_.refs_6_
  44.9 2.2 copy.74.refs_3_.refs_7_
  47.2 16.0 %attention_half.1 = (bf16[512,768]{1,0:T(8,128)(2,1)S(1)}, bf16[512,576]{1,0:T(8,128)(2,1)S(1)}, bf16[512,576]{1,0:T(8,128)(2,1)S(1)}, bf16[512,576]{1,0:T(8,128...) custom-call(bf16[512,768]{1,0:T(8,128)(2,1)} %base.5, ...), custom_call_target="tpu_custom_call" | custom-call | flops 176160768 | bytes 983040 | tf_op jit(solution)/shard_map/attention_half/pallas_call | solution.py:334
  63.2 0.9 copy-done.16
  64.1 0.9 copy-done.17
  65.0 0.8 copy-done.19
  65.8 0.9 copy-done.20
  66.7 0.8 copy-done.21
  69.4 18.9 %collective-permute-done.6 = bf16[512,768]{1,0:T(8,128)(2,1)S(1)} collective-permute-done((bf16[512,768]{1,0:T(8,128)(2,1)}, bf16[512,768]{1,0:T(8,128)(2,1)S(1)}, u32[]{:S(2)}, u32[]{:S(2)}) %collective-permute-start.6) | collective-permute-done | bytes 786464 | tf_op jit(solution)/shard_map/ppermute | solution.py:38
  88.2 1.3 copy.79.refs_0_
  89.6 3.2 pad_maximum_fusion.1.refs_2_
  92.7 0.9 constant_dynamic-update-slice_fusion.3
  93.7 1.0 constant_dynamic-update-slice_fusion.2
  94.6 2.1 constant_dynamic-update-slice_fusion.1
  96.7 2.1 constant_dynamic-update-slice_fusion.refs_1_
  98.8 21.4 %experts_1.1 = (bf16[4,192,768]{2,1,0:T(8,128)(2,1)}, bf16[4,192,768]{2,1,0:T(8,128)(2,1)}, f32[2048,768]{1,0:T(8,128)}, f32[2048,768]{1,0:T(8,128)}) custom-call(f32[2048,16]{1,0:T(8,128)} %copy.79.refs_0_, bf16[2048,768]{1,0:T(8,128)(2,1)} %constant_dynamic-update-slice_fusion.refs_1_, bf16[2048,768]{1,0:T(8,128)(2,1)} %pad_maximum_fusion.1.refs_2_, ...), custom_call_target="tpu_custom_call" | custom-call | flops 905969664 | bytes 2260992 | tf_op jit(solution)/shard_map/experts_1/pallas_call | solution.py:726
  120.2 51.5 %experts_2.4 = (bf16[4,192,768]{2,1,0:T(8,128)(2,1)}, bf16[4,192,768]{2,1,0:T(8,128)(2,1)}, bf16[4,192,768]{2,1,0:T(8,128)(2,1)}, bf16[4,192,768]{2,1,0:T(8,128)...) custom-call(f32[2048,16]{1,0:T(8,128)} %copy.79.refs_0_, ...), custom_call_target="tpu_custom_call", output_to_operand_aliasing={{4}: (7, {}), {5}: (8, {})} | custom-call | flops 1811939328 | bytes 2555904 | tf_op jit(solution)/shard_map/experts_2/pallas_call | solution.py:726
  171.8 58.4 %experts_2.5 = (bf16[4,192,768]{2,1,0:T(8,128)(2,1)}, bf16[4,192,768]{2,1,0:T(8,128)(2,1)}, bf16[4,192,768]{2,1,0:T(8,128)(2,1)}, bf16[4,192,768]{2,1,0:T(8,128)...) custom-call(f32[2048,16]{1,0:T(8,128)} %copy.79.refs_0_, ...), custom_call_target="tpu_custom_call", output_to_operand_aliasing={{4}: (7, {}), {5}: (8, {})} | custom-call | flops 1811939328 | bytes 2555904 | tf_op jit(solution)/shard_map/experts_2/pallas_call | solution.py:726
  230.2 63.4 %experts_2.6 = (bf16[4,192,768]{2,1,0:T(8,128)(2,1)}, bf16[4,192,768]{2,1,0:T(8,128)(2,1)}, bf16[4,192,768]{2,1,0:T(8,128)(2,1)}, bf16[4,192,768]{2,1,0:T(8,128)...) custom-call(f32[2048,16]{1,0:T(8,128)} %copy.79.refs_0_, ...), custom_call_target="tpu_custom_call", output_to_operand_aliasing={{4}: (7, {}), {5}: (8, {})} | custom-call | flops 1811939328 | bytes 2555904 | tf_op jit(solution)/shard_map/experts_2/pallas_call | solution.py:726
  293.6 34.0 %experts_2.7 = (bf16[2048,768]{1,0:T(8,128)(2,1)}, bf16[2048,768]{1,0:T(8,128)(2,1)}, bf16[2048,768]{1,0:T(8,128)(2,1)}, bf16[2048,768]{1,0:T(8,128)(2,1)}, bf16...) custom-call(f32[2048,16]{1,0:T(8,128)} %copy.79.refs_0_, ...), custom_call_target="tpu_custom_call" | custom-call | flops 1207959552 | bytes 2555904 | tf_op jit(solution)/shard_map/experts_2/pallas_call | solution.py:726
  327.7 5.3 fusion.19
  334.0 1.7 slice_dynamic-update-slice_fusion.7
  335.7 1.7 bitcast_dynamic-update-slice_fusion.7
  337.4 0.7 slice_dynamic-update-slice_fusion.6
  338.9 0.8 slice_bitcast_fusion
  339.8 1.9 fusion.1
  341.7 1.0 slice.197
  343.6 0.8 copy-done.26
  344.4 1.2 fusion.21
  345.6 1.5 collective-permute-start.15
  347.1 37.0 %expert_grads.1 = (bf16[4,192,768]{2,1,0:T(8,128)(2,1)}, bf16[4,192,768]{2,1,0:T(8,128)(2,1)}, bf16[4,192,768]{2,1,0:T(8,128)(2,1)}, bf16[4,192,768]{2,1,0:T(8,1...) custom-call(f32[2048,16]{1,0:T(8,128)} %copy.79.refs_0_, ...), custom_call_target="tpu_custom_call" | custom-call | flops 603979776 | bytes 1179648 | tf_op jit(solution)/shard_map/expert_grads/pallas_call | solution.py:798
  384.2 1.8 slice_dynamic-update-slice_fusion.5
  386.0 1.7 bitcast_dynamic-update-slice_fusion.5
  387.7 1.7 slice_dynamic-update-slice_fusion.4
  389.4 1.7 bitcast_dynamic-update-slice_fusion.4
  391.2 4.3 fusion.3
  395.4 3.7 copy-done.3
  399.1 2.0 middle_back.1
  401.1 1.4 copy-done.9
  402.5 1.1 copy-done.11
  403.6 0.9 copy-done.18
  404.5 62.0 %attention_back.1 = (f32[512,768]{1,0:T(8,128)}, bf16[512,1536]{1,0:T(8,128)(2,1)}, bf16[16,96,768]{2,1,0:T(8,128)(2,1)}, bf16[16,96,768]{2,1,0:T(8,128)(2,1)}, ...) custom-call(bf16[512,768]{1,0:T(8,128)(2,1)} %base.5, ...), custom_call_target="tpu_custom_call" | custom-call | flops 364904448 | bytes 1474560 | tf_op jit(solution)/shard_map/attention_back/pallas_call | solution.py:513
  466.5 2.6 convert_reduce_fusion
  469.2 10.2 %fusion.7 = (bf16[512,768]{1,0:T(8,128)(2,1)}, f32[512,768]{1,0:T(8,128)}) fusion(bf16[512,768]{1,0:T(8,128)(2,1)S(1)} %copy-done.46, bf16[512,4608]{1,0:T(8,128)(2,1)S(1)} %get-tuple-element.228.refs_1_.refs_2_.refs_3_.refs_4_, bf16[768,4608]{1,0:T(8,128)(2,1)} %param.22), kind=kOutput, calls=%fused_computation.20 | convolution fusion | flops 3628597248 | bytes 14942208 | tf_op jit(solution)/shard_map/dot_general | solution.py:22
  480.9 12.7 %ada_grads.1 = (bf16[16,112,576]{2,1,0:T(8,128)(2,1)}, bf16[16,112,576]{2,1,0:T(8,128)(2,1)}, bf16[16,96,576]{2,1,0:T(8,128)(2,1)}, bf16[16,96,576]{2,1,0:T(8,128)(2,1)}) custom-call(s32[4]{0:T(128)} %iota_xor_fusion._, bf16[512,768]{1,0:T(8,128)(2,1)} %get-tuple-element.237.refs_0_, bf16[512,4608]{1,0:T(8,128)(2,1)} %copy-done.25, ...), custom_call_target="tpu_custom_call" | custom-call | flops 226492416 | bytes 1105920 | tf_op jit(solution)/shard_map/ada_grads/pallas_call | solution.py:588
  493.5 88.8 %drain.1 = (f32[1,96,768]{2,1,0:T(8,128)}, f32[1,112,576]{2,1,0:T(8,128)}, f32[1,96,576]{2,1,0:T(8,128)}, f32[1,192,768]{2,1,0:T(8,128)}, f32[1,192,768]{2,1,0:T(8,128)}) custom-call(bf16[16,96,768]{2,1,0:T(8,128)(2,1)} %get-tuple-element.161.refs_0_, bf16[16,96,768]{2,1,0:T(8,128)(2,1)} %get-tuple-element.162.refs_1_, ...), custom_call_target="tpu_custom_call" | custom-call | tf_op jit(solution)/shard_map/drain/pallas_call | solution.py:223
  582.4 1.1 slice.201
  583.5 1.0 slice_bitcast_fusion.3
  584.5 1.0 slice_bitcast_fusion.2
  585.4 1.3 slice.200
  586.8 0.9 copy.87
  587.7 0.7 copy.88
  588.5 0.7 slice_dynamic-update-slice_fusion.3
  589.9 0.7 slice_dynamic-update-slice_fusion.2
  594.4 0.9 pad_maximum_fusion.2
  595.2 1.1 copy.113
  (134 shorter events, 11.8 us)
Async XLA Ops:
  0.6 39.3 %copy-start = (s32[8,256]{1,0:T(8,128)S(1)}, s32[8,256]{1,0:T(8,128)}, u32[]{:S(2)}) copy-start(s32[8,256]{1,0:T(8,128)} %param.19) | copy-start | bytes 24580
  0.7 34.2 %copy-start.5 = (bf16[512,768]{1,0:T(8,128)(2,1)S(1)}, bf16[512,768]{1,0:T(8,128)(2,1)}, u32[]{:S(2)}) copy-start(bf16[512,768]{1,0:T(8,128)(2,1)} %cotangent.1) | copy-start | bytes 2359300
  0.7 23.8 %collective-permute-start = (bf16[768,576]{0,1:T(8,128)(2,1)}, bf16[768,576]{0,1:T(8,128)(2,1)}, u32[]{:S(2)}, u32[]{:S(2)}) collective-permute-start(bf16[768,576]{0,1:T(8,128)(2,1)} %bitcast.88), channel_id=1, source_target_pairs={{0,2},{1,3},{2,0},{3,1},{4,6},{5,7},{6,4},{7,5},{8,10},{9,11},{10,... | collective-permute-start | bytes 2654216 | tf_op jit(solution)/shard_map/ppermute | solution.py:38
  3.7 38.8 %collective-permute-start.1 = (bf16[768,576]{0,1:T(8,128)(2,1)}, bf16[768,576]{0,1:T(8,128)(2,1)}, u32[]{:S(2)}, u32[]{:S(2)}) collective-permute-start(bf16[768,576]{0,1:T(8,128)(2,1)} %bitcast.89), channel_id=1, source_target_pairs={{0,1},{1,0},{2,3},{3,2},{4,5},{5,4},{6,7},{7,6},{8,9},{9,8},{10,11... | collective-permute-start | bytes 2654216 | tf_op jit(solution)/shard_map/ppermute | solution.py:38
  3.7 34.6 %collective-permute-start.3 = (bf16[192,768]{1,0:T(8,128)(2,1)}, bf16[192,768]{1,0:T(8,128)(2,1)S(1)}, u32[]{:S(2)}, u32[]{:S(2)}) collective-permute-start(bf16[192,768]{1,0:T(8,128)(2,1)} %refs_8_.1), channel_id=1, source_target_pairs={{0,2},{1,3},{2,0},{3,1},{4,6},{5,7},{6,4},{7,5},{8,10},{9,11},{10,... | collective-permute-start | bytes 884744 | tf_op jit(solution)/shard_map/ppermute | solution.py:38
  24.5 20.5 %collective-permute-start.2 = (bf16[768,576]{0,1:T(8,128)(2,1)}, bf16[768,576]{0,1:T(8,128)(2,1)}, u32[]{:S(2)}, u32[]{:S(2)}) collective-permute-start(bf16[768,576]{0,1:T(8,128)(2,1)} %collective-permute-done), channel_id=1, source_target_pairs={{0,1},{1,0},{2,3},{3,2},{4,5},{5,4},{6,7},{7,6},{8,9},{9,8},{10,11... | collective-permute-start | bytes 2654216 | tf_op jit(solution)/shard_map/ppermute | solution.py:38
  31.2 3.7 copy-start.2
  34.9 3.2 copy-start.12
  34.9 3.7 copy-start.33
  36.0 32.6 %collective-permute-start.9 = (bf16[512,768]{1,0:T(8,128)(2,1)}, bf16[512,768]{1,0:T(8,128)(2,1)}, u32[]{:S(2)}, u32[]{:S(2)}) collective-permute-start(bf16[512,768]{1,0:T(8,128)(2,1)} %fusion.2), channel_id=1, source_target_pairs={{0,2},{1,3},{2,0},{3,1},{4,6},{5,7},{6,4},{7,5},{8,10},{9,11},{10,... | collective-permute-start | bytes 2359304 | tf_op jit(solution)/shard_map/ppermute | solution.py:38
  38.1 9.1 %collective-permute-start.4 = (bf16[192,768]{1,0:T(8,128)(2,1)S(1)}, bf16[192,768]{1,0:T(8,128)(2,1)S(1)}, u32[]{:S(2)}, u32[]{:S(2)}) collective-permute-start(bf16[192,768]{1,0:T(8,128)(2,1)S(1)} %copy-done.12), channel_id=1, source_target_pairs={{0,1},{1,0},{2,3},{3,2},{4,5},{5,4},{6,7},{7,6},{8,9},{9,8},{10,11... | collective-permute-start | bytes 884744 | tf_op jit(solution)/shard_map/ppermute | solution.py:38
  38.3 8.9 %copy-start.13 = (bf16[192,768]{1,0:T(8,128)(2,1)}, bf16[192,768]{1,0:T(8,128)(2,1)S(1)}, u32[]{:S(2)}) copy-start(bf16[192,768]{1,0:T(8,128)(2,1)S(1)} %collective-permute-done.3.refs_5_.refs_9_) | copy-start | bytes 884740
  38.3 8.9 %collective-permute-start.5 = (bf16[192,768]{1,0:T(8,128)(2,1)S(1)}, bf16[192,768]{1,0:T(8,128)(2,1)S(1)}, u32[]{:S(2)}, u32[]{:S(2)}) collective-permute-start(bf16[192,768]{1,0:T(8,128)(2,1)S(1)} %collective-permute-done.3.refs_5_.refs_9_), channel_id=1, source_target_pairs={{0,1},{1,0},{2,3},{3,2},{4,5},{5,4},{6,7},{7,6},{8,9},{9,8},{10,11... | collective-permute-start | bytes 884744 | tf_op jit(solution)/shard_map/ppermute | solution.py:38
  40.1 7.1 %copy-start.10 = (s32[2,256,1]{2,1,0:T(8,128)}, s32[2,256,1]{2,1,0:T(8,128)S(1)}, u32[]{:S(2)}) copy-start(s32[2,256,1]{2,1,0:T(8,128)S(1)} %copy.70.seg_col) | copy-start | bytes 6148
  40.2 7.1 %copy-start.24 = (s32[2,1,256]{2,1,0:T(1,128)}, s32[2,1,256]{2,1,0:T(1,128)S(1)}, u32[]{:S(2)}) copy-start(s32[2,1,256]{2,1,0:T(1,128)S(1)} %broadcast_in_dim.52.seg_row) | copy-start | bytes 6148
  42.5 47.1 %collective-permute-start.10 = (bf16[512,768]{1,0:T(8,128)(2,1)}, bf16[512,768]{1,0:T(8,128)(2,1)}, u32[]{:S(2)}, u32[]{:S(2)}) collective-permute-start(bf16[512,768]{1,0:T(8,128)(2,1)} %fusion.2), channel_id=1, source_target_pairs={{0,1},{1,0},{2,3},{3,2},{4,5},{5,4},{6,7},{7,6},{8,9},{9,8},{10,11... | collective-permute-start | bytes 2359304 | tf_op jit(solution)/shard_map/ppermute | solution.py:38
  47.2 21.4 %copy-start.42 = (f32[2048,2]{0,1:T(2,128)S(1)}, f32[2048,2]{0,1:T(2,128)}, u32[]{:S(2)}) copy-start(f32[2048,2]{0,1:T(2,128)} %param.21) | copy-start | bytes 49156
  47.2 21.4 %copy-start.43 = (s32[2048,2]{0,1:T(2,128)S(1)}, s32[2048,2]{0,1:T(2,128)}, u32[]{:S(2)}) copy-start(s32[2048,2]{0,1:T(2,128)} %param.20) | copy-start | bytes 49156
  47.2 16.0 %copy-start.14 = (bf16[192,768]{1,0:T(8,128)(2,1)}, bf16[192,768]{1,0:T(8,128)(2,1)S(1)}, u32[]{:S(2)}) copy-start(bf16[192,768]{1,0:T(8,128)(2,1)S(1)} %collective-permute-done.4.refs_6_.refs_10_) | copy-start | bytes 884740
  47.2 16.0 %copy-start.15 = (bf16[192,768]{1,0:T(8,128)(2,1)}, bf16[192,768]{1,0:T(8,128)(2,1)S(1)}, u32[]{:S(2)}) copy-start(bf16[192,768]{1,0:T(8,128)(2,1)S(1)} %collective-permute-done.5.refs_7_.refs_11_) | copy-start | bytes 884740
  63.2 0.9 copy-start.16
  64.1 0.9 copy-start.17
  65.0 0.8 copy-start.19
  65.8 0.9 copy-start.20
  66.7 0.8 copy-start.21
  67.6 0.7 copy-start.23
  68.3 24.5 %copy-start.22 = (bf16[512,576]{1,0:T(8,128)(2,1)}, bf16[512,576]{1,0:T(8,128)(2,1)S(1)}, u32[]{:S(2)}) copy-start(bf16[512,576]{1,0:T(8,128)(2,1)S(1)} %get-tuple-element.150.refs_3_) | copy-start | bytes 1769476
  68.3 19.9 %collective-permute-start.6 = (bf16[512,768]{1,0:T(8,128)(2,1)}, bf16[512,768]{1,0:T(8,128)(2,1)S(1)}, u32[]{:S(2)}, u32[]{:S(2)}) collective-permute-start(bf16[512,768]{1,0:T(8,128)(2,1)} %get-tuple-element.98), channel_id=1, source_target_pairs={{0,2},{1,3},{2,0},{3,1},{4,6},{5,7},{6,4},{7,5},{8,10},{9,11},{10,... | collective-permute-start | bytes 2359304 | tf_op jit(solution)/shard_map/ppermute | solution.py:38
  68.6 21.0 %collective-permute-start.11 = (bf16[512,768]{1,0:T(8,128)(2,1)}, bf16[512,768]{1,0:T(8,128)(2,1)S(1)}, u32[]{:S(2)}, u32[]{:S(2)}) collective-permute-start(bf16[512,768]{1,0:T(8,128)(2,1)} %collective-permute-done.9), channel_id=1, source_target_pairs={{0,1},{1,0},{2,3},{3,2},{4,5},{5,4},{6,7},{7,6},{8,9},{9,8},{10,11... | collective-permute-start | bytes 2359304 | tf_op jit(solution)/shard_map/ppermute | solution.py:38
  68.8 25.8 %collective-permute-start.7 = (bf16[512,768]{1,0:T(8,128)(2,1)}, bf16[512,768]{1,0:T(8,128)(2,1)}, u32[]{:S(2)}, u32[]{:S(2)}) collective-permute-start(bf16[512,768]{1,0:T(8,128)(2,1)} %get-tuple-element.98), channel_id=1, source_target_pairs={{0,1},{1,0},{2,3},{3,2},{4,5},{5,4},{6,7},{7,6},{8,9},{9,8},{10,11... | collective-permute-start | bytes 2359304 | tf_op jit(solution)/shard_map/ppermute | solution.py:38
  88.2 8.5 %collective-permute-start.8 = (bf16[512,768]{1,0:T(8,128)(2,1)S(1)}, bf16[512,768]{1,0:T(8,128)(2,1)}, u32[]{:S(2)}, u32[]{:S(2)}) collective-permute-start(bf16[512,768]{1,0:T(8,128)(2,1)S(1)} %collective-permute-done.6), channel_id=1, source_target_pairs={{0,1},{1,0},{2,3},{3,2},{4,5},{5,4},{6,7},{7,6},{8,9},{9,8},{10,11... | collective-permute-start | bytes 2359304 | tf_op jit(solution)/shard_map/ppermute | solution.py:38
  89.6 3.2 copy-start.34
  327.6 5.3 copy-start.44
  327.6 5.3 copy-start.45
  327.7 9.8 %copy-start.38 = (f32[1,192,768]{2,1,0:T(8,128)S(1)}, f32[1,192,768]{2,1,0:T(8,128)}, u32[]{:S(2)}) copy-start(f32[1,192,768]{2,1,0:T(8,128)} %get-tuple-element.176) | copy-start | bytes 1769476
  332.9 6.0 %copy-start.37 = (f32[1,192,768]{2,1,0:T(8,128)S(1)}, f32[1,192,768]{2,1,0:T(8,128)}, u32[]{:S(2)}) copy-start(f32[1,192,768]{2,1,0:T(8,128)} %get-tuple-element.174) | copy-start | bytes 1769476
  332.9 6.8 %collective-permute-start.12 = (bf16[2,512,768]{2,1,0:T(8,128)(2,1)}, bf16[2,512,768]{2,1,0:T(8,128)(2,1)}, u32[]{:S(2)}, u32[]{:S(2)}) collective-permute-start(bf16[2,512,768]{2,1,0:T(8,128)(2,1)} %bitcast.5), channel_id=1, source_target_pairs={{0,1},{1,0},{2,3},{3,2},{4,5},{5,4},{6,7},{7,6},{8,9},{9,8},{10,11... | collective-permute-start | bytes 4718600 | tf_op jit(solution)/shard_map/ppermute | solution.py:38
  332.9 6.8 %copy-start.30 = (bf16[1024,768]{1,0:T(8,128)(2,1)S(1)}, bf16[1024,768]{1,0:T(8,128)(2,1)}, u32[]{:S(2)}) copy-start(bf16[1024,768]{1,0:T(8,128)(2,1)} %get-tuple-element.245) | copy-start | bytes 4718596
  333.0 10.2 %collective-permute-start.14 = (bf16[2,512,768]{2,1,0:T(8,128)(2,1)S(1)}, bf16[2,512,768]{2,1,0:T(8,128)(2,1)S(1)}, u32[]{:S(2)}, u32[]{:S(2)}) collective-permute-start(bf16[2,512,768]{2,1,0:T(8,128)(2,1)S(1)} %bitcast.84), channel_id=1, source_target_pairs={{0,1},{1,0},{2,3},{3,2},{4,5},{5,4},{6,7},{7,6},{8,9},{9,8},{10,11... | collective-permute-start | bytes 4718600 | tf_op jit(solution)/shard_map/ppermute | solution.py:38
  339.8 3.5 copy-start.29
  341.7 1.9 copy-start.27
  342.7 48.5 %collective-permute-start.13 = (bf16[1,512,768]{2,1,0:T(8,128)(2,1)}, bf16[1,512,768]{2,1,0:T(8,128)(2,1)}, u32[]{:S(2)}, u32[]{:S(2)}) collective-permute-start(bf16[1,512,768]{2,1,0:T(8,128)(2,1)} %slice.197), channel_id=1, source_target_pairs={{0,2},{1,3},{2,0},{3,1},{4,6},{5,7},{6,4},{7,5},{8,10},{9,11},{10,... | collective-permute-start | bytes 2359304 | tf_op jit(solution)/shard_map/ppermute | solution.py:38
  343.2 1.2 copy-start.26
  345.6 49.8 %collective-permute-start.15 = (bf16[1,512,768]{2,1,0:T(8,128)(2,1)}, bf16[1,512,768]{2,1,0:T(8,128)(2,1)S(1)}, u32[]{:S(2)}, u32[]{:S(2)}) collective-permute-start(bf16[1,512,768]{2,1,0:T(8,128)(2,1)} %get-tuple-element.235), channel_id=1, source_target_pairs={{0,2},{1,3},{2,0},{3,1},{4,6},{5,7},{6,4},{7,5},{8,10},{9,11},{10,... | collective-permute-start | bytes 2359304 | tf_op jit(solution)/shard_map/ppermute | solution.py:38
  347.1 44.0 %copy-start.28 = (bf16[2,512,768]{2,1,0:T(8,128)(2,1)S(1)}, bf16[2,512,768]{2,1,0:T(8,128)(2,1)}, u32[]{:S(2)}) copy-start(bf16[2,512,768]{2,1,0:T(8,128)(2,1)} %copy-done.27) | copy-start | bytes 4718596
  384.2 7.0 %copy-start.4 = (bf16[512,768]{1,0:T(8,128)(2,1)S(1)}, bf16[512,768]{1,0:T(8,128)(2,1)}, u32[]{:S(2)}) copy-start(bf16[512,768]{1,0:T(8,128)(2,1)} %base.5) | copy-start | bytes 2359300
  384.2 7.0 %copy-start.6 = (f32[512,768]{1,0:T(8,128)S(1)}, f32[512,768]{1,0:T(8,128)}, u32[]{:S(2)}) copy-start(f32[512,768]{1,0:T(8,128)} %get-tuple-element.97.attn) | copy-start | bytes 4718596
  391.1 4.3 copy-start.7
  391.1 4.3 copy-start.8
  395.4 3.7 copy-start.3
  401.1 1.4 copy-start.9
  402.5 1.1 copy-start.11
  403.6 0.9 copy-start.18
  404.5 62.0 %copy-start.31 = (bf16[512,768]{1,0:T(8,128)(2,1)S(1)}, bf16[512,768]{1,0:T(8,128)(2,1)}, u32[]{:S(2)}) copy-start(bf16[512,768]{1,0:T(8,128)(2,1)} %get-tuple-element.233) | copy-start | bytes 2359300
  466.5 2.6 copy-start.46
  469.1 10.3 %copy-start.25 = (bf16[512,4608]{1,0:T(8,128)(2,1)}, bf16[512,4608]{1,0:T(8,128)(2,1)S(1)}, u32[]{:S(2)}) copy-start(bf16[512,4608]{1,0:T(8,128)(2,1)S(1)} %get-tuple-element.228.refs_1_.refs_2_.refs_3_.refs_4_) | copy-start | bytes 14155780
  582.4 6.1 %copy-start.36 = (f32[1,192,768]{2,1,0:T(8,128)S(1)}, f32[1,192,768]{2,1,0:T(8,128)}, u32[]{:S(2)}) copy-start(f32[1,192,768]{2,1,0:T(8,128)} %get-tuple-element.179) | copy-start | bytes 1769476
  582.4 7.6 %copy-start.35 = (f32[1,192,768]{2,1,0:T(8,128)S(1)}, f32[1,192,768]{2,1,0:T(8,128)}, u32[]{:S(2)}) copy-start(f32[1,192,768]{2,1,0:T(8,128)} %get-tuple-element.180) | copy-start | bytes 1769476
  582.4 9.0 %copy-start.40 = (f32[1,192,768]{2,1,0:T(8,128)S(1)}, f32[1,192,768]{2,1,0:T(8,128)}, u32[]{:S(2)}) copy-start(f32[1,192,768]{2,1,0:T(8,128)} %get-tuple-element.181) | copy-start | bytes 1769476
  586.7 6.2 %copy-start.39 = (f32[1,192,768]{2,1,0:T(8,128)S(1)}, f32[1,192,768]{2,1,0:T(8,128)}, u32[]{:S(2)}) copy-start(f32[1,192,768]{2,1,0:T(8,128)} %get-tuple-element.182) | copy-start | bytes 1769476
  588.5 5.9 copy-start.41
  589.9 5.3 copy-start.32
  592.9 3.5 copy-start.1

commit v2 on v1

v2 whole, which is shorter than its diff:
```python
import functools

import jax
import jax.numpy as jnp
from jax import lax
from jax.experimental import pallas as pl
from jax.experimental.pallas import tpu as pltpu
from jax.sharding import PartitionSpec as P

HEAD_DIM = 64
BF16 = jnp.bfloat16
F32 = jnp.float32
GELU_A = 0.7978845608028654
GELU_B = 0.044715


def nn(a, b):
    return lax.dot_general(a, b, (((1,), (0,)), ((), ())), preferred_element_type=F32)


def nt(a, b):
    return lax.dot_general(a, b, (((1,), (1,)), ((), ())), preferred_element_type=F32)


def tn(a, b):
    return lax.dot_general(a, b, (((0,), (0,)), ((), ())), preferred_element_type=F32)


def cost(flops, bytes_accessed, transcendentals):
    share = 16
    return pl.CostEstimate(
        flops=flops // share, bytes_accessed=bytes_accessed // share, transcendentals=transcendentals // share
    )


def swap(value, axis, mask):
    size = lax.axis_size(axis)
    return lax.ppermute(value, axis, [(i, i ^ mask) for i in range(size)])


def halves_evenly(n_dp, rows):
    return n_dp == 8 and rows % 16 == 0


def dp_steps(n_dp):
    return [("dp", 1 << bit) for bit in range(n_dp.bit_length() - 1)]


def block_order(steps):
    order = [(0, 0)]
    for axis, mask in reversed(steps):
        order = order + [(d ^ mask, m) if axis == "dp" else (d, m ^ mask) for d, m in order]
    return order


def flip(index, mask):
    bit = 1
    while bit <= mask:
        if mask & bit:
            index = index + bit * (1 - 2 * ((index // bit) % 2))
        bit *= 2
    return index


class Chain:
    def __init__(self, keep, send, steps, done=0):
        self.keep, self.send, self.steps, self.step = keep, send, steps, done
        self.shape = None if keep is None else keep.shape

    @classmethod
    def inside(cls, shape, steps):
        chain = cls(None, None, steps)
        chain.shape = shape
        return chain

    def take(self, results):
        if self.step == len(self.steps):
            self.result = results.pop(0)[0]
        else:
            self.keep, self.send = results.pop(0), results.pop(0)
            self.shape = self.keep.shape

    def advance(self):
        got = swap(self.send, *self.steps[self.step])
        total = self.keep.astype(F32) + got.astype(F32)
        half = total.shape[0] // 2
        self.step += 1
        self.take([total[:half].astype(BF16), total[half:].astype(BF16)] if half else [total])

    def finish(self):
        while self.step < len(self.steps):
            self.advance()
        return self.result


class Exchange:
    def __init__(self, jobs, sunk=False):
        self.jobs, self.sunk, self.sinks = jobs, sunk, {}
        self.operands, self.in_specs, self.out_specs, self.shapes, self.scratch = [], [], [], [], []
        self.plans = []
        for chain, count in jobs:
            blocks, tail = chain.shape[0], chain.shape[1:]
            steps = chain.steps[chain.step : chain.step + count]
            final = chain.step + count == len(chain.steps)
            self.plans.append((steps, final, blocks, chain.keep is None))
            if chain.keep is None:
                self.scratch.append(pltpu.VMEM(chain.shape, BF16))
            else:
                self.operands += [chain.keep, chain.send]
                self.in_specs += [pl.BlockSpec(memory_space=pl.ANY)] * 2
            left = blocks >> (count if not final else count - 1)
            kept = jax.ShapeDtypeStruct((left,) + tail, F32 if final else BF16)
            outs = [] if final and sunk else [kept] if final else [kept, kept]
            self.shapes += outs
            self.out_specs += [pl.BlockSpec(kept.shape, lambda *_: (0, 0, 0))] * len(outs)
            self.scratch.append(pltpu.VMEM((blocks,) + tail, BF16))
            self.scratch += [pltpu.VMEM((blocks >> n,) + tail, BF16) for n in range(count)]
            self.scratch += [
                pltpu.SemaphoreType.DMA((1,)),
                pltpu.SemaphoreType.DMA((count,)),
                pltpu.SemaphoreType.DMA((count,)),
            ]

    def bind(self, ins, outs, scratch):
        self.ins, self.outs, self.buffers, self.at = [], [], [], [0] * len(self.jobs)
        for steps, final, _, inner in self.plans:
            number = 0 if final and self.sunk else 1 if final else 2
            self.outs.append(outs[:number])
            outs = outs[number:]
            if inner:
                self.ins.append([None, scratch[0]])
                scratch = scratch[1:]
            else:
                self.ins.append(ins[:2])
                ins = ins[2:]
            number = len(steps) + 4
            self.buffers.append(scratch[:number])
            scratch = scratch[number:]

    @staticmethod
    def partner(axis, mask):
        return {axis: flip(lax.axis_index(axis), mask)}

    def load(self, n):
        return pltpu.make_async_copy(self.ins[n][0], self.buffers[n][0], self.buffers[n][-3].at[0])

    def copy(self, n, step):
        steps, _, blocks, _ = self.plans[n]
        work, send_sems, recv_sems = self.buffers[n][0], self.buffers[n][-2], self.buffers[n][-1]
        number = blocks >> step
        source = self.ins[n][1] if step == 0 else work.at[pl.ds(number, number)]
        return pltpu.make_async_remote_copy(
            src_ref=source,
            dst_ref=self.buffers[n][1 + step],
            send_sem=send_sems.at[step],
            recv_sem=recv_sems.at[step],
            device_id=self.partner(*steps[step]),
            device_id_type=pl.DeviceIdType.MESH,
        )

    def begin(self, others=()):
        partners = sorted({step for steps, *_ in self.plans for step in steps} | set(others))
        if partners:
            barrier = pltpu.get_barrier_semaphore()
            for step in partners:
                pl.semaphore_signal(
                    barrier, inc=1, device_id=self.partner(*step), device_id_type=pl.DeviceIdType.MESH
                )
            pl.semaphore_wait(barrier, len(partners))
        for n, (*_, inner) in enumerate(self.plans):
            if not inner:
                self.copy(n, 0).start()
                self.load(n).start()

    def halves(self, n):
        return self.buffers[n][0], self.ins[n][1]

    def start(self, n):
        self.copy(n, 0).start()

    def advance(self, n):
        steps, final, blocks, inner = self.plans[n]
        step = self.at[n]
        self.at[n] += 1
        work, got = self.buffers[n][0], self.buffers[n][1 + step]
        number = blocks >> step
        if step == 0 and not inner:
            self.load(n).wait()
        self.copy(n, step).wait()
        half = number // 2
        ending = step == len(steps) - 1

        def add(first, count, target, shift):
            def one(i, carry):
                total = work[i].astype(F32) + got[i].astype(F32)
                target[i - shift] = total.astype(target.dtype)
                return carry

            lax.fori_loop(first, first + count, one, 0)

        if ending and final and self.sunk:
            self.sinks[n](work[0].astype(F32) + got[0].astype(F32))
        elif ending and final:
            add(0, number, self.outs[n][0], 0)
        elif ending:
            add(0, half, self.outs[n][0], 0)
            add(half, half, self.outs[n][1], half)
        else:
            add(half, half, work, 0)
            self.copy(n, step + 1).start()
            add(0, half, work, 0)

    def left(self, n):
        return len(self.plans[n][0]) - self.at[n]

    def all_once(self):
        for n in range(len(self.jobs)):
            self.advance(n)

    def early(self, first=0, last=None):
        for n, (steps, *_) in list(enumerate(self.plans))[first:last]:
            while self.at[n] < len(steps) - 1:
                self.advance(n)

    def finish(self):
        for step in range(max([len(steps) for steps, *_ in self.plans], default=0)):
            for n, (steps, *_) in enumerate(self.plans):
                if self.at[n] == step and step < len(steps):
                    self.advance(n)

    def spread(self, results):
        results = list(results)
        for chain, count in self.jobs:
            chain.step += count
            if not (self.sunk and chain.step == len(chain.steps)):
                chain.take(results)


def remote(exchange, number, vmem, always=False):
    if not (exchange.jobs or always):
        return pltpu.CompilerParams(vmem_limit_bytes=vmem << 20)
    return pltpu.CompilerParams(vmem_limit_bytes=vmem << 20, collective_id=number, has_side_effects=True)


MP_STEPS = [("mp", 1), ("mp", 2)]
MP_ORDER = [m for _, m in block_order(MP_STEPS)]


def gather_mp(own):
    far = swap(own, "mp", 2)
    return [own, far, swap(own, "mp", 1), swap(far, "mp", 1)]


def normalize(values):
    center = values - jnp.mean(values, axis=-1, keepdims=True)
    inverse = lax.rsqrt(jnp.mean(center * center, axis=-1, keepdims=True) + 1e-06)
    return center * inverse, inverse


def normalize_back(normal, inverse, grad):
    return inverse * (
        grad
        - jnp.mean(grad, axis=-1, keepdims=True)
        - normal * jnp.mean(grad * normal, axis=-1, keepdims=True)
    )


def forward_kernel(
    heads, base, shift_one, scale_one, gate_one, shift_two, scale_two, seg_col, seg_row, *refs
):
    weights, out_weights = refs[:4], refs[4:8]
    normed_out, qkv, attended, lse_out, attn_out, second_out = refs[8], refs[9:13], *refs[13:]
    span = heads * HEAD_DIM
    x = base[...].astype(F32)
    normed = (normalize(x)[0] * (1.0 + scale_one[...]) + shift_one[...]).astype(BF16)
    normed_out[...] = normed
    same = seg_col[0] == seg_row[0]
    lane = lax.broadcasted_iota(jnp.int32, (1, 128), 1)
    lse_all = jnp.zeros(lse_out.shape, F32)
    attn = jnp.zeros(x.shape, F32)
    for block in range(4):
        qkv[block][...] = nn(normed, weights[block][...]).astype(BF16)
        for head in range(heads):
            at = head * HEAD_DIM
            q = qkv[block][:, at : at + HEAD_DIM]
            k = qkv[block][:, span + at : span + at + HEAD_DIM]
            v = qkv[block][:, 2 * span + at : 2 * span + at + HEAD_DIM]
            scores = jnp.where(same, nt(q, k) * (HEAD_DIM**-0.5), -1000000000.0)
            top = jnp.max(scores, axis=-1, keepdims=True)
            expo = jnp.exp(scores - top)
            total = jnp.sum(expo, axis=-1, keepdims=True)
            light = (expo * (1.0 / total)).astype(BF16)
            start = block * span + at
            attended[:, start : start + HEAD_DIM] = nn(light, v).astype(BF16)
            lse_all = jnp.where(lane == block * heads + head, top + jnp.log(total), lse_all)
        attn += nn(attended[:, block * span : (block + 1) * span], out_weights[block][...])
    lse_out[...] = lse_all
    attn_out[...] = attn
    middle = x + gate_one[...] * attn
    second_out[...] = (normalize(middle)[0] * (1.0 + scale_two[...]) + shift_two[...]).astype(BF16)


def rows_of(owner, rows):
    return pl.multiple_of(flip(lax.axis_index("dp"), owner) * rows, 8)


def store_blocks(order, m, total, halves, rows, columns=slice(None)):
    half = len(order) // 2
    for place, owner in enumerate(order):
        if owner[1] == m:
            start = 0 if rows == total.shape[0] else rows_of(owner[0], rows)
            halves[place // half][place % half, :rows, :] = total[pl.ds(start, rows), columns].astype(BF16)


def row_block(seq, columns):
    return pl.BlockSpec((seq, columns), lambda i, *_: (i, 0))


def column_block(seq, width, number):
    return pl.BlockSpec((seq, width), lambda i, *_: (i, number))


def whole_block(array):
    return pl.BlockSpec(array.shape, lambda i, *_: (0,) * array.ndim, pipeline_mode=pl.Buffered(1))


def segment_blocks(seq):
    return [
        pl.BlockSpec((1, seq, 1), lambda i, *_: (i, 0, 0)),
        pl.BlockSpec((1, 1, seq), lambda i, *_: (i, 0, 0)),
    ]


def run_forward(patches, modulation, segments, qkv_parts, out_parts):
    rows, seq = segments.shape
    tokens, width = patches.shape
    columns = qkv_parts[0].shape[1]
    heads = columns // (3 * HEAD_DIM)
    work = rows * 4 * heads * seq * seq
    shapes = (
        [(width, BF16)] + [(columns, BF16)] * 4 + [(width, BF16), (128, F32), (width, F32), (width, BF16)]
    )
    return pl.pallas_call(
        functools.partial(forward_kernel, heads),
        grid=(rows,),
        in_specs=[row_block(seq, width)]
        + [column_block(seq, width, n) for n in range(5)]
        + segment_blocks(seq)
        + [whole_block(w) for w in qkv_parts + out_parts],
        out_specs=[row_block(seq, c) for c, _ in shapes],
        out_shape=[jax.ShapeDtypeStruct((tokens, c), t) for c, t in shapes],
        compiler_params=pltpu.CompilerParams(vmem_limit_bytes=48 << 20),
        cost_estimate=cost(
            flops=4 * work * HEAD_DIM + 8 * tokens * width * width,
            bytes_accessed=40 * tokens * width,
            transcendentals=work,
        ),
        name="attention_half",
    )(
        patches,
        *([modulation] * 5),
        segments[:, :, None],
        segments[:, None, :],
        *qkv_parts,
        *out_parts,
    )


def attention_back_kernel(
    heads,
    exchange,
    order,
    rows,
    base,
    scale_one,
    gate_one,
    scale_two,
    attn,
    cotangent,
    summed,
    normed,
    attended,
    lse,
    seg_col,
    seg_row,
    *refs,
):
    qkv, weights, out_weights = refs[:4], refs[4:8], refs[8:12]
    number = len(exchange.operands)
    moved, refs = refs[12 : 12 + number], refs[12 + number :]
    patches_grad, pieces, halves, refs = refs[0], refs[1], refs[2:4], refs[4:]
    number = len(exchange.shapes)
    moved_out, refs = refs[:number], refs[number:]
    totals, grad_qkv, refs = refs[:4], refs[4], refs[5:]
    step, last = pl.program_id(0), pl.num_programs(0) - 1
    exchange.bind(moved, moved_out, refs)

    @pl.when(step == 0)
    def _():
        exchange.begin()

    span = heads * HEAD_DIM
    width = base.shape[1]
    factor = HEAD_DIM**-0.5
    same = seg_col[0] == seg_row[0]
    grad, branch, gate = summed[...], attn[...], gate_one[...]
    normal, inverse = normalize(base[...].astype(F32) + gate * branch)
    middle_grad = cotangent[...].astype(F32) + normalize_back(
        normal, inverse, grad * (1.0 + scale_two[...])
    )
    patches_grad[...] = middle_grad
    pieces[:, 2 * width : 3 * width] = (middle_grad * branch).astype(BF16)
    pieces[:, 3 * width : 4 * width] = grad.astype(BF16)
    pieces[:, 4 * width :] = (grad * normal).astype(BF16)
    upper = (middle_grad * gate).astype(BF16)
    normed_grad = jnp.zeros(base.shape, F32)
    for block in range(4):
        if block == 0:

            @pl.when(step == last)
            def _():
                exchange.early(0, 1)

        if block == 2:

            @pl.when(step == last)
            def _():
                exchange.early(1)

        grad_heads = nt(upper, out_weights[block][...]).astype(BF16)
        for head in range(heads):
            at = head * HEAD_DIM
            n = block * heads + head
            q = qkv[block][:, at : at + HEAD_DIM]
            k = qkv[block][:, span + at : span + at + HEAD_DIM]
            v = qkv[block][:, 2 * span + at : 2 * span + at + HEAD_DIM]
            g = grad_heads[:, at : at + HEAD_DIM]
            scores = jnp.where(same, nt(q, k) * factor, -1000000000.0)
            probs = jnp.exp(scores - lse[:, n : n + 1])
            grad_probs = nt(g, v)
            term = jnp.sum(probs * grad_probs, axis=-1, keepdims=True)
            grad_scores = (probs * (grad_probs - term)).astype(BF16)
            grad_qkv[:, at : at + HEAD_DIM] = (nn(grad_scores, k) * factor).astype(BF16)
            grad_qkv[:, span + at : span + at + HEAD_DIM] = (tn(grad_scores, q) * factor).astype(BF16)
            grad_qkv[:, 2 * span + at : 2 * span + at + HEAD_DIM] = tn(
                probs.astype(BF16), g
            ).astype(BF16)
        made = grad_qkv[...]
        normed_grad += nt(made, weights[block][...])
        of_qkv = tn(normed[...], made)
        of_out = tn(upper, attended[:, block * span : (block + 1) * span])

        @pl.when(step == 0)
        def _():
            totals[block][:, : 3 * span] = of_qkv
            totals[block][:, 3 * span :] = of_out

        @pl.when(step > 0)
        def _():
            totals[block][:, : 3 * span] += of_qkv
            totals[block][:, 3 * span :] += of_out

        @pl.when(step == last)
        def _():
            store_blocks(order, MP_ORDER[block], totals[block], halves, rows)

    normal, inverse = normalize(base[...].astype(F32))
    patches_grad[...] += normalize_back(normal, inverse, normed_grad * (1.0 + scale_one[...]))
    pieces[:, :width] = normed_grad.astype(BF16)
    pieces[:, width : 2 * width] = (normed_grad * normal).astype(BF16)

    @pl.when(step == last)
    def _():
        exchange.finish()


def run_attention_back(
    patches,
    modulation,
    attn,
    cotangent,
    summed,
    normed,
    attended,
    lse,
    segments,
    qkv,
    qkv_parts,
    out_parts,
    order,
    rows,
    jobs,
    number,
):
    count, seq = segments.shape
    tokens, width = patches.shape
    columns = qkv[0].shape[1]
    heads = columns // (3 * HEAD_DIM)
    work = count * 4 * heads * seq * seq
    wide = row_block(seq, width)
    half = (len(order) // 2, rows, 4 * columns // 3)
    exchange = Exchange(jobs)
    results = pl.pallas_call(
        functools.partial(attention_back_kernel, heads, exchange, order, rows),
        grid_spec=pltpu.PrefetchScalarGridSpec(
            num_scalar_prefetch=0,
            grid=(count,),
            in_specs=[wide]
            + [column_block(seq, width, n) for n in (1, 2, 4)]
            + [wide] * 5
            + [row_block(seq, 128)]
            + segment_blocks(seq)
            + [row_block(seq, columns)] * 4
            + [whole_block(w) for w in qkv_parts + out_parts]
            + exchange.in_specs,
            out_specs=[wide, row_block(seq, 5 * width)]
            + [pl.BlockSpec(half, lambda i, *_: (0, 0, 0))] * 2
            + exchange.out_specs,
            scratch_shapes=[pltpu.VMEM((width, 4 * columns // 3), F32)] * 4
            + [pltpu.VMEM((seq, columns), BF16)]
            + exchange.scratch,
        ),
        out_shape=[
            jax.ShapeDtypeStruct((tokens, width), F32),
            jax.ShapeDtypeStruct((tokens, 5 * width), BF16),
        ]
        + [jax.ShapeDtypeStruct(half, BF16)] * 2
        + exchange.shapes,
        compiler_params=remote(exchange, number, 62),
        cost_estimate=cost(
            flops=10 * work * HEAD_DIM + 16 * tokens * width * width,
            bytes_accessed=60 * tokens * width,
            transcendentals=work,
        ),
        name="attention_back",
    )(
        patches,
        *([modulation] * 3),
        attn,
        cotangent,
        summed,
        normed,
        attended,
        lse,
        segments[:, :, None],
        segments[:, None, :],
        *qkv,
        *qkv_parts,
        *out_parts,
        *exchange.operands,
    )
    exchange.spread(results[4:])
    return results[:4]


BIAS_ROWS = 16


def tail_kernel(
    orders,
    rows,
    exchange,
    cond,
    silu_cond,
    base,
    attn,
    gate_one,
    gate_two,
    cotangent,
    mlp,
    pieces,
    weight,
    *refs,
):
    number = len(exchange.operands)
    moved, refs = refs[:number], refs[number:]
    cond_grad, output, qkv_grad, out_grad, ada_grad, bias_grad, refs = *refs[:6], refs[6:]
    number = len(exchange.jobs) - 3
    late, refs = refs[:number], refs[number:]
    modulation_grad, weight_here, total, load_sems, refs = *refs[:4], refs[4:]
    exchange.bind(moved, (), refs)
    tokens, width = base.shape
    pieces_load = pltpu.make_async_copy(
        pieces, modulation_grad.at[:, pl.ds(0, pieces.shape[1])], load_sems.at[0]
    )
    weight_load = pltpu.make_async_copy(weight, weight_here, load_sems.at[1])
    pieces_load.start()
    weight_load.start()
    exchange.begin()
    grad_out, branch = cotangent[...].astype(F32), mlp[...]
    modulation_grad[:, 5 * width :] = (grad_out * branch).astype(BF16)
    middle = base[...].astype(F32) + gate_one[...] * attn[...]
    output[...] = (middle + gate_two[...] * branch).astype(BF16)
    pieces_load.wait()

    columns = modulation_grad.shape[1] // 4
    split = columns // 2
    heads = qkv_grad.shape[1]
    mp = lax.axis_index("mp")

    def keep_heads(value):
        qkv_grad[...] = value[:, :heads]
        out_grad[...] = value[:, heads:]

    def keep_low(value):
        ada_grad[:, :split] = value[:rows]
        bias_grad[...] = value[rows:]

    def keep_high(value):
        ada_grad[:, split:] = value

    def keep_late(target, value):
        target[...] = value

    exchange.sinks = {0: keep_low, 1: keep_high, 2: keep_heads}
    for n, target in enumerate(late):
        exchange.sinks[3 + n] = functools.partial(keep_late, target)
    bias = jnp.sum(modulation_grad[...].astype(F32), axis=0, keepdims=True).astype(BF16)
    lines = [bias[:, n * split : (n + 1) * split] for n in range(8)]
    lines = jnp.concatenate(lines + [jnp.zeros_like(lines[0])] * (BIAS_ROWS - 8), axis=0)
    for place in range(len(orders[0])):
        half = len(orders[0]) // 2
        exchange.halves(0)[place // half][place % half, rows:, :] = lines
    half = MP_ORDER[len(MP_ORDER) // 2 :]
    for m in half + [m for m in MP_ORDER if m not in half]:
        first = pl.multiple_of(flip(mp, m) * columns, 128)
        total[...] = tn(silu_cond[...], modulation_grad[:, pl.ds(first, columns)])
        for part, order in enumerate(orders):
            own = slice(part * split, (part + 1) * split)
            store_blocks(order, m, total, exchange.halves(part), rows, own)
        if m == half[0]:
            exchange.advance(2)
        if m == half[-1]:
            exchange.start(0)
            exchange.start(1)
    exchange.advance(0)
    exchange.advance(1)
    weight_load.wait()
    value = cond[...].astype(F32)
    gate = 1.0 / (1.0 + jnp.exp(-value))
    cond_grad[...] = nt(modulation_grad[...], weight_here[...]) * (gate * (1.0 + value * (1.0 - gate)))
    for n in (2, 0, 1, 2):
        exchange.advance(n) if exchange.left(n) > 1 else None
    for n in range(len(late)):
        exchange.advance(3 + n)
    for n in (0, 2, 1):
        exchange.advance(n) if exchange.left(n) > 1 else None
    exchange.finish()


def run_tail(
    conditioning, silu_cond, patches, attn, modulation, cotangent, mlp, pieces, ada_weight, orders, rows, jobs, number
):
    tokens, width = silu_cond.shape
    exchange = Exchange(jobs, True)
    anywhere = pl.BlockSpec(memory_space=pl.ANY)
    columns = ada_weight.shape[1] // 4
    heads = jobs[2][0].shape[2]
    whole = lambda columns: pl.BlockSpec((tokens, columns), lambda i: (0, 0), pipeline_mode=pl.Buffered(1))
    gate = lambda n: pl.BlockSpec((tokens, width), lambda i: (0, n), pipeline_mode=pl.Buffered(1))
    shapes = [
        jax.ShapeDtypeStruct((tokens, width), F32),
        jax.ShapeDtypeStruct((tokens, width), BF16),
        jax.ShapeDtypeStruct((rows, heads * 3 // 4), F32),
        jax.ShapeDtypeStruct((rows, heads // 4), F32),
        jax.ShapeDtypeStruct((rows, columns), F32),
        jax.ShapeDtypeStruct((BIAS_ROWS, columns // 2), F32),
    ]
    shapes += [jax.ShapeDtypeStruct(chain.shape[1:], F32) for chain, _ in jobs[3:]]
    return pl.pallas_call(
        functools.partial(tail_kernel, orders, rows, exchange),
        grid=(1,),
        in_specs=[whole(width)] * 4
        + [gate(2), gate(5)]
        + [whole(width)] * 2
        + [anywhere] * 2
        + exchange.in_specs,
        out_specs=[constant_block(shape) for shape in shapes],
        out_shape=shapes,
        scratch_shapes=[
            pltpu.VMEM((tokens, ada_weight.shape[1]), BF16),
            pltpu.VMEM(ada_weight.shape, BF16),
            pltpu.VMEM((width, columns), F32),
            pltpu.SemaphoreType.DMA((2,)),
        ]
        + exchange.scratch,
        compiler_params=remote(exchange, number, 63),
        cost_estimate=cost(
            flops=16 * tokens * width * ada_weight.shape[1], bytes_accessed=100 * width * width, transcendentals=0
        ),
        name="tail",
    )(
        conditioning,
        silu_cond,
        patches,
        attn,
        modulation,
        modulation,
        cotangent,
        mlp,
        pieces,
        ada_weight,
        *exchange.operands,
    )


def finish_kernel(moves, rows, *refs):
    parts, refs = refs[: len(moves)], refs[len(moves) :]
    half = (len(refs) - 4) // 2
    plain, outs, experts = refs[:half], refs[half : 2 * half], refs[2 * half :]
    for source, target in zip(plain, outs):
        target[...] = source[...]
    for part, (expert, first, last) in zip(parts, moves):
        for kind in range(2):
            value = part[0, kind * rows : (kind + 1) * rows, :]
            if expert is None:
                experts[2 + kind][:, first:last] = value
            else:
                experts[kind][expert, :, first:last] = value


def run_finish(moves, plain, experts, rows, width):
    def block(array, index):
        return pl.BlockSpec((1,) + array.shape[1:], lambda i: (index, 0, 0), pipeline_mode=pl.Buffered(1))

    shapes = [jax.ShapeDtypeStruct(a.shape, a.dtype) for a in plain]
    shapes += [jax.ShapeDtypeStruct((experts, rows, width), F32)] * 2
    shapes += [jax.ShapeDtypeStruct((rows, width), F32)] * 2
    return pl.pallas_call(
        functools.partial(finish_kernel, [move[2:] for move in moves], rows),
        grid=(1,),
        in_specs=[block(array, index) for array, index, *_ in moves] + [whole_block(a) for a in plain],
        out_specs=[constant_block(shape) for shape in shapes],
        out_shape=shapes,
        compiler_params=pltpu.CompilerParams(vmem_limit_bytes=60 << 20),
        name="finish",
    )(*[move[0] for move in moves], *plain)


def gelu_and_slope(values):
    square = values * values
    bent = jnp.tanh(values * (GELU_A + (GELU_A * GELU_B) * square))
    half = 0.5 * (1.0 + bent)
    active = values * half
    return active, half + active * (1.0 - bent) * (GELU_A + (3.0 * GELU_A * GELU_B) * square)


class Gather:
    def __init__(self, own, far, held, send_sems, recv_sems):
        self.own, self.far, self.held, self.send_sems, self.recv_sems = own, far, held, send_sems, recv_sems

    def copy(self, place):
        far = self.held.at[1] if self.far is None else self.far
        return pltpu.make_async_remote_copy(
            src_ref=far if place == 2 else self.own,
            dst_ref=self.held.at[place],
            send_sem=self.send_sems.at[place],
            recv_sem=self.recv_sems.at[place],
            device_id=Exchange.partner("mp", 2 if place == 1 else 1),
            device_id_type=pl.DeviceIdType.MESH,
        )

    def begin(self):
        self.held[3] = self.own[...]
        if self.far is None:
            self.copy(1).start()
            self.copy(0).start()
        else:
            self.held[1] = self.far[...]
            self.copy(0).start()
            self.copy(2).start()

    def tile(self, step):
        @pl.when(step == 1)
        def _():
            self.copy(0).wait()

        if self.far is None:

            @pl.when(step == 2)
            def _():
                self.copy(1).wait()
                self.copy(2).start()

        @pl.when(step == 3)
        def _():
            self.copy(2).wait()

        return self.held[(step + 3) % 4]


def gather_barrier():
    barrier = pltpu.get_barrier_semaphore()
    for mask in (1, 2):
        pl.semaphore_signal(
            barrier, inc=1, device_id=Exchange.partner("mp", mask), device_id_type=pl.DeviceIdType.MESH
        )
    pl.semaphore_wait(barrier, 2)


def expert_kernel(columns, gathers, first, last, grad_later, exchange, units, rows, *refs):
    count = len(columns)
    gates, tokens, grads, refs = *refs[:3], refs[3:]
    if gathers:
        grads_far, refs = refs[0], refs[1:]
    ups, downs, refs = refs[:count], refs[count : 2 * count], refs[2 * count :]
    if not first:
        old_out, old_back, refs = refs[0], refs[1], refs[2:]
    number = len(exchange.operands)
    moved, refs = refs[:number], refs[number:]
    number = 2 * count if grad_later else sum(2 * len(own) for own in units)
    halves, refs = refs[:number], refs[number:]
    number = 4 if last else 2
    made, refs = refs[:number], refs[number:]
    number = len(exchange.shapes)
    moved_out, refs = refs[:number], refs[number:]
    if gathers:
        gathered, refs = refs[:2], refs[2:]
    number = 0 if grad_later else 2 * count
    sums, refs = refs[:number], refs[number:]
    step, final = pl.program_id(0), pl.num_programs(0) - 1
    if gathers:
        gather = [Gather(tokens, None, *refs[:3]), Gather(grads, grads_far, *refs[3:6])]
        refs = refs[6:]
    exchange.bind(moved, moved_out, refs)

    @pl.when(step == 0)
    def _():
        exchange.begin()

    @pl.when(step == 2)
    def _():
        exchange.early()

    if not grad_later:
        start_sums(step, sums)
    if gathers:

        @pl.when(step == 0)
        def _():
            gather_barrier()
            for one in gather:
                one.begin()

        x, own_grads = [one.tile(step) for one in gather]
        gathered[0][...] = x
        gathered[1][...] = own_grads
    else:
        x, own_grads = tokens[...], grads[...]
    g32 = own_grads.astype(F32)
    routed = None if first else old_out[...]
    returned = None if first else old_back[...]
    for n, column in enumerate(columns):
        gate = gates[:, column : column + 1]
        slot_grad = (gate * g32).astype(BF16)
        hidden, grad_pre, one, two = expert_pass(x, slot_grad, gate, ups[n][0], downs[n][0])
        routed = one if routed is None else routed + one
        returned = two if returned is None else returned + two
        if grad_later:
            halves[2 * n][...] = hidden
            halves[2 * n + 1][...] = grad_pre
        else:
            sums[2 * n][...] += tn(x, grad_pre)
            sums[2 * n + 1][...] += tn(slot_grad, hidden)
    if last:
        for value, (kept, sent) in ((routed, made[:2]), (returned, made[2:])):

            @pl.when(step < 2)
            def _():
                kept[0] = value.astype(BF16)

            @pl.when(step >= 2)
            def _():
                sent[0] = value.astype(BF16)

    else:
        made[0][...] = routed
        made[1][...] = returned
    if not grad_later:
        store_halves(step, units, sums, halves, rows)

    @pl.when(step == final)
    def _():
        exchange.finish()


def start_sums(step, sums):
    @pl.when(step == 0)
    def _():
        for total in sums:
            total[...] = jnp.zeros_like(total)


def store_units(units, sums, targets, rows):
    for (columns, order), halves in zip(units, targets):
        half = len(order) // 2
        for place, owner in enumerate(order):
            start = place * rows if half == 1 else rows_of(owner, rows)
            for part, total in enumerate(sums):
                halves[place // half][place % half, part * rows : (part + 1) * rows, :] = total[
                    pl.ds(start, rows), columns
                ].astype(BF16)


def store_halves(step, units, sums, halves, rows):
    @pl.when(step == pl.num_programs(0) - 1)
    def _():
        start = 0
        for n, own in enumerate(units):
            pairs = [halves[start + 2 * u : start + 2 * u + 2] for u in range(len(own))]
            start += 2 * len(own)
            store_units(own, sums[2 * n : 2 * n + 2], pairs, rows)


def unit_shapes(units, rows, width):
    shapes = []
    for columns, order in units:
        number = len(range(*columns.indices(width)))
        shapes += [jax.ShapeDtypeStruct((len(order) // 2, 2 * rows, number), BF16)] * 2
    return shapes


def constant_block(shape):
    return pl.BlockSpec(shape.shape, lambda *_: (0,) * len(shape.shape))


def expert_pass(x, slot_grad, gate, up, down):
    pre = nn(x, up)
    grad_hidden = nt(slot_grad, down)
    hidden, slope = gelu_and_slope(pre)
    hidden = hidden.astype(BF16)
    grad_pre = (grad_hidden * slope).astype(BF16)
    return hidden, grad_pre, gate * nn(hidden, down), nt(grad_pre, up)


TILE = 512


def token_tiles(columns):
    return pl.BlockSpec((TILE, columns), lambda t: (t, 0))


def run_experts(
    columns, weights, units, rows, gates, tokens, grads, sums, last, grad_later, jobs, number, gathers=False
):
    count = len(columns)
    total, width = gates.shape[0], tokens.shape[1]
    hidden = weights[0][0].shape[2]
    steps = total // TILE
    first = sums is None
    exchange = Exchange(jobs)

    def weight(index, shape):
        return pl.BlockSpec((1,) + shape, lambda t: (index, 0, 0), pipeline_mode=pl.Buffered(1))

    def tiles(columns):
        return pl.BlockSpec((TILE, columns), lambda t: ((t % 2) * 2 + t // 2 if gathers else t, 0))

    in_specs = (
        [tiles(gates.shape[1])]
        + ([pl.BlockSpec((TILE, width), lambda t: (0, 0))] * 3 if gathers else [tiles(width)] * 2)
        + [weight(i, (width, hidden)) for _, _, i in weights]
        + [weight(i, (hidden, width)) for _, _, i in weights]
        + ([] if first else [token_tiles(width), token_tiles(width)])
    )
    given = len(in_specs)
    if grad_later:
        shapes = [jax.ShapeDtypeStruct((total, hidden), BF16)] * (2 * count)
        specs = [token_tiles(hidden)] * (2 * count)
    else:
        shapes = [shape for own in units for shape in unit_shapes(own, rows, hidden)]
        specs = [constant_block(shape) for shape in shapes]
    made = len(shapes)
    if last:
        block = (1, TILE, width)
        sum_specs = [
            pl.BlockSpec(block, lambda t: (jnp.minimum(t, 1), 0, 0)),
            pl.BlockSpec(block, lambda t: (jnp.maximum(t - 2, 0), 0, 0)),
        ] * 2
        sum_shapes = [jax.ShapeDtypeStruct((2, TILE, width), BF16)] * 4
    else:
        sum_specs = [tiles(width)] * 2
        sum_shapes = [jax.ShapeDtypeStruct((total, width), F32)] * 2
    gather_scratch, gather_shapes = [], []
    if gathers:
        gather_scratch = ([pltpu.VMEM((4, TILE, width), BF16)] + [pltpu.SemaphoreType.DMA((3,))] * 2) * 2
        gather_shapes = [jax.ShapeDtypeStruct((total, width), BF16)] * 2
    aliases = {} if first or last else {given - 2: made, given - 1: made + 1}
    results = pl.pallas_call(
        functools.partial(expert_kernel, columns, gathers, first, last, grad_later, exchange, units, rows),
        grid_spec=pltpu.PrefetchScalarGridSpec(
            num_scalar_prefetch=0,
            grid=(steps,),
            in_specs=in_specs + exchange.in_specs,
            out_specs=specs + sum_specs + exchange.out_specs + [tiles(width)] * (2 * gathers),
            scratch_shapes=([] if grad_later else [pltpu.VMEM((width, hidden), F32)] * (2 * count))
            + gather_scratch
            + exchange.scratch,
        ),
        out_shape=shapes + sum_shapes + exchange.shapes + gather_shapes,
        input_output_aliases=aliases,
        compiler_params=remote(exchange, number, 60, gathers),
        cost_estimate=cost(
            flops=(8 if grad_later else 12) * count * total * width * hidden,
            bytes_accessed=20 * total * width + 8 * count * width * hidden,
            transcendentals=count * total * hidden,
        ),
        name=f"experts_{count}",
    )(
        gates,
        tokens,
        *(grads if gathers else [grads]),
        *[up for up, _, _ in weights],
        *[down for _, down, _ in weights],
        *(() if first else sums),
        *exchange.operands,
    )
    number = made + len(sum_shapes)
    if gathers:
        return results[:made], results[made:number], results[number:]
    exchange.spread(results[number:])
    return results[:made], results[made:number]


SLOTS = 3


def long_kernel(count, exchange, units, unit_steps, rows, gates, tokens, grads, up, down, *refs):
    old = refs[:2]
    number = len(exchange.operands)
    moved, refs = refs[2 : 2 + number], refs[2 + number :]
    new, finals, last_final, refs = refs[:2], refs[2], refs[3], refs[4:]
    number = 2 * len(units)
    half_done, raw, refs = refs[:number], refs[number : 2 * number], refs[2 * number :]
    number = len(exchange.shapes)
    moved_out, refs = refs[:number], refs[number:]
    sums, totals, send, work, gots = refs[:2], refs[2:4], refs[4], refs[5], refs[6:9]
    send_sems, recv_sems, load_sems, store_sems, refs = *refs[9:13], refs[13:]
    exchange.bind(moved, moved_out, refs)
    e, t = pl.program_id(0), pl.program_id(1)
    tiles = 4

    def copy(chain, step, unit):
        slot = chain % SLOTS
        blocks = 4 >> step
        columns = units[unit][0]
        place = pl.ds(columns.start, columns.stop - columns.start)
        source = send if step == 0 else work
        first = 0 if step == 0 else blocks
        return pltpu.make_async_remote_copy(
            src_ref=source.at[slot, pl.ds(first, blocks), :, place],
            dst_ref=gots[step].at[slot, :, :, place],
            send_sem=send_sems.at[slot, step, unit],
            recv_sem=recv_sems.at[slot, step, unit],
            device_id=exchange.partner(*unit_steps[unit][step]),
            device_id_type=pl.DeviceIdType.MESH,
        )

    def launch(chain, step):
        for unit in range(len(units)):
            copy(chain, step, unit).start()

    def arrive(chain, step):
        for unit in range(len(units)):
            copy(chain, step, unit).wait()

    def add(chain, step):
        slot = chain % SLOTS

        def one(i, carry):
            total = work[slot, i].astype(F32) + gots[step][slot, i].astype(F32)
            work[slot, i] = total.astype(BF16)
            return carry

        lax.fori_loop(0, 4 >> step, one, 0)

    def close(chain, target):
        arrive(chain, 2)
        slot = chain % SLOTS
        target[0] = work[slot, 0].astype(F32) + gots[2][slot, 0].astype(F32)

    def loads(n, tile):
        return pltpu.make_async_copy(
            old[n].at[pl.ds(tile * TILE, TILE), :], totals[n].at[tile], load_sems.at[n, tile]
        )

    def stores(n, tile):
        return pltpu.make_async_copy(
            totals[n].at[tile], new[n].at[pl.ds(tile * TILE, TILE), :], store_sems.at[n, tile]
        )

    @pl.when((e == 0) & (t == 0))
    def _():
        for tile in range(tiles):
            for n in range(2):
                loads(n, tile).start()
        exchange.begin(sorted({step for steps in unit_steps for step in steps}))

    for tile in range(tiles):

        @pl.when((e == 0) & (t == tile))
        def _():
            for n in range(2):
                loads(n, tile).wait()

    @pl.when((e == 1) & (t == 0))
    def _():
        exchange.all_once()

    @pl.when((e == 1) & (t == 2))
    def _():
        exchange.all_once()

    @pl.when((e == 2) & (t == 0))
    def _():
        exchange.finish()

    @pl.when((e >= 2) & (t == 0))
    def _():
        arrive(e - 2, 0)
        add(e - 2, 0)
        launch(e - 2, 1)

    @pl.when((e >= 1) & (t == 0))
    def _():
        launch(e - 1, 0)

    @pl.when((e >= 3) & (t == 2))
    def _():
        close(e - 3, finals)

    @pl.when((e >= 2) & (t == 2))
    def _():
        arrive(e - 2, 1)
        add(e - 2, 1)
        launch(e - 2, 2)

    @pl.when(t == 0)
    def _():
        for total in sums:
            total[...] = jnp.zeros_like(total)

    lane = lax.broadcasted_iota(jnp.int32, (1, gates.shape[1]), 1)
    gate = jnp.sum(jnp.where(lane == e, gates[...], 0.0), axis=1, keepdims=True)
    x = tokens[...]
    slot_grad = (gate * grads[...].astype(F32)).astype(BF16)
    hidden, grad_pre, one, two = expert_pass(x, slot_grad, gate, up[0], down[0])
    totals[0][t] += one
    totals[1][t] += two
    sums[0][...] += tn(x, grad_pre)
    sums[1][...] += tn(slot_grad, hidden)

    for tile in range(tiles):

        @pl.when((e == count - 1) & (t == tile))
        def _():
            for n in range(2):
                stores(n, tile).start()

    @pl.when((t == tiles - 1) & (e < count - 1))
    def _():
        slot = e % SLOTS
        pairs = [
            (work.at[slot, :, :, pl.ds(c.start, c.stop - c.start)], send.at[slot, :, :, pl.ds(c.start, c.stop - c.start)])
            for c, _ in units
        ]
        store_units(units, sums, pairs, rows)

    @pl.when((t == tiles - 1) & (e == count - 1))
    def _():
        store_units(units, sums, [raw[2 * u : 2 * u + 2] for u in range(len(units))], rows)
        close(count - 3, last_final)
        arrive(count - 2, 0)
        add(count - 2, 0)
        slot = (count - 2) % SLOTS
        for u, (c, _) in enumerate(units):
            half_done[2 * u][...] = work[slot, 0:2, :, c]
            half_done[2 * u + 1][...] = work[slot, 2:4, :, c]
        for tile in range(tiles):
            for n in range(2):
                stores(n, tile).wait()


def run_long(count, units, unit_steps, rows, gates, tokens, grads, expert_up, expert_down, sums, jobs, number):
    total, width = tokens.shape
    hidden = expert_up.shape[2]
    exchange = Exchange(jobs)
    steps = total // TILE
    tile = lambda columns: pl.BlockSpec((TILE, columns), lambda e, t: (t, 0))
    weight = lambda shape: pl.BlockSpec((1,) + shape, lambda e, t: (e, 0, 0))
    anywhere = pl.BlockSpec(memory_space=pl.ANY)
    raw = unit_shapes(units, rows, hidden)
    half_done = [jax.ShapeDtypeStruct((s.shape[0] // 2,) + s.shape[1:], BF16) for s in raw]
    final = (1, 2 * rows, hidden)
    results = pl.pallas_call(
        functools.partial(long_kernel, count, exchange, units, unit_steps, rows),
        grid=(count, steps),
        in_specs=[
            tile(gates.shape[1]),
            tile(width),
            tile(width),
            weight((width, hidden)),
            weight((hidden, width)),
            anywhere,
            anywhere,
        ]
        + exchange.in_specs,
        out_specs=[anywhere, anywhere]
        + [pl.BlockSpec(final, lambda e, t: (jnp.maximum(e - 3, 0), 0, 0)), pl.BlockSpec(final, lambda e, t: (0, 0, 0))]
        + [constant_block(shape) for shape in half_done + raw]
        + exchange.out_specs,
        out_shape=[jax.ShapeDtypeStruct((total, width), F32)] * 2
        + [jax.ShapeDtypeStruct((count - 3,) + final[1:], F32), jax.ShapeDtypeStruct(final, F32)]
        + half_done
        + raw
        + exchange.shapes,
        scratch_shapes=[pltpu.VMEM((width, hidden), F32)] * 2
        + [pltpu.VMEM((steps, TILE, width), F32)] * 2
        + [pltpu.VMEM((SLOTS, 4, 2 * rows, hidden), BF16)] * 2
        + [pltpu.VMEM((SLOTS, 4 >> n, 2 * rows, hidden), BF16) for n in range(3)]
        + [pltpu.SemaphoreType.DMA((SLOTS, 3, len(units)))] * 2
        + [pltpu.SemaphoreType.DMA((2, steps))] * 2
        + exchange.scratch,
        compiler_params=remote(exchange, number, 62),
        cost_estimate=cost(
            flops=12 * count * total * width * hidden,
            bytes_accessed=8 * count * total * width,
            transcendentals=count * total * hidden,
        ),
        name="experts_long",
    )(gates, tokens, grads, expert_up, expert_down, *sums, *exchange.operands)
    made = len(raw)
    exchange.spread(results[4 + 2 * made :])
    finished = [(results[2], n) for n in range(count - 3)] + [(results[3], 0)]
    return results[:2], finished, results[4 : 4 + made], results[4 + made : 4 + 2 * made]


def expert_grads_kernel(columns, exchange, units, rows, *refs):
    count = len(columns)
    gates, tokens, grads = refs[:3]
    saved, refs = refs[3 : 3 + 2 * count], refs[3 + 2 * count :]
    number = len(exchange.operands)
    moved, refs = refs[:number], refs[number:]
    number = sum(2 * len(own) for own in units)
    halves, refs = refs[:number], refs[number:]
    number = len(exchange.shapes)
    moved_out, refs = refs[:number], refs[number:]
    sums, refs = refs[: 2 * count], refs[2 * count :]
    step, final = pl.program_id(0), pl.num_programs(0) - 1
    exchange.bind(moved, moved_out, refs)

    @pl.when(step == 0)
    def _():
        exchange.begin()

    @pl.when(step == 1)
    def _():
        exchange.early(0, 1)

    @pl.when(step == 2)
    def _():
        exchange.early(1)

    start_sums(step, sums)
    x = tokens[...]
    g32 = grads[...].astype(F32)
    for n, column in enumerate(columns):
        slot_grad = (gates[:, column : column + 1] * g32).astype(BF16)
        sums[2 * n][...] += tn(x, saved[2 * n + 1][...])
        sums[2 * n + 1][...] += tn(slot_grad, saved[2 * n][...])
    store_halves(step, units, sums, halves, rows)

    @pl.when(step == final)
    def _():
        exchange.finish()


def run_expert_grads(columns, saved, units, rows, gates, tokens, grads, jobs, number):
    count = len(columns)
    total, width = tokens.shape
    hidden = saved[0].shape[1]
    steps = total // TILE
    shapes = [shape for own in units for shape in unit_shapes(own, rows, hidden)]
    exchange = Exchange(jobs)
    results = pl.pallas_call(
        functools.partial(expert_grads_kernel, columns, exchange, units, rows),
        grid_spec=pltpu.PrefetchScalarGridSpec(
            num_scalar_prefetch=0,
            grid=(steps,),
            in_specs=[token_tiles(gates.shape[1]), token_tiles(width), token_tiles(width)]
            + [token_tiles(hidden)] * (2 * count)
            + exchange.in_specs,
            out_specs=[constant_block(shape) for shape in shapes] + exchange.out_specs,
            scratch_shapes=[pltpu.VMEM((width, hidden), F32)] * (2 * count) + exchange.scratch,
        ),
        out_shape=shapes + exchange.shapes,
        compiler_params=remote(exchange, number, 60),
        cost_estimate=cost(
            flops=4 * count * total * width * hidden,
            bytes_accessed=(4 + 4 * count) * total * width,
            transcendentals=0,
        ),
        name="expert_grads",
    )(gates, tokens, grads, *saved, *exchange.operands)
    exchange.spread(results[len(shapes) :])
    return results[: len(shapes)]


def local(
    patches,
    conditioning,
    cotangent,
    segments,
    routes,
    gate_values,
    ada_weight,
    ada_bias,
    qkv_weight,
    out_weight,
    shared_up,
    shared_down,
    expert_up,
    expert_down,
):
    tokens, width = patches.shape
    group = routes.shape[0]
    experts = expert_up.shape[0]
    seq = segments.shape[1]
    n_dp, n_mp = lax.axis_size("dp"), lax.axis_size("mp")
    dp, mp = lax.axis_index("dp"), lax.axis_index("mp")
    rows = width // n_dp

    qkv_parts = gather_mp(qkv_weight.reshape(width, -1))
    out_parts = gather_mp(out_weight)

    silu_cond = jax.nn.silu(conditioning.astype(F32)).astype(BF16)
    modulation = jnp.dot(silu_cond, ada_weight, preferred_element_type=F32) + ada_bias[None, :]
    gate_two = modulation[:, 5 * width :]
    grad_mlp = (cotangent.astype(F32) * gate_two).astype(BF16)
    grad_mlp, *far = lax.optimization_barrier((grad_mlp, qkv_parts[1], out_parts[1]))
    qkv_parts[1], out_parts[1] = far
    grad_far = swap(grad_mlp, "mp", 2)

    own_rows = tokens // seq
    own_segments = lax.dynamic_slice_in_dim(segments, mp * own_rows, own_rows, axis=0)
    results = run_forward(patches, modulation, own_segments, qkv_parts, out_parts)
    normed_one, qkv, attended, lse, attn_out, normed_two = results[0], results[1:5], *results[5:]

    number = jnp.arange(16, dtype=jnp.int32)[None, :]
    gates = jnp.sum(
        jnp.where(routes[:, :, None] == number[:, None, :], gate_values[:, :, None], 0.0), axis=1
    )
    gates = jnp.where(number == experts, 1.0, gates)
    gates = jnp.concatenate(
        [lax.dynamic_slice_in_dim(gates, (mp ^ m) * tokens, tokens, axis=0) for m in MP_ORDER],
        axis=0,
    )
    shared = (shared_up[None], shared_down[None], 0)
    weights = {e: (expert_up, expert_down, e) for e in range(experts)}
    weights[experts] = shared
    even = halves_evenly(n_dp, rows)
    step = rows if even else width // 2
    reduced, chains, wholes = {}, {}, {}
    if even:
        near_step, far_step, *rest = dp_steps(n_dp)
        hidden = expert_up.shape[2]
        cut = hidden * 2 // 3
        unit_steps = [[near_step, far_step] + rest, [far_step, near_step] + rest]
        parts = [(slice(0, cut), unit_steps[0]), (slice(cut, hidden), unit_steps[1])]
        kinds = {c: parts for c in weights}
        kinds[experts - 2] = [(slice(0, hidden), unit_steps[1])]
        kinds[experts - 1] = [(slice(0, hidden), unit_steps[0])]
        units = {
            c: [(columns, [d for d, _ in block_order(steps)]) for columns, steps in kind]
            for c, kind in kinds.items()
        }
    else:
        units = {c: [(slice(0, expert_up.shape[2]), [0, 1])] for c in weights}

    def take_halves(columns, halves, done=0):
        halves = list(halves)
        for column in columns:
            own = [halves.pop(0) for _ in range(2 * len(units[column]))]
            if even:
                chains[column] = [
                    Chain(own[2 * u], own[2 * u + 1], steps, done)
                    for u, (_, steps) in enumerate(kinds[column])
                ]
            else:
                wholes[column] = own

    def jobs(**counts):
        if not even:
            return []
        return [(c, int(count[1:])) for count, columns in counts.items() for x in columns for c in chains[x]]

    def call(columns, sums, last, moves, number):
        return run_experts(
            columns,
            [weights[c] for c in columns],
            [units[c] for c in columns],
            step,
            gates,
            all_tokens,
            all_grads,
            sums,
            last,
            last,
            moves,
            number,
        )

    halves, sums, (all_tokens, all_grads) = run_experts(
        (experts,),
        [weights[experts]],
        [units[experts]],
        step,
        gates,
        normed_two,
        [grad_mlp, grad_far],
        None,
        False,
        False,
        [],
        0,
        True,
    )
    take_halves((experts,), halves)
    late = (experts - 2, experts - 1)
    if even:
        sums, finished, half_done, raw = run_long(
            experts - 2,
            units[0],
            unit_steps,
            rows,
            gates,
            all_tokens,
            all_grads,
            expert_up,
            expert_down,
            sums,
            jobs(n3=(experts,)),
            1,
        )
        take_halves((experts - 4,), half_done, 1)
        take_halves((experts - 3,), raw)
    else:
        for e in range(0, experts - 2, 2):
            halves, sums = call((e, e + 1), sums, False, [], 1 + e // 2)
            take_halves((e, e + 1), halves)
    saved, sums = call(late, sums, True, jobs(n2=(experts - 4,), n1=(experts - 3,)), 4)
    out_chain, back_chain = Chain(*sums[:2], MP_STEPS), Chain(*sums[2:], MP_STEPS)
    halves = run_expert_grads(
        late,
        saved,
        [units[c] for c in late],
        step,
        gates,
        all_tokens,
        all_grads,
        [(back_chain, 2)] + jobs(n2=(experts - 3,)),
        5,
    )
    take_halves(late, halves)
    tail_steps = [MP_STEPS] * 3
    if even:
        y, z, rest = dp_steps(n_dp)[0], dp_steps(n_dp)[1], dp_steps(n_dp)[2:]
        core, x = MP_STEPS
        tail_steps = [[core, x, y, z] + rest, [core, y, x, z] + rest, [core, x, y, z] + rest]
    tail_orders = [block_order(steps) for steps in tail_steps]

    tail_rows = rows if even else width
    results = run_attention_back(
        patches,
        modulation,
        attn_out,
        cotangent,
        back_chain.result,
        normed_one,
        attended,
        lse,
        own_segments,
        qkv,
        qkv_parts,
        out_parts,
        tail_orders[0],
        tail_rows,
        [(out_chain, 2)] + jobs(n2=late),
        6,
    )
    patches_grad, pieces, heads_halves = results[0], results[1], results[2:4]
    heads_chain = Chain(*heads_halves, tail_steps[0])
    split = ada_weight.shape[1] // n_mp // 2
    half = len(tail_orders[1]) // 2
    ada_chains = [
        Chain.inside((half, tail_rows + BIAS_ROWS, split), tail_steps[1]),
        Chain.inside((half, tail_rows, split), tail_steps[2]),
    ]
    number = len(tail_steps[0])
    results = run_tail(
        conditioning,
        silu_cond,
        patches,
        attn_out,
        modulation,
        cotangent,
        out_chain.result,
        pieces,
        ada_weight,
        tail_orders[1:],
        tail_rows,
        [(c, number) for c in ada_chains] + [(heads_chain, number)] + jobs(n1=late),
        7,
    )
    conditioning_grad, output, qkv_sum, out_total, ada_sum, bias_all = results[:6]
    bias_all = bias_all[: 2 * n_mp].reshape(-1)
    if even:
        moves = [(array, index, e, 0, hidden) for e, (array, index) in enumerate(finished)]
        moves += [(array[None], 0, column, 0, hidden) for column, array in zip(late, results[6:])]
        for column, own in chains.items():
            if column not in late:
                for chain, (columns, _) in zip(own, kinds[column]):
                    place = None if column == experts else column
                    moves.append((chain.result[None], 0, place, columns.start, columns.stop))
        results = run_finish(
            moves, [output, patches_grad, conditioning_grad, ada_sum], experts, rows, hidden
        )
        output, patches_grad, conditioning_grad, ada_sum = results[:4]
        expert_up_sum, expert_down_sum, up_sum, down_sum = results[4:]
    else:
        for column, (first, second) in wholes.items():
            whole = jnp.stack([first[0], second[0]]).reshape(2, 2, step, -1)
            whole = jnp.swapaxes(whole, 0, 1).reshape(2, width, -1)
            part = lax.psum_scatter(whole, "dp", scatter_dimension=1, tiled=True).astype(F32)
            reduced[column] = part[0], part[1]
        up_sum, down_sum = reduced[experts]
        expert_up_sum, expert_down_sum = [
            jnp.stack([reduced[e][part] for e in range(experts)]) for part in range(2)
        ]
        qkv_sum, out_total, ada_sum = [
            lax.psum_scatter(a.astype(BF16), "dp", scatter_dimension=0, tiled=True).astype(F32)
            for a in (qkv_sum, out_total, ada_sum)
        ]
        bias_all = lax.psum(bias_all, "dp")
    share = bias_all.shape[0] // (n_dp * n_mp)
    return (
        output,
        patches_grad,
        conditioning_grad,
        ada_sum,
        lax.dynamic_slice_in_dim(bias_all, (dp * n_mp + mp) * share, share),
        qkv_sum.reshape(rows, 3, -1),
        out_total.T,
        up_sum,
        down_sum.T,
        expert_up_sum,
        jnp.swapaxes(expert_down_sum, 1, 2),
    )


def solution(mesh):
    in_specs = (
        P(("dp", "mp"), None),
        P(("dp", "mp"), None),
        P(("dp", "mp"), None),
        P("dp", None),
        P("dp", None),
        P("dp", None),
        P(),
        P(),
        P(None, None, "mp"),
        P("mp", None),
        P(None, "mp"),
        P("mp", None),
        P(None, None, "mp"),
        P(None, "mp", None),
    )
    out_specs = (
        P(("dp", "mp"), None),
        P(("dp", "mp"), None),
        P(("dp", "mp"), None),
        P("dp", "mp"),
        P(("dp", "mp")),
        P("dp", None, "mp"),
        P("mp", "dp"),
        P("dp", "mp"),
        P("mp", "dp"),
        P(None, "dp", "mp"),
        P(None, "mp", "dp"),
    )
    return jax.shard_map(local, mesh=mesh, in_specs=in_specs, out_specs=out_specs, check_vma=False)
```

time: 604 us -> 479 us (0.79)
  local copies, waits for them, and re-layouts: 67 us -> 20.8 us
  waiting for transfers between devices: 39.5 us -> 13.1 us
  Pallas kernels: 447 us -> 421 us
  other arithmetic: 15 us -> 3.17 us
  matrix products: 17 us -> 10.7 us
    unnamed x114 -> x44, local copies, waits for them, and re-layouts: 39.6 us -> 8.49 us
    ppermute x16 -> x7, waiting for transfers between devices: 39.5 us -> 13.1 us  [swap(): return lax.ppermute(value, axis, [(i, i ^ mask) for i in range(size)])]
    dot_general x1 -> x0, matrix products: 10.2 us -> none  [nt(): lax.dot_general(a, b, (((1,), (1,)), ((), ())), preferred_element_type=F32)]
    slice x7 -> x1, local copies, waits for them, and re-layouts: 11 us -> 0.73 us  [local(): bias_all = bias_all[:2 * n_mp].reshape(-1)]
    pallas_call x1, Pallas kernels: 62 us -> 51.9 us  [run_attention_back(): pl.pallas_call(functools.partial(attention_back_kernel, heads, exchange,...]
    pallas_call x8 -> x5, Pallas kernels: 332 us -> 323 us  [the longest x1 148 us: run_long(): pl.pallas_call(functools.partial(long_kernel, count, exchange, units, uni...]
    pallas_call x1, Pallas kernels: 37 us -> 30.7 us  [run_expert_grads(): pl.pallas_call(functools.partial(expert_grads_kernel, columns, exchange,...]
  transfers between devices with their start and end apart: 16 -> 7, of which waited for: 2 -> 2; matrix products, arithmetic and copies ran while one was open for 8% -> 5% of each run, Pallas kernels for 9% -> 3%
where the time goes in v2:
time: 479 us; the launch traced here: 476 us
  Pallas kernels  421 us (88%)
  local copies, waits for them, and re-layouts  20.8 us (4%)
  waiting for transfers between devices  13.1 us (3%)
  matrix products  10.7 us (2%)
  starting transfers between devices  5.33 us (1%)
    pallas_call x1, Pallas kernels, run_long(): pl.pallas_call(functools.partial(long_kernel, count, exchange, units, uni...  148 us
    pallas_call x1, Pallas kernels, run_tail(): pl.pallas_call(functools.partial(tail_kernel, orders, rows, exchange), gr...  98.4 us
    pallas_call x2, Pallas kernels, run_experts(): pl.pallas_call(functools.partial(expert_kernel, columns, gathers, first,...  68.5 us
    pallas_call x1, Pallas kernels, run_attention_back(): pl.pallas_call(functools.partial(attention_back_kernel, heads, exchange,...  51.9 us
    pallas_call x1, Pallas kernels, run_expert_grads(): pl.pallas_call(functools.partial(expert_grads_kernel, columns, exchange,...  30.7 us
    pallas_call x1, Pallas kernels, run_forward(): pl.pallas_call(functools.partial(forward_kernel, heads), grid=(rows,), in...  16 us
    ppermute x7, waiting for transfers between devices, swap(): return lax.ppermute(value, axis, [(i, i ^ mask) for i in range(size)])  13.1 us
    dot_general x1, matrix products, local(): jnp.dot(silu_cond, ada_weight, preferred_element_type=F32)  10.7 us
  transfers between devices with their start and end apart: 7, of which 2 were waited for; matrix products, arithmetic and copies ran while one was open for 5% of the time, Pallas kernels for 3%

profile of v2, /device:TPU:0, one launch (start us, length us, event | category | flops | bytes accessed | tf_op | source)
XLA Modules:
  0.0 475.6 jit_solution(7010919301892365720)
XLA Ops:
  0.6 0.0 copy-start
  0.7 0.0 copy-start.19
  0.7 0.0 copy-start.20
  0.7 0.0 copy-start.15
  0.7 3.0 collective-permute-start
  3.7 0.0 collective-permute-start.2
  3.7 0.2 collective-permute-start.1
  3.9 0.3 collective-permute-start.4
  4.2 10.7 %convolution_add_fusion.shift_one.scale_one.gate_one.shift_two.scale_two.gate_two = f32[512,4608]{1,0:T(8,128)} fusion(bf16[768,4608]{1,0:T(8,128)(2,1)} %weight.1, f32[4608]{0:T(1024)} %param.21, bf16[512,768]{1,0:T(8,128)(2,1)} %cond.1), kind=kOutput, calls=%fused_computation | convolution fusion | flops 3628597248 | bytes 17319936 | tf_op jit(solution)/shard_map/dot_general | solution.py:1337
  14.9 0.0 copy-done.19
  14.9 0.0 copy-done.20
  14.9 0.1 broadcast_select_fusion
  15.0 0.0 copy-done.15
  15.0 0.0 copy-start.18
  15.1 1.7 fusion.4.refs_2_
  16.8 7.7 %collective-permute-done = bf16[768,576]{0,1:T(8,128)(2,1)} collective-permute-done((bf16[768,576]{0,1:T(8,128)(2,1)}, bf16[768,576]{0,1:T(8,128)(2,1)}, u32[]{:S(2)}, u32[]{:S(2)}) %collective-permute-start) | collective-permute-done | bytes 884768 | tf_op jit(solution)/shard_map/ppermute | solution.py:38
  24.5 0.0 collective-permute-start.3
  24.5 5.4 %collective-permute-done.1.refs_5_.refs_9_ = bf16[192,768]{1,0:T(8,128)(2,1)S(1)} collective-permute-done((bf16[192,768]{1,0:T(8,128)(2,1)}, bf16[192,768]{1,0:T(8,128)(2,1)S(1)}, u32[]{:S(2)}, u32[]{:S(2)}) %collective-permute-start.1) | collective-permute-done | bytes 294944 | tf_op jit(solution)/shard_map/ppermute | solution.py:38
  29.9 1.7 collective-permute-start.6
  31.6 0.0 copy-start.17
  31.7 1.5 copy.61.refs_0_.refs_4_
  33.2 1.3 copy.66.refs_0_.gates
  34.5 0.0 copy-done.16
  34.5 0.1 copy.60.seg_col
  34.6 0.0 copy-start.2
  34.7 0.0 copy-start.14
  34.7 0.1 collective-permute-start.5
  34.8 1.4 fusion.3.silu_cond
  36.1 2.2 copy.62.refs_1_.refs_5_
  38.4 0.0 collective-permute-done.2
  38.4 2.3 copy.63.refs_2_.refs_6_
  40.7 0.0 collective-permute-done.3
  40.7 2.2 copy.64.refs_3_.refs_7_
  42.9 0.0 collective-permute-done.4.refs_6_.refs_10_
  42.9 0.0 collective-permute-done.5.refs_7_.refs_11_
  42.9 0.0 copy-done.4
  42.9 0.0 copy-done.2
  42.9 0.0 copy-done.14
  42.9 0.0 copy-done.3
  43.0 0.0 copy-start.6
  43.0 16.0 %attention_half.1 = (bf16[512,768]{1,0:T(8,128)(2,1)S(1)}, bf16[512,576]{1,0:T(8,128)(2,1)S(1)}, bf16[512,576]{1,0:T(8,128)(2,1)S(1)}, bf16[512,576]{1,0:T(8,128...) custom-call(bf16[512,768]{1,0:T(8,128)(2,1)} %base.5, ...), custom_call_target="tpu_custom_call" | custom-call | flops 176160768 | bytes 983040 | tf_op jit(solution)/shard_map/attention_half/pallas_call | solution.py:343
  58.9 0.0 copy-done.6
  58.9 0.0 copy-start.7
  59.0 0.9 copy-done.7
  59.9 0.9 copy-done.8
  60.8 0.9 copy-done.9
  61.6 0.9 copy-done.10
  62.5 0.8 copy-done.11
  63.3 0.8 copy-done.12
  64.2 0.7 copy-done.13
  64.9 0.0 collective-permute-done.6.refs_3_
  64.9 34.2 %experts_1.1 = (bf16[4,192,512]{2,1,0:T(8,128)(2,1)}, bf16[4,192,512]{2,1,0:T(8,128)(2,1)}, bf16[4,192,256]{2,1,0:T(8,128)(2,1)}, bf16[4,192,256]{2,1,0:T(8,128)...) custom-call(f32[2048,16]{1,0:T(8,128)} %copy.66.refs_0_.gates, ...), custom_call_target="tpu_custom_call" | custom-call | flops 905969664 | bytes 2260992 | tf_op jit(solution)/shard_map/experts_1/pallas_call | solution.py:989
  99.1 148.4 %experts_long.1 = (f32[2048,768]{1,0:T(8,128)}, f32[2048,768]{1,0:T(8,128)}, f32[3,192,768]{2,1,0:T(8,128)}, f32[1,192,768]{2,1,0:T(8,128)}, bf16[2,192,512]{2,1...) custom-call(f32[2048,16]{1,0:T(8,128)} %copy.66.refs_0_.gates, ...), custom_call_target="tpu_custom_call" | custom-call | flops 5435817984 | bytes 4718592 | tf_op jit(solution)/shard_map/experts_long/pallas_call | solution.py:1195
  247.5 34.2 %experts_2.1 = (bf16[2048,768]{1,0:T(8,128)(2,1)}, bf16[2048,768]{1,0:T(8,128)(2,1)}, bf16[2048,768]{1,0:T(8,128)(2,1)}, bf16[2048,768]{1,0:T(8,128)(2,1)}, bf16...) custom-call(f32[2048,16]{1,0:T(8,128)} %copy.66.refs_0_.gates, ...), custom_call_target="tpu_custom_call" | custom-call | flops 1207959552 | bytes 2555904 | tf_op jit(solution)/shard_map/experts_2/pallas_call | solution.py:989
  281.8 30.7 %expert_grads.1 = (bf16[4,192,768]{2,1,0:T(8,128)(2,1)}, bf16[4,192,768]{2,1,0:T(8,128)(2,1)}, bf16[4,192,768]{2,1,0:T(8,128)(2,1)}, bf16[4,192,768]{2,1,0:T(8,1...) custom-call(f32[2048,16]{1,0:T(8,128)} %copy.66.refs_0_.gates, ...), custom_call_target="tpu_custom_call" | custom-call | flops 603979776 | bytes 1179648 | tf_op jit(solution)/shard_map/expert_grads/pallas_call | solution.py:1285
  312.5 51.9 %attention_back.1 = (f32[512,768]{1,0:T(8,128)}, bf16[512,3840]{1,0:T(8,128)(2,1)}, bf16[16,96,768]{2,1,0:T(8,128)(2,1)}, bf16[16,96,768]{2,1,0:T(8,128)(2,1)}, ...) custom-call(bf16[512,768]{1,0:T(8,128)(2,1)} %base.5, ...), custom_call_target="tpu_custom_call" | custom-call | flops 364904448 | bytes 1474560 | tf_op jit(solution)/shard_map/attention_back/pallas_call | solution.py:503
  364.3 98.4 %tail.1 = (f32[512,768]{1,0:T(8,128)}, bf16[512,768]{1,0:T(8,128)(2,1)}, f32[96,576]{1,0:T(8,128)}, f32[96,192]{1,0:T(8,128)}, f32[96,1152]{1,0:T(8,128)}, /*ind...) custom-call(bf16[512,768]{1,0:T(8,128)(2,1)} %cond.1, bf16[512,768]{1,0:T(8,128)(2,1)} %fusion.3.silu_cond, ...), custom_call_target="tpu_custom_call" | custom-call | flops 1811939328 | bytes 3686400 | tf_op jit(solution)/shard_map/tail/pallas_call | solution.py:670
  462.7 1.1 copy.74
  463.8 0.9 copy.75
  464.7 1.6 copy.76
  466.3 0.7 slice.7
  467.1 0.1 reshape.40
  467.1 0.6 dynamic_slice.23
  467.8 7.6 %finish.1 = (bf16[512,768]{1,0:T(8,128)(2,1)}, f32[512,768]{1,0:T(8,128)}, f32[512,768]{1,0:T(8,128)}, f32[96,1152]{1,0:T(8,128)}, f32[8,96,768]{2,1,0:T(8,128)}...) custom-call(f32[3,192,768]{2,1,0:T(8,128)} %get-tuple-element.103.refs_0_.refs_1_.refs_2_, ...), custom_call_target="tpu_custom_call" | custom-call | tf_op jit(solution)/shard_map/finish/pallas_call | solution.py:729
  (23 shorter events, 0.1 us)
Async XLA Ops:
  0.6 33.8 %copy-start = (s32[8,256]{1,0:T(8,128)S(1)}, s32[8,256]{1,0:T(8,128)}, u32[]{:S(2)}) copy-start(s32[8,256]{1,0:T(8,128)} %param.17) | copy-start | bytes 24580
  0.7 14.2 %copy-start.19 = (f32[2048,2]{0,1:T(2,128)S(1)}, f32[2048,2]{0,1:T(2,128)}, u32[]{:S(2)}) copy-start(f32[2048,2]{0,1:T(2,128)} %param.19) | copy-start | bytes 49156
  0.7 14.2 %copy-start.20 = (s32[2048,2]{0,1:T(2,128)S(1)}, s32[2048,2]{0,1:T(2,128)}, u32[]{:S(2)}) copy-start(s32[2048,2]{0,1:T(2,128)} %param.18) | copy-start | bytes 49156
  0.7 14.4 %copy-start.15 = (bf16[512,768]{1,0:T(8,128)(2,1)S(1)}, bf16[512,768]{1,0:T(8,128)(2,1)}, u32[]{:S(2)}) copy-start(bf16[512,768]{1,0:T(8,128)(2,1)} %cotangent.3) | copy-start | bytes 2359300
  0.7 23.8 %collective-permute-start = (bf16[768,576]{0,1:T(8,128)(2,1)}, bf16[768,576]{0,1:T(8,128)(2,1)}, u32[]{:S(2)}, u32[]{:S(2)}) collective-permute-start(bf16[768,576]{0,1:T(8,128)(2,1)} %bitcast.19), channel_id=1, source_target_pairs={{0,2},{1,3},{2,0},{3,1},{4,6},{5,7},{6,4},{7,5},{8,10},{9,11},{10,... | collective-permute-start | bytes 2654216 | tf_op jit(solution)/shard_map/ppermute | solution.py:38
  3.7 34.7 %collective-permute-start.2 = (bf16[768,576]{0,1:T(8,128)(2,1)}, bf16[768,576]{0,1:T(8,128)(2,1)}, u32[]{:S(2)}, u32[]{:S(2)}) collective-permute-start(bf16[768,576]{0,1:T(8,128)(2,1)} %bitcast.20), channel_id=1, source_target_pairs={{0,1},{1,0},{2,3},{3,2},{4,5},{5,4},{6,7},{7,6},{8,9},{9,8},{10,11... | collective-permute-start | bytes 2654216 | tf_op jit(solution)/shard_map/ppermute | solution.py:38
  3.7 26.2 %collective-permute-start.1 = (bf16[192,768]{1,0:T(8,128)(2,1)}, bf16[192,768]{1,0:T(8,128)(2,1)S(1)}, u32[]{:S(2)}, u32[]{:S(2)}) collective-permute-start(bf16[192,768]{1,0:T(8,128)(2,1)} %refs_8_.1), channel_id=1, source_target_pairs={{0,2},{1,3},{2,0},{3,1},{4,6},{5,7},{6,4},{7,5},{8,10},{9,11},{10,... | collective-permute-start | bytes 884744 | tf_op jit(solution)/shard_map/ppermute | solution.py:38
  3.9 39.0 %collective-permute-start.4 = (bf16[192,768]{1,0:T(8,128)(2,1)}, bf16[192,768]{1,0:T(8,128)(2,1)S(1)}, u32[]{:S(2)}, u32[]{:S(2)}) collective-permute-start(bf16[192,768]{1,0:T(8,128)(2,1)} %refs_8_.1), channel_id=1, source_target_pairs={{0,1},{1,0},{2,3},{3,2},{4,5},{5,4},{6,7},{7,6},{8,9},{9,8},{10,11... | collective-permute-start | bytes 884744 | tf_op jit(solution)/shard_map/ppermute | solution.py:38
  15.0 16.6 %copy-start.18 = (bf16[768,3,192]{0,2,1:T(8,128)(2,1)S(1)}, bf16[768,3,192]{0,2,1:T(8,128)(2,1)}, u32[]{:S(2)}) copy-start(bf16[768,3,192]{0,2,1:T(8,128)(2,1)} %param.22) | copy-start | bytes 2654212
  16.7 17.7 %copy-start.16 = (bf16[512,768]{1,0:T(8,128)(2,1)}, bf16[512,768]{1,0:T(8,128)(2,1)S(1)}, u32[]{:S(2)}) copy-start(bf16[512,768]{1,0:T(8,128)(2,1)S(1)} %fusion.4.refs_2_) | copy-start | bytes 2359300
  24.5 16.2 %collective-permute-start.3 = (bf16[768,576]{0,1:T(8,128)(2,1)}, bf16[768,576]{0,1:T(8,128)(2,1)}, u32[]{:S(2)}, u32[]{:S(2)}) collective-permute-start(bf16[768,576]{0,1:T(8,128)(2,1)} %collective-permute-done), channel_id=1, source_target_pairs={{0,1},{1,0},{2,3},{3,2},{4,5},{5,4},{6,7},{7,6},{8,9},{9,8},{10,11... | collective-permute-start | bytes 2654216 | tf_op jit(solution)/shard_map/ppermute | solution.py:38
  29.9 13.0 %copy-start.4 = (bf16[192,768]{1,0:T(8,128)(2,1)}, bf16[192,768]{1,0:T(8,128)(2,1)S(1)}, u32[]{:S(2)}) copy-start(bf16[192,768]{1,0:T(8,128)(2,1)S(1)} %collective-permute-done.1.refs_5_.refs_9_) | copy-start | bytes 884740
  29.9 35.0 %collective-permute-start.6 = (bf16[512,768]{1,0:T(8,128)(2,1)S(1)}, bf16[512,768]{1,0:T(8,128)(2,1)}, u32[]{:S(2)}, u32[]{:S(2)}) collective-permute-start(bf16[512,768]{1,0:T(8,128)(2,1)S(1)} %fusion.4.refs_2_), channel_id=1, source_target_pairs={{0,2},{1,3},{2,0},{3,1},{4,6},{5,7},{6,4},{7,5},{8,10},{9,11},{10,... | collective-permute-start | bytes 2359304 | tf_op jit(solution)/shard_map/ppermute | solution.py:38
  31.6 3.1 copy-start.17
  34.6 8.3 %copy-start.2 = (s32[2,256,1]{2,1,0:T(8,128)}, s32[2,256,1]{2,1,0:T(8,128)S(1)}, u32[]{:S(2)}) copy-start(s32[2,256,1]{2,1,0:T(8,128)S(1)} %copy.60.seg_col) | copy-start | bytes 6148
  34.7 8.3 %copy-start.14 = (s32[2,1,256]{2,1,0:T(1,128)}, s32[2,1,256]{2,1,0:T(1,128)S(1)}, u32[]{:S(2)}) copy-start(s32[2,1,256]{2,1,0:T(1,128)S(1)} %broadcast_in_dim.53.seg_row) | copy-start | bytes 6148
  34.7 8.2 %collective-permute-start.5 = (bf16[192,768]{1,0:T(8,128)(2,1)S(1)}, bf16[192,768]{1,0:T(8,128)(2,1)S(1)}, u32[]{:S(2)}, u32[]{:S(2)}) collective-permute-start(bf16[192,768]{1,0:T(8,128)(2,1)S(1)} %collective-permute-done.1.refs_5_.refs_9_), channel_id=1, source_target_pairs={{0,1},{1,0},{2,3},{3,2},{4,5},{5,4},{6,7},{7,6},{8,9},{9,8},{10,11... | collective-permute-start | bytes 884744 | tf_op jit(solution)/shard_map/ppermute | solution.py:38
  38.4 4.6 copy-start.3
  42.9 16.0 %copy-start.5 = (bf16[192,768]{1,0:T(8,128)(2,1)}, bf16[192,768]{1,0:T(8,128)(2,1)S(1)}, u32[]{:S(2)}) copy-start(bf16[192,768]{1,0:T(8,128)(2,1)S(1)} %collective-permute-done.4.refs_6_.refs_10_) | copy-start | bytes 884740
  43.0 16.0 %copy-start.6 = (bf16[192,768]{1,0:T(8,128)(2,1)}, bf16[192,768]{1,0:T(8,128)(2,1)S(1)}, u32[]{:S(2)}) copy-start(bf16[192,768]{1,0:T(8,128)(2,1)S(1)} %collective-permute-done.5.refs_7_.refs_11_) | copy-start | bytes 884740
  58.9 0.9 copy-start.7
  59.9 0.9 copy-start.8
  60.8 0.9 copy-start.9
  61.6 0.9 copy-start.10
  62.5 0.8 copy-start.11
  63.3 0.8 copy-start.12
  64.2 0.7 copy-start.13
  467.8 7.6 %copy-start.1 = (s32[8,256]{1,0:T(8,128)S(1)}, s32[8,256]{1,0:T(8,128)}, u32[]{:S(2)}) copy-start(s32[8,256]{1,0:T(8,128)} %param.17) | copy-start | bytes 24580

commit v3 on v2

--- a/solution.py
+++ b/solution.py
@@ -279,7 +279,7 @@
     lse_all = jnp.zeros(lse_out.shape, F32)
     attn = jnp.zeros(x.shape, F32)
     for block in range(4):
-        qkv[block][...] = nn(normed, weights[block][...]).astype(BF16)
+        qkv[block][...] = nt(normed, weights[block][...]).astype(BF16)
         for head in range(heads):
             at = head * HEAD_DIM
             q = qkv[block][:, at : at + HEAD_DIM]
@@ -334,7 +334,7 @@
 def run_forward(patches, modulation, segments, qkv_parts, out_parts):
     rows, seq = segments.shape
     tokens, width = patches.shape
-    columns = qkv_parts[0].shape[1]
+    columns = qkv_parts[0].shape[0]
     heads = columns // (3 * HEAD_DIM)
     work = rows * 4 * heads * seq * seq
     shapes = (
@@ -349,7 +349,7 @@
         + [whole_block(w) for w in qkv_parts + out_parts],
         out_specs=[row_block(seq, c) for c, _ in shapes],
         out_shape=[jax.ShapeDtypeStruct((tokens, c), t) for c, t in shapes],
-        compiler_params=pltpu.CompilerParams(vmem_limit_bytes=48 << 20),
+        compiler_params=pltpu.CompilerParams(vmem_limit_bytes=62 << 20),
         cost_estimate=cost(
             flops=4 * work * HEAD_DIM + 8 * tokens * width * width,
             bytes_accessed=40 * tokens * width,
@@ -446,7 +446,7 @@
                 probs.astype(BF16), g
             ).astype(BF16)
         made = grad_qkv[...]
-        normed_grad += nt(made, weights[block][...])
+        normed_grad += nn(made, weights[block][...])
         of_qkv = tn(normed[...], made)
         of_out = tn(upper, attended[:, block * span : (block + 1) * span])
 
@@ -633,6 +633,8 @@
         if m == half[-1]:
             exchange.start(0)
             exchange.start(1)
+            for n in range(len(late)):
+                exchange.advance(3 + n)
     exchange.advance(0)
     exchange.advance(1)
     weight_load.wait()
@@ -1330,7 +1332,7 @@
     dp, mp = lax.axis_index("dp"), lax.axis_index("mp")
     rows = width // n_dp
 
-    qkv_parts = gather_mp(qkv_weight.reshape(width, -1))
+    qkv_parts = gather_mp(jnp.transpose(qkv_weight, (1, 2, 0)).reshape(-1, width))
     out_parts = gather_mp(out_weight)
 
     silu_cond = jax.nn.silu(conditioning.astype(F32)).astype(BF16)
@@ -1485,7 +1487,7 @@
         out_parts,
         tail_orders[0],
         tail_rows,
-        [(out_chain, 2)] + jobs(n2=late),
+        [(out_chain, 2)] + jobs(n1=late),
         6,
     )
     patches_grad, pieces, heads_halves = results[0], results[1], results[2:4]
@@ -1509,7 +1511,7 @@
         ada_weight,
         tail_orders[1:],
         tail_rows,
-        [(c, number) for c in ada_chains] + [(heads_chain, number)] + jobs(n1=late),
+        [(c, number) for c in ada_chains] + [(heads_chain, number)] + jobs(n2=late),
         7,
     )
     conditioning_grad, output, qkv_sum, out_total, ada_sum, bias_all = results[:6]

time: 479 us -> 464 us (0.969)
  local copies, waits for them, and re-layouts: 20.8 us -> 9.97 us
  Pallas kernels: 421 us -> 416 us
    pallas_call x1, Pallas kernels: 51.9 us -> 43.5 us  [run_attention_back(): pl.pallas_call(functools.partial(attention_back_kernel, heads, exchange,...]
  transfers between devices with their start and end apart: 7 -> 7, of which waited for: 2 -> 3; matrix products, arithmetic and copies ran while one was open for 5% -> 4% of each run, Pallas kernels for 3% -> 4%
where the time goes in v3:
time: 464 us; the launch traced here: 460 us
  Pallas kernels  416 us (90%)
  waiting for transfers between devices  12.6 us (3%)
  matrix products  10.7 us (2%)
  local copies, waits for them, and re-layouts  9.97 us (2%)
  starting transfers between devices  5.26 us (1%)
    pallas_call x1, Pallas kernels, run_long(): pl.pallas_call(functools.partial(long_kernel, count, exchange, units, uni...  149 us
    pallas_call x1, Pallas kernels, run_tail(): pl.pallas_call(functools.partial(tail_kernel, orders, rows, exchange), gr...  98.7 us
    pallas_call x2, Pallas kernels, run_experts(): pl.pallas_call(functools.partial(expert_kernel, columns, gathers, first,...  68.7 us
    pallas_call x1, Pallas kernels, run_attention_back(): pl.pallas_call(functools.partial(attention_back_kernel, heads, exchange,...  43.5 us
    pallas_call x1, Pallas kernels, run_expert_grads(): pl.pallas_call(functools.partial(expert_grads_kernel, columns, exchange,...  30.6 us
    pallas_call x1, Pallas kernels, run_forward(): pl.pallas_call(functools.partial(forward_kernel, heads), grid=(rows,), in...  18.4 us
    ppermute x7, waiting for transfers between devices, swap(): return lax.ppermute(value, axis, [(i, i ^ mask) for i in range(size)])  12.6 us
    dot_general x1, matrix products, local(): jnp.dot(silu_cond, ada_weight, preferred_element_type=F32)  10.7 us
  transfers between devices with their start and end apart: 7, of which 3 were waited for; matrix products, arithmetic and copies ran while one was open for 4% of the time, Pallas kernels for 4%

profile of v3, /device:TPU:0, one launch (start us, length us, event | category | flops | bytes accessed | tf_op | source)
XLA Modules:
  0.0 459.6 jit_solution(6655891696274414426)
XLA Ops:
  0.6 0.0 copy-start
  0.7 0.0 copy-start.9
  0.7 0.0 copy-start.10
  0.7 0.0 copy-start.2
  0.7 3.0 collective-permute-start
  3.7 0.0 collective-permute-start.2
  3.7 0.2 collective-permute-start.1
  3.9 0.4 collective-permute-start.4
  4.2 10.7 %convolution_add_fusion.shift_one.scale_one.gate_one.shift_two.scale_two.gate_two = f32[512,4608]{1,0:T(8,128)} fusion(bf16[768,4608]{1,0:T(8,128)(2,1)} %weight.1, f32[4608]{0:T(1024)} %param.21, bf16[512,768]{1,0:T(8,128)(2,1)} %cond.1), kind=kOutput, calls=%fused_computation | convolution fusion | flops 3628597248 | bytes 17319936 | tf_op jit(solution)/shard_map/dot_general | solution.py:1339
  14.9 0.0 copy-done.9
  14.9 0.0 copy-done.10
  15.0 0.1 broadcast_select_fusion
  15.1 0.0 copy-done.2
  15.1 2.5 fusion.4.refs_2_
  17.6 0.0 copy-start.5
  17.6 6.8 %collective-permute-done.refs_1_.refs_5_ = bf16[576,768]{1,0:T(8,128)(2,1)S(1)} collective-permute-done((bf16[576,768]{1,0:T(8,128)(2,1)}, bf16[576,768]{1,0:T(8,128)(2,1)S(1)}, u32[]{:S(2)}, u32[]{:S(2)}) %collective-permute-start) | collective-permute-done | bytes 884768 | tf_op jit(solution)/shard_map/ppermute | solution.py:38
  24.4 0.0 copy-start.3
  24.4 0.0 collective-permute-start.3
  24.4 5.5 %collective-permute-done.1.refs_5_.refs_9_ = bf16[192,768]{1,0:T(8,128)(2,1)S(1)} collective-permute-done((bf16[192,768]{1,0:T(8,128)(2,1)}, bf16[192,768]{1,0:T(8,128)(2,1)S(1)}, u32[]{:S(2)}, u32[]{:S(2)}) %collective-permute-start.1) | collective-permute-done | bytes 294944 | tf_op jit(solution)/shard_map/ppermute | solution.py:38
  29.9 0.0 copy-start.6
  29.9 1.7 collective-permute-start.6
  31.7 1.3 copy.49.refs_0_.gates
  33.0 0.0 copy-done
  33.0 0.9 copy.47.seg_col
  33.8 0.6 broadcast_in_dim.53.seg_row
  34.4 0.0 collective-permute-start.5
  34.4 0.0 copy-done.5
  34.4 1.3 fusion.3.silu_cond
  35.8 0.0 copy-done.3
  35.8 0.0 copy-done.6
  35.8 0.0 collective-permute-done.4.refs_6_.refs_10_
  35.8 0.0 copy-start.7
  35.8 0.2 collective-permute-done.5.refs_7_.refs_11_
  36.0 0.5 copy-done.7
  36.5 0.0 copy-start.8
  36.5 0.0 collective-permute-done.2.refs_2_.refs_6_
  36.5 0.7 copy-done.8
  37.2 0.0 collective-permute-done.3.refs_3_.refs_7_
  37.2 0.0 copy-start.4
  37.2 0.9 copy-done.4
  38.1 18.4 %attention_half.1 = (bf16[512,768]{1,0:T(8,128)(2,1)}, bf16[512,576]{1,0:T(8,128)(2,1)}, bf16[512,576]{1,0:T(8,128)(2,1)}, bf16[512,576]{1,0:T(8,128)(2,1)}, bf1...) custom-call(bf16[512,768]{1,0:T(8,128)(2,1)} %base.5, ...), custom_call_target="tpu_custom_call" | custom-call | flops 176160768 | bytes 983040 | tf_op jit(solution)/shard_map/attention_half/pallas_call | solution.py:343
  56.5 0.0 collective-permute-done.6.refs_3_
  56.5 34.3 %experts_1.1 = (bf16[4,192,512]{2,1,0:T(8,128)(2,1)}, bf16[4,192,512]{2,1,0:T(8,128)(2,1)}, bf16[4,192,256]{2,1,0:T(8,128)(2,1)}, bf16[4,192,256]{2,1,0:T(8,128)...) custom-call(f32[2048,16]{1,0:T(8,128)} %copy.49.refs_0_.gates, ...), custom_call_target="tpu_custom_call" | custom-call | flops 905969664 | bytes 2260992 | tf_op jit(solution)/shard_map/experts_1/pallas_call | solution.py:991
  90.9 148.5 %experts_long.1 = (f32[2048,768]{1,0:T(8,128)}, f32[2048,768]{1,0:T(8,128)}, f32[3,192,768]{2,1,0:T(8,128)}, f32[1,192,768]{2,1,0:T(8,128)}, bf16[2,192,512]{2,1...) custom-call(f32[2048,16]{1,0:T(8,128)} %copy.49.refs_0_.gates, ...), custom_call_target="tpu_custom_call" | custom-call | flops 5435817984 | bytes 4718592 | tf_op jit(solution)/shard_map/experts_long/pallas_call | solution.py:1197
  239.4 34.4 %experts_2.1 = (bf16[2048,768]{1,0:T(8,128)(2,1)}, bf16[2048,768]{1,0:T(8,128)(2,1)}, bf16[2048,768]{1,0:T(8,128)(2,1)}, bf16[2048,768]{1,0:T(8,128)(2,1)}, bf16...) custom-call(f32[2048,16]{1,0:T(8,128)} %copy.49.refs_0_.gates, ...), custom_call_target="tpu_custom_call" | custom-call | flops 1207959552 | bytes 2555904 | tf_op jit(solution)/shard_map/experts_2/pallas_call | solution.py:991
  273.8 30.6 %expert_grads.1 = (bf16[4,192,768]{2,1,0:T(8,128)(2,1)}, bf16[4,192,768]{2,1,0:T(8,128)(2,1)}, bf16[4,192,768]{2,1,0:T(8,128)(2,1)}, bf16[4,192,768]{2,1,0:T(8,1...) custom-call(f32[2048,16]{1,0:T(8,128)} %copy.49.refs_0_.gates, ...), custom_call_target="tpu_custom_call" | custom-call | flops 603979776 | bytes 1179648 | tf_op jit(solution)/shard_map/expert_grads/pallas_call | solution.py:1287
  304.4 43.5 %attention_back.1 = (f32[512,768]{1,0:T(8,128)}, bf16[512,3840]{1,0:T(8,128)(2,1)}, bf16[16,96,768]{2,1,0:T(8,128)(2,1)}, bf16[16,96,768]{2,1,0:T(8,128)(2,1)}, ...) custom-call(bf16[512,768]{1,0:T(8,128)(2,1)} %base.5, ...), custom_call_target="tpu_custom_call" | custom-call | flops 364904448 | bytes 1474560 | tf_op jit(solution)/shard_map/attention_back/pallas_call | solution.py:503
  347.9 98.7 %tail.1 = (f32[512,768]{1,0:T(8,128)}, bf16[512,768]{1,0:T(8,128)(2,1)}, f32[96,576]{1,0:T(8,128)}, f32[96,192]{1,0:T(8,128)}, f32[96,1152]{1,0:T(8,128)}, /*ind...) custom-call(bf16[512,768]{1,0:T(8,128)(2,1)} %cond.1, bf16[512,768]{1,0:T(8,128)(2,1)} %fusion.3.silu_cond, ...), custom_call_target="tpu_custom_call" | custom-call | flops 1811939328 | bytes 3686400 | tf_op jit(solution)/shard_map/tail/pallas_call | solution.py:672
  446.7 1.1 copy.53
  447.8 0.9 copy.54
  448.6 1.6 copy.55
  450.3 0.7 slice.7
  451.0 0.1 reshape.40
  451.1 0.6 dynamic_slice.23
  451.7 0.0 copy-start.1
  451.7 7.6 %finish.1 = (bf16[512,768]{1,0:T(8,128)(2,1)}, f32[512,768]{1,0:T(8,128)}, f32[512,768]{1,0:T(8,128)}, f32[96,1152]{1,0:T(8,128)}, f32[8,96,768]{2,1,0:T(8,128)}...) custom-call(f32[3,192,768]{2,1,0:T(8,128)} %get-tuple-element.103.refs_0_.refs_1_.refs_2_, ...), custom_call_target="tpu_custom_call" | custom-call | tf_op jit(solution)/shard_map/finish/pallas_call | solution.py:731
  459.3 0.0 copy-done.1
  (6 shorter events, 0.1 us)
Async XLA Ops:
  0.6 32.3 %copy-start = (s32[8,256]{1,0:T(8,128)S(1)}, s32[8,256]{1,0:T(8,128)}, u32[]{:S(2)}) copy-start(s32[8,256]{1,0:T(8,128)} %param.17) | copy-start | bytes 24580
  0.7 14.3 %copy-start.9 = (f32[2048,2]{0,1:T(2,128)S(1)}, f32[2048,2]{0,1:T(2,128)}, u32[]{:S(2)}) copy-start(f32[2048,2]{0,1:T(2,128)} %param.19) | copy-start | bytes 49156
  0.7 14.3 %copy-start.10 = (s32[2048,2]{0,1:T(2,128)S(1)}, s32[2048,2]{0,1:T(2,128)}, u32[]{:S(2)}) copy-start(s32[2048,2]{0,1:T(2,128)} %param.18) | copy-start | bytes 49156
  0.7 14.4 %copy-start.2 = (bf16[512,768]{1,0:T(8,128)(2,1)S(1)}, bf16[512,768]{1,0:T(8,128)(2,1)}, u32[]{:S(2)}) copy-start(bf16[512,768]{1,0:T(8,128)(2,1)} %cotangent.3) | copy-start | bytes 2359300
  0.7 23.7 %collective-permute-start = (bf16[576,768]{1,0:T(8,128)(2,1)}, bf16[576,768]{1,0:T(8,128)(2,1)S(1)}, u32[]{:S(2)}, u32[]{:S(2)}) collective-permute-start(bf16[576,768]{1,0:T(8,128)(2,1)} %bitcast.16), channel_id=1, source_target_pairs={{0,2},{1,3},{2,0},{3,1},{4,6},{5,7},{6,4},{7,5},{8,10},{9,11},{10,... | collective-permute-start | bytes 2654216 | tf_op jit(solution)/shard_map/ppermute | solution.py:38
  3.7 32.8 %collective-permute-start.2 = (bf16[576,768]{1,0:T(8,128)(2,1)}, bf16[576,768]{1,0:T(8,128)(2,1)}, u32[]{:S(2)}, u32[]{:S(2)}) collective-permute-start(bf16[576,768]{1,0:T(8,128)(2,1)} %bitcast.17), channel_id=1, source_target_pairs={{0,1},{1,0},{2,3},{3,2},{4,5},{5,4},{6,7},{7,6},{8,9},{9,8},{10,11... | collective-permute-start | bytes 2654216 | tf_op jit(solution)/shard_map/ppermute | solution.py:38
  3.7 26.2 %collective-permute-start.1 = (bf16[192,768]{1,0:T(8,128)(2,1)}, bf16[192,768]{1,0:T(8,128)(2,1)S(1)}, u32[]{:S(2)}, u32[]{:S(2)}) collective-permute-start(bf16[192,768]{1,0:T(8,128)(2,1)} %refs_8_.1), channel_id=1, source_target_pairs={{0,2},{1,3},{2,0},{3,1},{4,6},{5,7},{6,4},{7,5},{8,10},{9,11},{10,... | collective-permute-start | bytes 884744 | tf_op jit(solution)/shard_map/ppermute | solution.py:38
  3.9 31.9 %collective-permute-start.4 = (bf16[192,768]{1,0:T(8,128)(2,1)}, bf16[192,768]{1,0:T(8,128)(2,1)S(1)}, u32[]{:S(2)}, u32[]{:S(2)}) collective-permute-start(bf16[192,768]{1,0:T(8,128)(2,1)} %refs_8_.1), channel_id=1, source_target_pairs={{0,1},{1,0},{2,3},{3,2},{4,5},{5,4},{6,7},{7,6},{8,9},{9,8},{10,11... | collective-permute-start | bytes 884744 | tf_op jit(solution)/shard_map/ppermute | solution.py:38
  17.6 16.9 %copy-start.5 = (bf16[512,768]{1,0:T(8,128)(2,1)S(1)}, bf16[512,768]{1,0:T(8,128)(2,1)}, u32[]{:S(2)}) copy-start(bf16[512,768]{1,0:T(8,128)(2,1)} %cond.1) | copy-start | bytes 2359300
  24.4 11.4 %copy-start.3 = (bf16[576,768]{1,0:T(8,128)(2,1)}, bf16[576,768]{1,0:T(8,128)(2,1)S(1)}, u32[]{:S(2)}) copy-start(bf16[576,768]{1,0:T(8,128)(2,1)S(1)} %collective-permute-done.refs_1_.refs_5_) | copy-start | bytes 2654212
  24.4 12.8 %collective-permute-start.3 = (bf16[576,768]{1,0:T(8,128)(2,1)S(1)}, bf16[576,768]{1,0:T(8,128)(2,1)S(1)}, u32[]{:S(2)}, u32[]{:S(2)}) collective-permute-start(bf16[576,768]{1,0:T(8,128)(2,1)S(1)} %collective-permute-done.refs_1_.refs_5_), channel_id=1, source_target_pairs={{0,1},{1,0},{2,3},{3,2},{4,5},{5,4},{6,7},{7,6},{8,9},{9,8},{10,11... | collective-permute-start | bytes 2654216 | tf_op jit(solution)/shard_map/ppermute | solution.py:38
  29.9 5.9 %copy-start.6 = (bf16[192,768]{1,0:T(8,128)(2,1)}, bf16[192,768]{1,0:T(8,128)(2,1)S(1)}, u32[]{:S(2)}) copy-start(bf16[192,768]{1,0:T(8,128)(2,1)S(1)} %collective-permute-done.1.refs_5_.refs_9_) | copy-start | bytes 884740
  29.9 26.7 %collective-permute-start.6 = (bf16[512,768]{1,0:T(8,128)(2,1)}, bf16[512,768]{1,0:T(8,128)(2,1)}, u32[]{:S(2)}, u32[]{:S(2)}) collective-permute-start(bf16[512,768]{1,0:T(8,128)(2,1)} %fusion.4.refs_2_), channel_id=1, source_target_pairs={{0,2},{1,3},{2,0},{3,1},{4,6},{5,7},{6,4},{7,5},{8,10},{9,11},{10,... | collective-permute-start | bytes 2359304 | tf_op jit(solution)/shard_map/ppermute | solution.py:38
  34.4 1.6 collective-permute-start.5
  35.8 0.7 copy-start.7
  36.5 0.7 copy-start.8
  37.2 0.9 copy-start.4
  451.7 7.6 %copy-start.1 = (s32[8,256]{1,0:T(8,128)S(1)}, s32[8,256]{1,0:T(8,128)}, u32[]{:S(2)}) copy-start(s32[8,256]{1,0:T(8,128)} %param.17) | copy-start | bytes 24580

commit v4 on v3

--- a/solution.py
+++ b/solution.py
@@ -641,12 +641,9 @@
     value = cond[...].astype(F32)
     gate = 1.0 / (1.0 + jnp.exp(-value))
     cond_grad[...] = nt(modulation_grad[...], weight_here[...]) * (gate * (1.0 + value * (1.0 - gate)))
-    for n in (2, 0, 1, 2):
-        exchange.advance(n) if exchange.left(n) > 1 else None
-    for n in range(len(late)):
-        exchange.advance(3 + n)
-    for n in (0, 2, 1):
-        exchange.advance(n) if exchange.left(n) > 1 else None
+    for n in [2] + [3 + n for n in range(len(late))] + [0, 1, 0, 2, 1, 2, 0, 1]:
+        if n > 2 or exchange.left(n) > 1:
+            exchange.advance(n)
     exchange.finish()
 
 
@@ -1339,15 +1336,8 @@
     modulation = jnp.dot(silu_cond, ada_weight, preferred_element_type=F32) + ada_bias[None, :]
     gate_two = modulation[:, 5 * width :]
     grad_mlp = (cotangent.astype(F32) * gate_two).astype(BF16)
-    grad_mlp, *far = lax.optimization_barrier((grad_mlp, qkv_parts[1], out_parts[1]))
-    qkv_parts[1], out_parts[1] = far
-    grad_far = swap(grad_mlp, "mp", 2)
-
     own_rows = tokens // seq
     own_segments = lax.dynamic_slice_in_dim(segments, mp * own_rows, own_rows, axis=0)
-    results = run_forward(patches, modulation, own_segments, qkv_parts, out_parts)
-    normed_one, qkv, attended, lse, attn_out, normed_two = results[0], results[1:5], *results[5:]
-
     number = jnp.arange(16, dtype=jnp.int32)[None, :]
     gates = jnp.sum(
         jnp.where(routes[:, :, None] == number[:, None, :], gate_values[:, :, None], 0.0), axis=1
@@ -1357,6 +1347,14 @@
         [lax.dynamic_slice_in_dim(gates, (mp ^ m) * tokens, tokens, axis=0) for m in MP_ORDER],
         axis=0,
     )
+    grad_mlp, qkv_parts[1], out_parts[1], gates, own_segments, silu_cond = lax.optimization_barrier(
+        (grad_mlp, qkv_parts[1], out_parts[1], gates, own_segments, silu_cond)
+    )
+    grad_far = swap(grad_mlp, "mp", 2)
+
+    results = run_forward(patches, modulation, own_segments, qkv_parts, out_parts)
+    normed_one, qkv, attended, lse, attn_out, normed_two = results[0], results[1:5], *results[5:]
+
     shared = (shared_up[None], shared_down[None], 0)
     weights = {e: (expert_up, expert_down, e) for e in range(experts)}
     weights[experts] = shared
@@ -1468,7 +1466,7 @@
     if even:
         y, z, rest = dp_steps(n_dp)[0], dp_steps(n_dp)[1], dp_steps(n_dp)[2:]
         core, x = MP_STEPS
-        tail_steps = [[core, x, y, z] + rest, [core, y, x, z] + rest, [core, x, y, z] + rest]
+        tail_steps = [[core, x, y, z] + rest, [core, y, x, z] + rest, [core, z, x, y] + rest]
     tail_orders = [block_order(steps) for steps in tail_steps]
 
     tail_rows = rows if even else width

time: 464 us -> 461 us (level)
    pallas_call x1, Pallas kernels: 98.7 us -> 92 us  [run_tail(): pl.pallas_call(functools.partial(tail_kernel, orders, rows, exchange), gr...]
  transfers between devices with their start and end apart: 7 -> 7, of which waited for: 3 -> 2; matrix products, arithmetic and copies ran while one was open for 4% -> 3% of each run, Pallas kernels for 4% -> 4%
where the time goes in v4:
time: 461 us; the launch traced here: 454 us
  Pallas kernels  412 us (89%)
  waiting for transfers between devices  13.6 us (3%)
  local copies, waits for them, and re-layouts  13.3 us (3%)
  matrix products  6.85 us (1%)
  starting transfers between devices  5.45 us (1%)
    pallas_call x1, Pallas kernels, run_long(): pl.pallas_call(functools.partial(long_kernel, count, exchange, units, uni...  146 us
    pallas_call x1, Pallas kernels, run_tail(): pl.pallas_call(functools.partial(tail_kernel, orders, rows, exchange), gr...  92 us
    pallas_call x2, Pallas kernels, run_experts(): pl.pallas_call(functools.partial(expert_kernel, columns, gathers, first,...  70.6 us
    pallas_call x1, Pallas kernels, run_attention_back(): pl.pallas_call(functools.partial(attention_back_kernel, heads, exchange,...  43.1 us
    pallas_call x1, Pallas kernels, run_expert_grads(): pl.pallas_call(functools.partial(expert_grads_kernel, columns, exchange,...  34 us
    pallas_call x1, Pallas kernels, run_forward(): pl.pallas_call(functools.partial(forward_kernel, heads), grid=(rows,), in...  18.2 us
    ppermute x7, waiting for transfers between devices, swap(): return lax.ppermute(value, axis, [(i, i ^ mask) for i in range(size)])  13.6 us
  transfers between devices with their start and end apart: 7, of which 2 were waited for; matrix products, arithmetic and copies ran while one was open for 3% of the time, Pallas kernels for 4%

profile of v4, /device:TPU:0, one launch (start us, length us, event | category | flops | bytes accessed | tf_op | source)
XLA Modules:
  0.0 454.4 jit_solution(9074695665661999673)
XLA Ops:
  0.6 0.0 copy-start
  0.7 0.5 collective-permute-start.2
  1.2 2.6 collective-permute-start
  3.7 0.1 collective-permute-start.1
  3.8 0.8 select_reduce_fusion
  4.6 0.0 copy-start.3
  4.6 0.0 copy-start.7
  4.6 6.9 %convolution_add_fusion.shift_one.scale_one.gate_one.shift_two.scale_two.gate_two = f32[512,4608]{1,0:T(8,128)S(1)} fusion(bf16[768,4608]{1,0:T(8,128)(2,1)} %weight.1, f32[4608]{0:T(1024)} %param.21, bf16[512,768]{1,0:T(8,128)(2,1)} %cond.1), kind=kOutput, calls=%fused_computation | convolution fusion | flops 3628597248 | bytes 17319936 | tf_op jit(solution)/shard_map/dot_general | solution.py:1336
  11.5 0.0 copy-start.2
  11.5 0.1 broadcast_select_fusion
  11.6 3.6 copy-done.2
  15.2 0.0 copy-done.3
  15.2 0.0 copy-done.7
  15.2 0.0 copy-start.8
  15.2 1.7 fusion.3
  16.9 7.6 %collective-permute-done.refs_1_.refs_5_ = bf16[576,768]{1,0:T(8,128)(2,1)S(1)} collective-permute-done((bf16[576,768]{1,0:T(8,128)(2,1)}, bf16[576,768]{1,0:T(8,128)(2,1)S(1)}, u32[]{:S(2)}, u32[]{:S(2)}) %collective-permute-start) | collective-permute-done | bytes 884768 | tf_op jit(solution)/shard_map/ppermute | solution.py:38
  24.5 0.0 copy-start.5
  24.5 0.0 collective-permute-start.3
  24.5 0.0 copy-done
  24.5 6.0 %collective-permute-done.1.refs_5_.refs_9_ = bf16[192,768]{1,0:T(8,128)(2,1)S(1)} collective-permute-done((bf16[192,768]{1,0:T(8,128)(2,1)}, bf16[192,768]{1,0:T(8,128)(2,1)S(1)}, u32[]{:S(2)}, u32[]{:S(2)}) %collective-permute-start.1) | collective-permute-done | bytes 294944 | tf_op jit(solution)/shard_map/ppermute | solution.py:38
  30.5 0.0 copy-start.9
  30.5 1.8 collective-permute-start.6
  32.3 0.0 copy-done.8
  32.3 0.0 collective-permute-start.4
  32.3 0.5 collective-permute-start.5
  32.8 0.6 broadcast_in_dim.53.seg_row
  33.4 0.9 copy.49.seg_col
  34.2 1.3 copy.51.refs_0_.gates
  35.5 0.0 collective-permute-done.4.refs_6_.refs_10_
  35.5 0.0 collective-permute-done.5.refs_7_.refs_11_
  35.5 0.0 collective-permute-done.2.refs_2_.refs_6_
  35.5 0.0 copy-done.5
  35.6 0.0 copy-done.9
  35.6 0.0 copy-start.4
  35.6 0.0 collective-permute-done.3.refs_3_.refs_7_
  35.6 0.9 copy-done.4
  36.5 0.0 copy-start.6
  36.5 0.9 copy-done.6
  37.4 18.2 %attention_half.1 = (bf16[512,768]{1,0:T(8,128)(2,1)}, bf16[512,576]{1,0:T(8,128)(2,1)}, bf16[512,576]{1,0:T(8,128)(2,1)}, bf16[512,576]{1,0:T(8,128)(2,1)}, bf1...) custom-call(bf16[512,768]{1,0:T(8,128)(2,1)} %base.5, ...), custom_call_target="tpu_custom_call" | custom-call | flops 176160768 | bytes 983040 | tf_op jit(solution)/shard_map/attention_half/pallas_call | solution.py:343
  55.6 0.0 collective-permute-done.6.refs_3_
  55.6 34.2 %experts_1.1 = (bf16[4,192,512]{2,1,0:T(8,128)(2,1)}, bf16[4,192,512]{2,1,0:T(8,128)(2,1)}, bf16[4,192,256]{2,1,0:T(8,128)(2,1)}, bf16[4,192,256]{2,1,0:T(8,128)...) custom-call(f32[2048,16]{1,0:T(8,128)} %copy.51.refs_0_.gates, ...), custom_call_target="tpu_custom_call" | custom-call | flops 905969664 | bytes 2260992 | tf_op jit(solution)/shard_map/experts_1/pallas_call | solution.py:988
  89.9 146.0 %experts_long.1 = (f32[2048,768]{1,0:T(8,128)}, f32[2048,768]{1,0:T(8,128)}, f32[3,192,768]{2,1,0:T(8,128)}, f32[1,192,768]{2,1,0:T(8,128)}, bf16[2,192,512]{2,1...) custom-call(f32[2048,16]{1,0:T(8,128)} %copy.51.refs_0_.gates, ...), custom_call_target="tpu_custom_call" | custom-call | flops 5435817984 | bytes 4718592 | tf_op jit(solution)/shard_map/experts_long/pallas_call | solution.py:1194
  235.9 36.4 %experts_2.1 = (bf16[2048,768]{1,0:T(8,128)(2,1)}, bf16[2048,768]{1,0:T(8,128)(2,1)}, bf16[2048,768]{1,0:T(8,128)(2,1)}, bf16[2048,768]{1,0:T(8,128)(2,1)}, bf16...) custom-call(f32[2048,16]{1,0:T(8,128)} %copy.51.refs_0_.gates, ...), custom_call_target="tpu_custom_call" | custom-call | flops 1207959552 | bytes 2555904 | tf_op jit(solution)/shard_map/experts_2/pallas_call | solution.py:988
  272.3 34.0 %expert_grads.1 = (bf16[4,192,768]{2,1,0:T(8,128)(2,1)}, bf16[4,192,768]{2,1,0:T(8,128)(2,1)}, bf16[4,192,768]{2,1,0:T(8,128)(2,1)}, bf16[4,192,768]{2,1,0:T(8,1...) custom-call(f32[2048,16]{1,0:T(8,128)} %copy.51.refs_0_.gates, ...), custom_call_target="tpu_custom_call" | custom-call | flops 603979776 | bytes 1179648 | tf_op jit(solution)/shard_map/expert_grads/pallas_call | solution.py:1284
  306.4 43.1 %attention_back.1 = (f32[512,768]{1,0:T(8,128)}, bf16[512,3840]{1,0:T(8,128)(2,1)}, bf16[16,96,768]{2,1,0:T(8,128)(2,1)}, bf16[16,96,768]{2,1,0:T(8,128)(2,1)}, ...) custom-call(bf16[512,768]{1,0:T(8,128)(2,1)} %base.5, ...), custom_call_target="tpu_custom_call" | custom-call | flops 364904448 | bytes 1474560 | tf_op jit(solution)/shard_map/attention_back/pallas_call | solution.py:503
  349.5 92.0 %tail.1 = (f32[512,768]{1,0:T(8,128)}, bf16[512,768]{1,0:T(8,128)(2,1)}, f32[96,576]{1,0:T(8,128)}, f32[96,192]{1,0:T(8,128)}, f32[96,1152]{1,0:T(8,128)}, /*ind...) custom-call(bf16[512,768]{1,0:T(8,128)(2,1)} %cond.1, bf16[512,768]{1,0:T(8,128)(2,1)} %get-tuple-element.110.silu_cond, ...), custom_call_target="tpu_custom_call" | custom-call | flops 1811939328 | bytes 3686400 | tf_op jit(solution)/shard_map/tail/pallas_call | solution.py:669
  441.5 0.7 slice.7
  442.2 0.1 reshape.40
  442.3 1.6 copy.57
  443.9 1.1 copy.55
  445.0 0.9 copy.56
  445.9 0.6 dynamic_slice.23
  446.6 0.0 copy-start.1
  446.6 7.6 %finish.1 = (bf16[512,768]{1,0:T(8,128)(2,1)}, f32[512,768]{1,0:T(8,128)}, f32[512,768]{1,0:T(8,128)}, f32[96,1152]{1,0:T(8,128)}, f32[8,96,768]{2,1,0:T(8,128)}...) custom-call(f32[3,192,768]{2,1,0:T(8,128)} %get-tuple-element.108.refs_0_.refs_1_.refs_2_, ...), custom_call_target="tpu_custom_call" | custom-call | tf_op jit(solution)/shard_map/finish/pallas_call | solution.py:728
  454.1 0.0 copy-done.1
  (4 shorter events, 0.0 us)
Async XLA Ops:
  0.6 23.8 %copy-start = (s32[8,256]{1,0:T(8,128)S(1)}, s32[8,256]{1,0:T(8,128)}, u32[]{:S(2)}) copy-start(s32[8,256]{1,0:T(8,128)} %param.17) | copy-start | bytes 24580
  0.7 34.9 %collective-permute-start.2 = (bf16[576,768]{1,0:T(8,128)(2,1)}, bf16[576,768]{1,0:T(8,128)(2,1)S(1)}, u32[]{:S(2)}, u32[]{:S(2)}) collective-permute-start(bf16[576,768]{1,0:T(8,128)(2,1)} %bitcast.15), channel_id=1, source_target_pairs={{0,1},{1,0},{2,3},{3,2},{4,5},{5,4},{6,7},{7,6},{8,9},{9,8},{10,11... | collective-permute-start | bytes 2654216 | tf_op jit(solution)/shard_map/ppermute | solution.py:38
  1.2 23.3 %collective-permute-start = (bf16[576,768]{1,0:T(8,128)(2,1)}, bf16[576,768]{1,0:T(8,128)(2,1)S(1)}, u32[]{:S(2)}, u32[]{:S(2)}) collective-permute-start(bf16[576,768]{1,0:T(8,128)(2,1)} %bitcast.16), channel_id=1, source_target_pairs={{0,2},{1,3},{2,0},{3,1},{4,6},{5,7},{6,4},{7,5},{8,10},{9,11},{10,... | collective-permute-start | bytes 2654216 | tf_op jit(solution)/shard_map/ppermute | solution.py:38
  3.7 26.8 %collective-permute-start.1 = (bf16[192,768]{1,0:T(8,128)(2,1)}, bf16[192,768]{1,0:T(8,128)(2,1)S(1)}, u32[]{:S(2)}, u32[]{:S(2)}) collective-permute-start(bf16[192,768]{1,0:T(8,128)(2,1)} %refs_8_.1), channel_id=1, source_target_pairs={{0,2},{1,3},{2,0},{3,1},{4,6},{5,7},{6,4},{7,5},{8,10},{9,11},{10,... | collective-permute-start | bytes 884744 | tf_op jit(solution)/shard_map/ppermute | solution.py:38
  4.6 10.6 %copy-start.3 = (bf16[512,768]{1,0:T(8,128)(2,1)S(1)}, bf16[512,768]{1,0:T(8,128)(2,1)}, u32[]{:S(2)}) copy-start(bf16[512,768]{1,0:T(8,128)(2,1)} %cotangent.3) | copy-start | bytes 2359300
  4.6 10.6 %copy-start.7 = (bf16[512,768]{1,0:T(8,128)(2,1)S(1)}, bf16[512,768]{1,0:T(8,128)(2,1)}, u32[]{:S(2)}) copy-start(bf16[512,768]{1,0:T(8,128)(2,1)} %cond.1) | copy-start | bytes 2359300
  11.5 3.7 copy-start.2
  15.2 17.1 %copy-start.8 = (bf16[192,768]{1,0:T(8,128)(2,1)S(1)}, bf16[192,768]{1,0:T(8,128)(2,1)}, u32[]{:S(2)}) copy-start(bf16[192,768]{1,0:T(8,128)(2,1)} %refs_8_.1) | copy-start | bytes 884740
  24.5 11.1 %copy-start.5 = (bf16[576,768]{1,0:T(8,128)(2,1)}, bf16[576,768]{1,0:T(8,128)(2,1)S(1)}, u32[]{:S(2)}) copy-start(bf16[576,768]{1,0:T(8,128)(2,1)S(1)} %collective-permute-done.refs_1_.refs_5_) | copy-start | bytes 2654212
  24.5 11.1 %collective-permute-start.3 = (bf16[576,768]{1,0:T(8,128)(2,1)S(1)}, bf16[576,768]{1,0:T(8,128)(2,1)S(1)}, u32[]{:S(2)}, u32[]{:S(2)}) collective-permute-start(bf16[576,768]{1,0:T(8,128)(2,1)S(1)} %collective-permute-done.refs_1_.refs_5_), channel_id=1, source_target_pairs={{0,1},{1,0},{2,3},{3,2},{4,5},{5,4},{6,7},{7,6},{8,9},{9,8},{10,11... | collective-permute-start | bytes 2654216 | tf_op jit(solution)/shard_map/ppermute | solution.py:38
  30.5 5.0 %copy-start.9 = (bf16[192,768]{1,0:T(8,128)(2,1)}, bf16[192,768]{1,0:T(8,128)(2,1)S(1)}, u32[]{:S(2)}) copy-start(bf16[192,768]{1,0:T(8,128)(2,1)S(1)} %collective-permute-done.1.refs_5_.refs_9_) | copy-start | bytes 884740
  30.5 25.1 %collective-permute-start.6 = (bf16[512,768]{1,0:T(8,128)(2,1)}, bf16[512,768]{1,0:T(8,128)(2,1)}, u32[]{:S(2)}, u32[]{:S(2)}) collective-permute-start(bf16[512,768]{1,0:T(8,128)(2,1)} %get-tuple-element.99.refs_2_), channel_id=1, source_target_pairs={{0,2},{1,3},{2,0},{3,1},{4,6},{5,7},{6,4},{7,5},{8,10},{9,11},{10,... | collective-permute-start | bytes 2359304 | tf_op jit(solution)/shard_map/ppermute | solution.py:38
  32.3 3.3 collective-permute-start.4
  32.3 3.3 collective-permute-start.5
  35.6 0.9 copy-start.4
  36.5 0.9 copy-start.6
  446.6 7.6 %copy-start.1 = (s32[8,256]{1,0:T(8,128)S(1)}, s32[8,256]{1,0:T(8,128)}, u32[]{:S(2)}) copy-start(s32[8,256]{1,0:T(8,128)} %param.17) | copy-start | bytes 24580

commit v5 on v4

--- a/solution.py
+++ b/solution.py
@@ -1448,7 +1448,7 @@
         for e in range(0, experts - 2, 2):
             halves, sums = call((e, e + 1), sums, False, [], 1 + e // 2)
             take_halves((e, e + 1), halves)
-    saved, sums = call(late, sums, True, jobs(n2=(experts - 4,), n1=(experts - 3,)), 4)
+    saved, sums = call(late, sums, True, jobs(n1=(experts - 4, experts - 3)), 4)
     out_chain, back_chain = Chain(*sums[:2], MP_STEPS), Chain(*sums[2:], MP_STEPS)
     halves = run_expert_grads(
         late,
@@ -1458,7 +1458,7 @@
         gates,
         all_tokens,
         all_grads,
-        [(back_chain, 2)] + jobs(n2=(experts - 3,)),
+        [(back_chain, 2)] + jobs(n1=(experts - 4, experts - 3)),
         5,
     )
     take_halves(late, halves)
@@ -1485,7 +1485,7 @@
         out_parts,
         tail_orders[0],
         tail_rows,
-        [(out_chain, 2)] + jobs(n1=late),
+        [(out_chain, 2)] + jobs(n1=late + (experts - 3,)),
         6,
     )
     patches_grad, pieces, heads_halves = results[0], results[1], results[2:4]

time: 461 us -> 457 us (level)
  no operation moved by 1% of the time
where the time goes in v5:
time: 457 us; the launch traced here: 450 us
  Pallas kernels  408 us (89%)
  waiting for transfers between devices  13.6 us (3%)
  local copies, waits for them, and re-layouts  13.3 us (3%)
  matrix products  6.85 us (1%)
  starting transfers between devices  5.45 us (1%)
    pallas_call x1, Pallas kernels, run_long(): pl.pallas_call(functools.partial(long_kernel, count, exchange, units, uni...  146 us
    pallas_call x1, Pallas kernels, run_tail(): pl.pallas_call(functools.partial(tail_kernel, orders, rows, exchange), gr...  92.4 us
    pallas_call x2, Pallas kernels, run_experts(): pl.pallas_call(functools.partial(expert_kernel, columns, gathers, first,...  68.5 us
    pallas_call x1, Pallas kernels, run_attention_back(): pl.pallas_call(functools.partial(attention_back_kernel, heads, exchange,...  44.6 us
    pallas_call x1, Pallas kernels, run_expert_grads(): pl.pallas_call(functools.partial(expert_grads_kernel, columns, exchange,...  30.2 us
    pallas_call x1, Pallas kernels, run_forward(): pl.pallas_call(functools.partial(forward_kernel, heads), grid=(rows,), in...  18.2 us
    ppermute x7, waiting for transfers between devices, swap(): return lax.ppermute(value, axis, [(i, i ^ mask) for i in range(size)])  13.6 us
  transfers between devices with their start and end apart: 7, of which 2 were waited for; matrix products, arithmetic and copies ran while one was open for 3% of the time, Pallas kernels for 4%

profile of v5, /device:TPU:0, one launch (start us, length us, event | category | flops | bytes accessed | tf_op | source)
XLA Modules:
  0.0 450.3 jit_solution(14171798332068446518)
XLA Ops:
  0.6 0.0 copy-start
  0.7 0.5 collective-permute-start.2
  1.2 2.6 collective-permute-start
  3.7 0.1 collective-permute-start.1
  3.8 0.8 select_reduce_fusion
  4.6 0.0 copy-start.3
  4.6 0.0 copy-start.7
  4.6 6.9 %convolution_add_fusion.shift_one.scale_one.gate_one.shift_two.scale_two.gate_two = f32[512,4608]{1,0:T(8,128)S(1)} fusion(bf16[768,4608]{1,0:T(8,128)(2,1)} %weight.1, f32[4608]{0:T(1024)} %param.21, bf16[512,768]{1,0:T(8,128)(2,1)} %cond.1), kind=kOutput, calls=%fused_computation | convolution fusion | flops 3628597248 | bytes 17319936 | tf_op jit(solution)/shard_map/dot_general | solution.py:1336
  11.5 0.0 copy-start.2
  11.5 0.1 broadcast_select_fusion
  11.6 3.6 copy-done.2
  15.2 0.0 copy-done.3
  15.2 0.0 copy-done.7
  15.2 0.0 copy-start.8
  15.2 1.6 fusion.3
  16.9 7.6 %collective-permute-done.refs_1_.refs_5_ = bf16[576,768]{1,0:T(8,128)(2,1)S(1)} collective-permute-done((bf16[576,768]{1,0:T(8,128)(2,1)}, bf16[576,768]{1,0:T(8,128)(2,1)S(1)}, u32[]{:S(2)}, u32[]{:S(2)}) %collective-permute-start) | collective-permute-done | bytes 884768 | tf_op jit(solution)/shard_map/ppermute | solution.py:38
  24.5 0.0 copy-start.5
  24.5 0.0 collective-permute-start.3
  24.5 0.0 copy-done
  24.5 6.0 %collective-permute-done.1.refs_5_.refs_9_ = bf16[192,768]{1,0:T(8,128)(2,1)S(1)} collective-permute-done((bf16[192,768]{1,0:T(8,128)(2,1)}, bf16[192,768]{1,0:T(8,128)(2,1)S(1)}, u32[]{:S(2)}, u32[]{:S(2)}) %collective-permute-start.1) | collective-permute-done | bytes 294944 | tf_op jit(solution)/shard_map/ppermute | solution.py:38
  30.5 0.0 copy-start.9
  30.5 1.8 collective-permute-start.6
  32.3 0.0 copy-done.8
  32.3 0.0 collective-permute-start.4
  32.3 0.5 collective-permute-start.5
  32.8 0.6 broadcast_in_dim.53.seg_row
  33.4 0.9 copy.49.seg_col
  34.2 1.3 copy.51.refs_0_.gates
  35.5 0.0 collective-permute-done.4.refs_6_.refs_10_
  35.5 0.0 collective-permute-done.5.refs_7_.refs_11_
  35.5 0.0 collective-permute-done.2.refs_2_.refs_6_
  35.5 0.0 copy-done.5
  35.6 0.0 copy-done.9
  35.6 0.0 copy-start.4
  35.6 0.0 collective-permute-done.3.refs_3_.refs_7_
  35.6 0.9 copy-done.4
  36.5 0.0 copy-start.6
  36.5 0.9 copy-done.6
  37.4 18.2 %attention_half.1 = (bf16[512,768]{1,0:T(8,128)(2,1)}, bf16[512,576]{1,0:T(8,128)(2,1)}, bf16[512,576]{1,0:T(8,128)(2,1)}, bf16[512,576]{1,0:T(8,128)(2,1)}, bf1...) custom-call(bf16[512,768]{1,0:T(8,128)(2,1)} %base.5, ...), custom_call_target="tpu_custom_call" | custom-call | flops 176160768 | bytes 983040 | tf_op jit(solution)/shard_map/attention_half/pallas_call | solution.py:343
  55.6 0.0 collective-permute-done.6.refs_3_
  55.7 34.2 %experts_1.1 = (bf16[4,192,512]{2,1,0:T(8,128)(2,1)}, bf16[4,192,512]{2,1,0:T(8,128)(2,1)}, bf16[4,192,256]{2,1,0:T(8,128)(2,1)}, bf16[4,192,256]{2,1,0:T(8,128)...) custom-call(f32[2048,16]{1,0:T(8,128)} %copy.51.refs_0_.gates, ...), custom_call_target="tpu_custom_call" | custom-call | flops 905969664 | bytes 2260992 | tf_op jit(solution)/shard_map/experts_1/pallas_call | solution.py:988
  89.9 146.0 %experts_long.1 = (f32[2048,768]{1,0:T(8,128)}, f32[2048,768]{1,0:T(8,128)}, f32[3,192,768]{2,1,0:T(8,128)}, f32[1,192,768]{2,1,0:T(8,128)}, bf16[2,192,512]{2,1...) custom-call(f32[2048,16]{1,0:T(8,128)} %copy.51.refs_0_.gates, ...), custom_call_target="tpu_custom_call" | custom-call | flops 5435817984 | bytes 4718592 | tf_op jit(solution)/shard_map/experts_long/pallas_call | solution.py:1194
  235.9 34.3 %experts_2.1 = (bf16[2048,768]{1,0:T(8,128)(2,1)}, bf16[2048,768]{1,0:T(8,128)(2,1)}, bf16[2048,768]{1,0:T(8,128)(2,1)}, bf16[2048,768]{1,0:T(8,128)(2,1)}, bf16...) custom-call(f32[2048,16]{1,0:T(8,128)} %copy.51.refs_0_.gates, ...), custom_call_target="tpu_custom_call" | custom-call | flops 1207959552 | bytes 2555904 | tf_op jit(solution)/shard_map/experts_2/pallas_call | solution.py:988
  270.2 30.2 %expert_grads.1 = (bf16[4,192,768]{2,1,0:T(8,128)(2,1)}, bf16[4,192,768]{2,1,0:T(8,128)(2,1)}, bf16[4,192,768]{2,1,0:T(8,128)(2,1)}, bf16[4,192,768]{2,1,0:T(8,1...) custom-call(f32[2048,16]{1,0:T(8,128)} %copy.51.refs_0_.gates, ...), custom_call_target="tpu_custom_call" | custom-call | flops 603979776 | bytes 1179648 | tf_op jit(solution)/shard_map/expert_grads/pallas_call | solution.py:1284
  300.4 44.6 %attention_back.1 = (f32[512,768]{1,0:T(8,128)}, bf16[512,3840]{1,0:T(8,128)(2,1)}, bf16[16,96,768]{2,1,0:T(8,128)(2,1)}, bf16[16,96,768]{2,1,0:T(8,128)(2,1)}, ...) custom-call(bf16[512,768]{1,0:T(8,128)(2,1)} %base.5, ...), custom_call_target="tpu_custom_call" | custom-call | flops 364904448 | bytes 1474560 | tf_op jit(solution)/shard_map/attention_back/pallas_call | solution.py:503
  345.0 92.4 %tail.1 = (f32[512,768]{1,0:T(8,128)}, bf16[512,768]{1,0:T(8,128)(2,1)}, f32[96,576]{1,0:T(8,128)}, f32[96,192]{1,0:T(8,128)}, f32[96,1152]{1,0:T(8,128)}, /*ind...) custom-call(bf16[512,768]{1,0:T(8,128)(2,1)} %cond.1, bf16[512,768]{1,0:T(8,128)(2,1)} %get-tuple-element.118.silu_cond, ...), custom_call_target="tpu_custom_call" | custom-call | flops 1811939328 | bytes 3686400 | tf_op jit(solution)/shard_map/tail/pallas_call | solution.py:669
  437.4 0.7 slice.7
  438.2 0.1 reshape.40
  438.2 1.6 copy.57
  439.9 1.1 copy.55
  441.0 0.9 copy.56
  441.8 0.6 dynamic_slice.23
  442.5 0.0 copy-start.1
  442.5 7.6 %finish.1 = (bf16[512,768]{1,0:T(8,128)(2,1)}, f32[512,768]{1,0:T(8,128)}, f32[512,768]{1,0:T(8,128)}, f32[96,1152]{1,0:T(8,128)}, f32[8,96,768]{2,1,0:T(8,128)}...) custom-call(f32[3,192,768]{2,1,0:T(8,128)} %get-tuple-element.116.refs_0_.refs_1_.refs_2_, ...), custom_call_target="tpu_custom_call" | custom-call | tf_op jit(solution)/shard_map/finish/pallas_call | solution.py:728
  450.1 0.0 copy-done.1
  (4 shorter events, 0.0 us)
Async XLA Ops:
  0.6 23.8 %copy-start = (s32[8,256]{1,0:T(8,128)S(1)}, s32[8,256]{1,0:T(8,128)}, u32[]{:S(2)}) copy-start(s32[8,256]{1,0:T(8,128)} %param.17) | copy-start | bytes 24580
  0.7 34.9 %collective-permute-start.2 = (bf16[576,768]{1,0:T(8,128)(2,1)}, bf16[576,768]{1,0:T(8,128)(2,1)S(1)}, u32[]{:S(2)}, u32[]{:S(2)}) collective-permute-start(bf16[576,768]{1,0:T(8,128)(2,1)} %bitcast.15), channel_id=1, source_target_pairs={{0,1},{1,0},{2,3},{3,2},{4,5},{5,4},{6,7},{7,6},{8,9},{9,8},{10,11... | collective-permute-start | bytes 2654216 | tf_op jit(solution)/shard_map/ppermute | solution.py:38
  1.2 23.3 %collective-permute-start = (bf16[576,768]{1,0:T(8,128)(2,1)}, bf16[576,768]{1,0:T(8,128)(2,1)S(1)}, u32[]{:S(2)}, u32[]{:S(2)}) collective-permute-start(bf16[576,768]{1,0:T(8,128)(2,1)} %bitcast.16), channel_id=1, source_target_pairs={{0,2},{1,3},{2,0},{3,1},{4,6},{5,7},{6,4},{7,5},{8,10},{9,11},{10,... | collective-permute-start | bytes 2654216 | tf_op jit(solution)/shard_map/ppermute | solution.py:38
  3.7 26.8 %collective-permute-start.1 = (bf16[192,768]{1,0:T(8,128)(2,1)}, bf16[192,768]{1,0:T(8,128)(2,1)S(1)}, u32[]{:S(2)}, u32[]{:S(2)}) collective-permute-start(bf16[192,768]{1,0:T(8,128)(2,1)} %refs_8_.1), channel_id=1, source_target_pairs={{0,2},{1,3},{2,0},{3,1},{4,6},{5,7},{6,4},{7,5},{8,10},{9,11},{10,... | collective-permute-start | bytes 884744 | tf_op jit(solution)/shard_map/ppermute | solution.py:38
  4.6 10.6 %copy-start.3 = (bf16[512,768]{1,0:T(8,128)(2,1)S(1)}, bf16[512,768]{1,0:T(8,128)(2,1)}, u32[]{:S(2)}) copy-start(bf16[512,768]{1,0:T(8,128)(2,1)} %cotangent.3) | copy-start | bytes 2359300
  4.6 10.6 %copy-start.7 = (bf16[512,768]{1,0:T(8,128)(2,1)S(1)}, bf16[512,768]{1,0:T(8,128)(2,1)}, u32[]{:S(2)}) copy-start(bf16[512,768]{1,0:T(8,128)(2,1)} %cond.1) | copy-start | bytes 2359300
  11.5 3.7 copy-start.2
  15.2 17.1 %copy-start.8 = (bf16[192,768]{1,0:T(8,128)(2,1)S(1)}, bf16[192,768]{1,0:T(8,128)(2,1)}, u32[]{:S(2)}) copy-start(bf16[192,768]{1,0:T(8,128)(2,1)} %refs_8_.1) | copy-start | bytes 884740
  24.5 11.1 %copy-start.5 = (bf16[576,768]{1,0:T(8,128)(2,1)}, bf16[576,768]{1,0:T(8,128)(2,1)S(1)}, u32[]{:S(2)}) copy-start(bf16[576,768]{1,0:T(8,128)(2,1)S(1)} %collective-permute-done.refs_1_.refs_5_) | copy-start | bytes 2654212
  24.5 11.1 %collective-permute-start.3 = (bf16[576,768]{1,0:T(8,128)(2,1)S(1)}, bf16[576,768]{1,0:T(8,128)(2,1)S(1)}, u32[]{:S(2)}, u32[]{:S(2)}) collective-permute-start(bf16[576,768]{1,0:T(8,128)(2,1)S(1)} %collective-permute-done.refs_1_.refs_5_), channel_id=1, source_target_pairs={{0,1},{1,0},{2,3},{3,2},{4,5},{5,4},{6,7},{7,6},{8,9},{9,8},{10,11... | collective-permute-start | bytes 2654216 | tf_op jit(solution)/shard_map/ppermute | solution.py:38
  30.5 5.0 %copy-start.9 = (bf16[192,768]{1,0:T(8,128)(2,1)}, bf16[192,768]{1,0:T(8,128)(2,1)S(1)}, u32[]{:S(2)}) copy-start(bf16[192,768]{1,0:T(8,128)(2,1)S(1)} %collective-permute-done.1.refs_5_.refs_9_) | copy-start | bytes 884740
  30.5 25.1 %collective-permute-start.6 = (bf16[512,768]{1,0:T(8,128)(2,1)}, bf16[512,768]{1,0:T(8,128)(2,1)}, u32[]{:S(2)}, u32[]{:S(2)}) collective-permute-start(bf16[512,768]{1,0:T(8,128)(2,1)} %get-tuple-element.107.refs_2_), channel_id=1, source_target_pairs={{0,2},{1,3},{2,0},{3,1},{4,6},{5,7},{6,4},{7,5},{8,10},{9,11},{10,... | collective-permute-start | bytes 2359304 | tf_op jit(solution)/shard_map/ppermute | solution.py:38
  32.3 3.3 collective-permute-start.4
  32.3 3.3 collective-permute-start.5
  35.6 0.9 copy-start.4
  36.5 0.9 copy-start.6
  442.5 7.6 %copy-start.1 = (s32[8,256]{1,0:T(8,128)S(1)}, s32[8,256]{1,0:T(8,128)}, u32[]{:S(2)}) copy-start(s32[8,256]{1,0:T(8,128)} %param.17) | copy-start | bytes 24580

commit v6 on v5

--- a/solution.py
+++ b/solution.py
@@ -621,6 +621,7 @@
     for place in range(len(orders[0])):
         half = len(orders[0]) // 2
         exchange.halves(0)[place // half][place % half, rows:, :] = lines
+    exchange.advance(2)
     half = MP_ORDER[len(MP_ORDER) // 2 :]
     for m in half + [m for m in MP_ORDER if m not in half]:
         first = pl.multiple_of(flip(mp, m) * columns, 128)
@@ -628,8 +629,6 @@
         for part, order in enumerate(orders):
             own = slice(part * split, (part + 1) * split)
             store_blocks(order, m, total, exchange.halves(part), rows, own)
-        if m == half[0]:
-            exchange.advance(2)
         if m == half[-1]:
             exchange.start(0)
             exchange.start(1)
@@ -760,14 +759,14 @@
         )
 
     def begin(self):
-        self.held[3] = self.own[...]
         if self.far is None:
             self.copy(1).start()
             self.copy(0).start()
         else:
-            self.held[1] = self.far[...]
             self.copy(0).start()
             self.copy(2).start()
+            self.held[1] = self.far[...]
+        self.held[3] = self.own[...]
 
     def tile(self, step):
         @pl.when(step == 1)

time: 457 us -> 457 us (level)
  no operation moved by 1% of the time
where the time goes in v6:
time: 457 us; the launch traced here: 450 us
  Pallas kernels  408 us (89%)
  waiting for transfers between devices  13.6 us (3%)
  local copies, waits for them, and re-layouts  13.3 us (3%)
  matrix products  6.85 us (1%)
  starting transfers between devices  5.45 us (1%)
    pallas_call x1, Pallas kernels, run_long(): pl.pallas_call(functools.partial(long_kernel, count, exchange, units, uni...  146 us
    pallas_call x1, Pallas kernels, run_tail(): pl.pallas_call(functools.partial(tail_kernel, orders, rows, exchange), gr...  92.5 us
    pallas_call x2, Pallas kernels, run_experts(): pl.pallas_call(functools.partial(expert_kernel, columns, gathers, first,...  68.4 us
    pallas_call x1, Pallas kernels, run_attention_back(): pl.pallas_call(functools.partial(attention_back_kernel, heads, exchange,...  44.6 us
    pallas_call x1, Pallas kernels, run_expert_grads(): pl.pallas_call(functools.partial(expert_grads_kernel, columns, exchange,...  30.2 us
    pallas_call x1, Pallas kernels, run_forward(): pl.pallas_call(functools.partial(forward_kernel, heads), grid=(rows,), in...  18.2 us
    ppermute x7, waiting for transfers between devices, swap(): return lax.ppermute(value, axis, [(i, i ^ mask) for i in range(size)])  13.6 us
  transfers between devices with their start and end apart: 7, of which 2 were waited for; matrix products, arithmetic and copies ran while one was open for 3% of the time, Pallas kernels for 4%

profile of v6, /device:TPU:0, one launch (start us, length us, event | category | flops | bytes accessed | tf_op | source)
XLA Modules:
  0.0 450.3 jit_solution(4790552130098028031)
XLA Ops:
  0.6 0.0 copy-start
  0.7 0.5 collective-permute-start.2
  1.2 2.6 collective-permute-start
  3.7 0.1 collective-permute-start.1
  3.8 0.8 select_reduce_fusion
  4.6 0.0 copy-start.3
  4.6 0.0 copy-start.7
  4.6 6.9 %convolution_add_fusion.shift_one.scale_one.gate_one.shift_two.scale_two.gate_two = f32[512,4608]{1,0:T(8,128)S(1)} fusion(bf16[768,4608]{1,0:T(8,128)(2,1)} %weight.1, f32[4608]{0:T(1024)} %param.21, bf16[512,768]{1,0:T(8,128)(2,1)} %cond.1), kind=kOutput, calls=%fused_computation | convolution fusion | flops 3628597248 | bytes 17319936 | tf_op jit(solution)/shard_map/dot_general | solution.py:1335
  11.5 0.0 copy-start.2
  11.5 0.1 broadcast_select_fusion
  11.6 3.6 copy-done.2
  15.2 0.0 copy-done.3
  15.2 0.0 copy-done.7
  15.2 0.0 copy-start.8
  15.2 1.6 fusion.3
  16.9 7.6 %collective-permute-done.refs_1_.refs_5_ = bf16[576,768]{1,0:T(8,128)(2,1)S(1)} collective-permute-done((bf16[576,768]{1,0:T(8,128)(2,1)}, bf16[576,768]{1,0:T(8,128)(2,1)S(1)}, u32[]{:S(2)}, u32[]{:S(2)}) %collective-permute-start) | collective-permute-done | bytes 884768 | tf_op jit(solution)/shard_map/ppermute | solution.py:38
  24.5 0.0 copy-start.5
  24.5 0.0 collective-permute-start.3
  24.5 0.0 copy-done
  24.5 6.0 %collective-permute-done.1.refs_5_.refs_9_ = bf16[192,768]{1,0:T(8,128)(2,1)S(1)} collective-permute-done((bf16[192,768]{1,0:T(8,128)(2,1)}, bf16[192,768]{1,0:T(8,128)(2,1)S(1)}, u32[]{:S(2)}, u32[]{:S(2)}) %collective-permute-start.1) | collective-permute-done | bytes 294944 | tf_op jit(solution)/shard_map/ppermute | solution.py:38
  30.5 0.0 copy-start.9
  30.5 1.8 collective-permute-start.6
  32.3 0.0 copy-done.8
  32.3 0.0 collective-permute-start.4
  32.3 0.5 collective-permute-start.5
  32.8 0.6 broadcast_in_dim.53.seg_row
  33.4 0.9 copy.49.seg_col
  34.2 1.3 copy.51.refs_0_.gates
  35.5 0.0 collective-permute-done.4.refs_6_.refs_10_
  35.5 0.0 collective-permute-done.5.refs_7_.refs_11_
  35.5 0.0 collective-permute-done.2.refs_2_.refs_6_
  35.5 0.0 copy-done.5
  35.6 0.0 copy-done.9
  35.6 0.0 copy-start.4
  35.6 0.0 collective-permute-done.3.refs_3_.refs_7_
  35.6 0.9 copy-done.4
  36.5 0.0 copy-start.6
  36.5 0.9 copy-done.6
  37.4 18.2 %attention_half.1 = (bf16[512,768]{1,0:T(8,128)(2,1)}, bf16[512,576]{1,0:T(8,128)(2,1)}, bf16[512,576]{1,0:T(8,128)(2,1)}, bf16[512,576]{1,0:T(8,128)(2,1)}, bf1...) custom-call(bf16[512,768]{1,0:T(8,128)(2,1)} %base.5, ...), custom_call_target="tpu_custom_call" | custom-call | flops 176160768 | bytes 983040 | tf_op jit(solution)/shard_map/attention_half/pallas_call | solution.py:343
  55.6 0.0 collective-permute-done.6.refs_3_
  55.7 34.2 %experts_1.1 = (bf16[4,192,512]{2,1,0:T(8,128)(2,1)}, bf16[4,192,512]{2,1,0:T(8,128)(2,1)}, bf16[4,192,256]{2,1,0:T(8,128)(2,1)}, bf16[4,192,256]{2,1,0:T(8,128)...) custom-call(f32[2048,16]{1,0:T(8,128)} %copy.51.refs_0_.gates, ...), custom_call_target="tpu_custom_call" | custom-call | flops 905969664 | bytes 2260992 | tf_op jit(solution)/shard_map/experts_1/pallas_call | solution.py:987
  89.8 146.0 %experts_long.1 = (f32[2048,768]{1,0:T(8,128)}, f32[2048,768]{1,0:T(8,128)}, f32[3,192,768]{2,1,0:T(8,128)}, f32[1,192,768]{2,1,0:T(8,128)}, bf16[2,192,512]{2,1...) custom-call(f32[2048,16]{1,0:T(8,128)} %copy.51.refs_0_.gates, ...), custom_call_target="tpu_custom_call" | custom-call | flops 5435817984 | bytes 4718592 | tf_op jit(solution)/shard_map/experts_long/pallas_call | solution.py:1193
  235.9 34.3 %experts_2.1 = (bf16[2048,768]{1,0:T(8,128)(2,1)}, bf16[2048,768]{1,0:T(8,128)(2,1)}, bf16[2048,768]{1,0:T(8,128)(2,1)}, bf16[2048,768]{1,0:T(8,128)(2,1)}, bf16...) custom-call(f32[2048,16]{1,0:T(8,128)} %copy.51.refs_0_.gates, ...), custom_call_target="tpu_custom_call" | custom-call | flops 1207959552 | bytes 2555904 | tf_op jit(solution)/shard_map/experts_2/pallas_call | solution.py:987
  270.2 30.2 %expert_grads.1 = (bf16[4,192,768]{2,1,0:T(8,128)(2,1)}, bf16[4,192,768]{2,1,0:T(8,128)(2,1)}, bf16[4,192,768]{2,1,0:T(8,128)(2,1)}, bf16[4,192,768]{2,1,0:T(8,1...) custom-call(f32[2048,16]{1,0:T(8,128)} %copy.51.refs_0_.gates, ...), custom_call_target="tpu_custom_call" | custom-call | flops 603979776 | bytes 1179648 | tf_op jit(solution)/shard_map/expert_grads/pallas_call | solution.py:1283
  300.4 44.6 %attention_back.1 = (f32[512,768]{1,0:T(8,128)}, bf16[512,3840]{1,0:T(8,128)(2,1)}, bf16[16,96,768]{2,1,0:T(8,128)(2,1)}, bf16[16,96,768]{2,1,0:T(8,128)(2,1)}, ...) custom-call(bf16[512,768]{1,0:T(8,128)(2,1)} %base.5, ...), custom_call_target="tpu_custom_call" | custom-call | flops 364904448 | bytes 1474560 | tf_op jit(solution)/shard_map/attention_back/pallas_call | solution.py:503
  344.9 92.5 %tail.1 = (f32[512,768]{1,0:T(8,128)}, bf16[512,768]{1,0:T(8,128)(2,1)}, f32[96,576]{1,0:T(8,128)}, f32[96,192]{1,0:T(8,128)}, f32[96,1152]{1,0:T(8,128)}, /*ind...) custom-call(bf16[512,768]{1,0:T(8,128)(2,1)} %cond.1, bf16[512,768]{1,0:T(8,128)(2,1)} %get-tuple-element.118.silu_cond, ...), custom_call_target="tpu_custom_call" | custom-call | flops 1811939328 | bytes 3686400 | tf_op jit(solution)/shard_map/tail/pallas_call | solution.py:668
  437.4 0.7 slice.7
  438.1 0.1 reshape.40
  438.2 1.6 copy.57
  439.9 1.1 copy.55
  440.9 0.9 copy.56
  441.8 0.6 dynamic_slice.23
  442.5 0.0 copy-start.1
  442.5 7.6 %finish.1 = (bf16[512,768]{1,0:T(8,128)(2,1)}, f32[512,768]{1,0:T(8,128)}, f32[512,768]{1,0:T(8,128)}, f32[96,1152]{1,0:T(8,128)}, f32[8,96,768]{2,1,0:T(8,128)}...) custom-call(f32[3,192,768]{2,1,0:T(8,128)} %get-tuple-element.116.refs_0_.refs_1_.refs_2_, ...), custom_call_target="tpu_custom_call" | custom-call | tf_op jit(solution)/shard_map/finish/pallas_call | solution.py:727
  450.0 0.0 copy-done.1
  (4 shorter events, 0.0 us)
Async XLA Ops:
  0.6 23.8 %copy-start = (s32[8,256]{1,0:T(8,128)S(1)}, s32[8,256]{1,0:T(8,128)}, u32[]{:S(2)}) copy-start(s32[8,256]{1,0:T(8,128)} %param.17) | copy-start | bytes 24580
  0.7 34.9 %collective-permute-start.2 = (bf16[576,768]{1,0:T(8,128)(2,1)}, bf16[576,768]{1,0:T(8,128)(2,1)S(1)}, u32[]{:S(2)}, u32[]{:S(2)}) collective-permute-start(bf16[576,768]{1,0:T(8,128)(2,1)} %bitcast.15), channel_id=1, source_target_pairs={{0,1},{1,0},{2,3},{3,2},{4,5},{5,4},{6,7},{7,6},{8,9},{9,8},{10,11... | collective-permute-start | bytes 2654216 | tf_op jit(solution)/shard_map/ppermute | solution.py:38
  1.2 23.3 %collective-permute-start = (bf16[576,768]{1,0:T(8,128)(2,1)}, bf16[576,768]{1,0:T(8,128)(2,1)S(1)}, u32[]{:S(2)}, u32[]{:S(2)}) collective-permute-start(bf16[576,768]{1,0:T(8,128)(2,1)} %bitcast.16), channel_id=1, source_target_pairs={{0,2},{1,3},{2,0},{3,1},{4,6},{5,7},{6,4},{7,5},{8,10},{9,11},{10,... | collective-permute-start | bytes 2654216 | tf_op jit(solution)/shard_map/ppermute | solution.py:38
  3.7 26.8 %collective-permute-start.1 = (bf16[192,768]{1,0:T(8,128)(2,1)}, bf16[192,768]{1,0:T(8,128)(2,1)S(1)}, u32[]{:S(2)}, u32[]{:S(2)}) collective-permute-start(bf16[192,768]{1,0:T(8,128)(2,1)} %refs_8_.1), channel_id=1, source_target_pairs={{0,2},{1,3},{2,0},{3,1},{4,6},{5,7},{6,4},{7,5},{8,10},{9,11},{10,... | collective-permute-start | bytes 884744 | tf_op jit(solution)/shard_map/ppermute | solution.py:38
  4.6 10.6 %copy-start.3 = (bf16[512,768]{1,0:T(8,128)(2,1)S(1)}, bf16[512,768]{1,0:T(8,128)(2,1)}, u32[]{:S(2)}) copy-start(bf16[512,768]{1,0:T(8,128)(2,1)} %cotangent.3) | copy-start | bytes 2359300
  4.6 10.6 %copy-start.7 = (bf16[512,768]{1,0:T(8,128)(2,1)S(1)}, bf16[512,768]{1,0:T(8,128)(2,1)}, u32[]{:S(2)}) copy-start(bf16[512,768]{1,0:T(8,128)(2,1)} %cond.1) | copy-start | bytes 2359300
  11.5 3.7 copy-start.2
  15.2 17.1 %copy-start.8 = (bf16[192,768]{1,0:T(8,128)(2,1)S(1)}, bf16[192,768]{1,0:T(8,128)(2,1)}, u32[]{:S(2)}) copy-start(bf16[192,768]{1,0:T(8,128)(2,1)} %refs_8_.1) | copy-start | bytes 884740
  24.5 11.1 %copy-start.5 = (bf16[576,768]{1,0:T(8,128)(2,1)}, bf16[576,768]{1,0:T(8,128)(2,1)S(1)}, u32[]{:S(2)}) copy-start(bf16[576,768]{1,0:T(8,128)(2,1)S(1)} %collective-permute-done.refs_1_.refs_5_) | copy-start | bytes 2654212
  24.5 11.1 %collective-permute-start.3 = (bf16[576,768]{1,0:T(8,128)(2,1)S(1)}, bf16[576,768]{1,0:T(8,128)(2,1)S(1)}, u32[]{:S(2)}, u32[]{:S(2)}) collective-permute-start(bf16[576,768]{1,0:T(8,128)(2,1)S(1)} %collective-permute-done.refs_1_.refs_5_), channel_id=1, source_target_pairs={{0,1},{1,0},{2,3},{3,2},{4,5},{5,4},{6,7},{7,6},{8,9},{9,8},{10,11... | collective-permute-start | bytes 2654216 | tf_op jit(solution)/shard_map/ppermute | solution.py:38
  30.5 5.0 %copy-start.9 = (bf16[192,768]{1,0:T(8,128)(2,1)}, bf16[192,768]{1,0:T(8,128)(2,1)S(1)}, u32[]{:S(2)}) copy-start(bf16[192,768]{1,0:T(8,128)(2,1)S(1)} %collective-permute-done.1.refs_5_.refs_9_) | copy-start | bytes 884740
  30.5 25.1 %collective-permute-start.6 = (bf16[512,768]{1,0:T(8,128)(2,1)}, bf16[512,768]{1,0:T(8,128)(2,1)}, u32[]{:S(2)}, u32[]{:S(2)}) collective-permute-start(bf16[512,768]{1,0:T(8,128)(2,1)} %get-tuple-element.107.refs_2_), channel_id=1, source_target_pairs={{0,2},{1,3},{2,0},{3,1},{4,6},{5,7},{6,4},{7,5},{8,10},{9,11},{10,... | collective-permute-start | bytes 2359304 | tf_op jit(solution)/shard_map/ppermute | solution.py:38
  32.3 3.3 collective-permute-start.4
  32.3 3.3 collective-permute-start.5
  35.6 0.9 copy-start.4
  36.5 0.9 copy-start.6
  442.5 7.6 %copy-start.1 = (s32[8,256]{1,0:T(8,128)S(1)}, s32[8,256]{1,0:T(8,128)}, u32[]{:S(2)}) copy-start(s32[8,256]{1,0:T(8,128)} %param.17) | copy-start | bytes 24580
